TPU v7x, 256 devices: a whole 4x4x8 slice. The times are simulated.
256 devices in a mesh: member: 8 (over z_hi, core), lat: 32 (over y, z_lo, x).
Axes of the slice: x: 4, y: 4, z: 8 (z_hi: 4, z_lo: 2; z = z_hi * 2 + z_lo), core: 2. Of those that a mesh axis runs over, the one named last changes fastest.
Arguments:
- ensemble: bfloat16 [16, 64, 128, 256], P('member', None, 'lat'), may hold values from -6 to 6
- cotangent: bfloat16 [16, 64, 128, 256], P('member', None, 'lat'), may hold values from -6 to 6
- conv_in: bfloat16 [3, 3, 64, 128], replicated, may hold values from -0.25 to 0.25
- pool_weight: bfloat16 [256, 128], replicated, may hold values from -1 to 1
- conv_out: bfloat16 [3, 3, 128, 64], replicated, may hold values from -0.1875 to 0.1875
Outputs:
- encoded: bfloat16 [16, 64, 128, 256], P('member', None, 'lat')
- d_input: bfloat16 [16, 64, 128, 256], P('member', None, 'lat')
- grad_conv_in: float32 [3, 3, 64, 128], replicated
- grad_pool: float32 [256, 128], replicated
- grad_conv_out: float32 [3, 3, 128, 64], replicated
All inputs are finite; a program needn't handle non-finite values.
Results may differ from a plain program's by a relative error of at most 0.0085.
Values may be sent and summed in bfloat16 or wider, within the bound.
No kernel may reach another device: no remote copies, remote signals or barrier semaphores. Data moves between devices by JAX's collectives and lax.ppermute only.
A program may use at most 64 MiB of HBM per device.

v0:
```python
import functools
import math

import jax
import jax.numpy as jnp
from jax import lax
from jax.experimental import pallas as pl
from jax.experimental.pallas import tpu as pltpu
from jax.sharding import PartitionSpec as P


BF = jnp.bfloat16
F32 = jnp.float32
WIDE = 80


def swap(value, steps, cross, groups):
    chips = groups // 2
    pairs = [
        (2 * z + c, 2 * ((z + steps) % chips) + (c + cross) % 2) for z in range(chips) for c in range(2)
    ]
    return lax.ppermute(value, "member", pairs)


def column_block(device, steps, cross, groups):
    chips = groups // 2
    return 2 * lax.rem(device // 2 + steps, chips) + lax.rem(device + cross, 2)


def near(*values):
    return [pltpu.with_memory_space_constraint(v, pltpu.VMEM) for v in values]


def sigmoid(v):
    return 1.0 / (1.0 + jnp.exp(-v))


def split3(v):
    a = v.astype(BF)
    r = v - a.astype(F32)
    b = r.astype(BF)
    c = (r - b.astype(F32)).astype(BF)
    return a, b, c


def dot(a, b):
    return jnp.dot(a, b, preferred_element_type=F32)


def dot_t(a, b, dims):
    return lax.dot_general(a, b, (dims, ((), ())), preferred_element_type=F32)


def dot_rows(a, b):
    return dot_t(a, b, ((0,), (0,)))


def pack_kernel(me_ref, ens_ref, cot_ref, keep_ref, give_ref, plane):
    chips, _, width, _ = keep_ref.shape
    mem_local, _, rows, lon = ens_ref.shape
    for m in range(mem_local):
        for r in range(rows):
            both = jnp.concatenate([ens_ref[m, :, r, :], cot_ref[m, :, r, :]], axis=0).astype(F32).T
            plane[r, pl.ds(4 + m, lon, stride=2), :] = both
            plane[r, pl.ds(m, 2, stride=2), :] = both[lon - 2 :]
            plane[r, pl.ds(4 + 2 * lon + m, 2, stride=2), :] = both[:2]
    for d in range(chips):
        for cross, ref in enumerate((keep_ref, give_ref)):
            k = column_block(me_ref[0], d, cross, 2 * chips)
            for r in range(rows):
                ref[d, r] = plane[r, pl.ds(pl.multiple_of(k * (width - 8), 8), width), :].astype(BF)


def pair_kernel(keep_ref, got_ref, *out_refs):
    for d, ref in enumerate(out_refs):
        ref[0] = keep_ref[d]
        ref[1] = got_ref[d]


def edges_kernel(*refs):
    tiles, (head_ref, tail_ref) = refs[:-2], refs[-2:]
    rows = tiles[0].shape[1]
    for d, tile in enumerate(tiles):
        head_ref[2 * d : 2 * d + 2] = tile[:, :2]
        tail_ref[2 * d : 2 * d + 2] = tile[:, rows - 2 :]


def other_kernel(*refs):
    for d, tile in enumerate(refs[:-1]):
        refs[-1][d] = tile[1]


def unpack_kernel(me_ref, *refs):
    tiles, (theirs_ref, enc_ref, din_ref, plane) = refs[:-4], refs[-4:]
    chips = len(tiles)
    mem_local, half, rows, lon = enc_ref.shape
    width = theirs_ref.shape[2]
    for d in range(chips):
        for cross in range(2):
            k = column_block(me_ref[0], d, cross, 2 * chips)
            for r in range(rows):
                piece = theirs_ref[d, r] if cross else tiles[d][0, r]
                plane[r, pl.ds(pl.multiple_of(k * width, 8), width), :] = piece.astype(F32)
    for m in range(mem_local):
        for r in range(rows):
            both = plane[r, pl.ds(m, lon, stride=2), :].T.astype(BF)
            enc_ref[m, :, r, :] = both[:half]
            din_ref[m, :, r, :] = both[half:]


def tile_kernel(
    lat_ref, t0, t1, t2, t3, top_ref, bot_ref, w1_ref, pool_ref, _,
    grads_ref, hid_ref, dpre_ref,
    own_ref, pre_s, dh_s, act_s, xo_s, hq_s, dpo_s, hid_s, dpre_s, sum_s, var_s, shared_s, ca_s, cs_s, sems,
):
    srcs, rows, width, _ = own_ref.shape
    inner = rows + 2
    cols = xo_s.shape[2]
    nlat = lat_ref[1]
    for d, tile in enumerate((t0, t1, t2, t3)):
        own_ref[2 * d : 2 * d + 2] = tile[...]
    members = 2 * srcs
    channels = pre_s.shape[-1]
    shape = (inner, WIDE, channels)

    def up(v, n):
        return pltpu.roll(v, WIDE - n, 1) if n else v

    parity = lax.broadcasted_iota(jnp.int32, shape, 1) % 2

    def pair_sum(v):
        return v + jnp.where(parity == 0, up(v, 1), pltpu.roll(v, 1, 1))

    row_id = lax.broadcasted_iota(jnp.int32, shape, 0) + lat_ref[0] * rows - 1
    inside = jnp.logical_and(row_id >= 0, row_id < nlat)

    sum_s[...] = jnp.zeros(shape, F32)

    def first(s, carry):
        x = jnp.concatenate([top_ref[s], own_ref[s], bot_ref[s]], axis=0).astype(F32)
        x = jnp.concatenate([x, jnp.zeros((rows + 4, WIDE - width, 128), F32)], axis=1)
        x1, x2, x3 = up(x, 2), up(x, 4), up(x, 6)
        xs = jnp.concatenate([x, x1, x2], axis=-1).astype(BF)
        xo_s[s] = jnp.concatenate([v[1 : 1 + inner, :cols] for v in (x1, x2, x3)], axis=-1).astype(BF)
        acc = dot(xs[0:inner].reshape(inner * WIDE, 384), w1_ref[0])
        acc += dot(xs[1 : 1 + inner].reshape(inner * WIDE, 384), w1_ref[1])
        acc += dot(xs[2 : 2 + inner].reshape(inner * WIDE, 384), w1_ref[2])
        pre = acc[:, :channels].reshape(shape)
        pre_s[s] = pre
        dh_s[s] = acc[:, channels:].reshape(shape)
        act = (pre * sigmoid(pre)).astype(BF).astype(F32)
        act_s[s] = act
        sum_s[...] += act
        return carry

    lax.fori_loop(0, srcs, first, 0)
    average = pair_sum(sum_s[...]) * (1.0 / members)
    sum_s[...] = average
    var_s[...] = jnp.zeros(shape, F32)

    def second(s, carry):
        d = act_s[s] - sum_s[...]
        var_s[...] += d * d
        return carry

    lax.fori_loop(0, srcs, second, 0)
    spread = jnp.sqrt(pair_sum(var_s[...]) * (1.0 / members) + 0.1)
    var_s[...] = spread
    stats = jnp.concatenate([sum_s[...], spread], axis=-1).reshape(inner * WIDE, 2 * channels)
    s1, s2, s3 = split3(stats)
    pool = pool_ref[...]
    shared_s[...] = (dot(s1, pool) + dot(s2, pool) + dot(s3, pool)).reshape(shape)
    ca_s[...] = jnp.zeros(shape, F32)

    def third(s, carry):
        zed = act_s[s] + shared_s[...]
        sig = sigmoid(zed)
        hid = jnp.where(inside, (zed * sig).astype(BF).astype(F32), 0.0)
        dz = (dh_s[s] * (sig * (1.0 + zed * (1.0 - sig)))).astype(BF).astype(F32)
        dh_s[s] = dz
        ca_s[...] += dz
        hid_s[s] = hid[:, :width].astype(BF)
        hq_s[s] = jnp.concatenate([up(hid, 2 * q)[:, :cols] for q in range(3)], axis=-1).astype(BF)
        return carry

    lax.fori_loop(0, srcs, third, 0)
    hid_copy = pltpu.make_async_copy(hid_s, hid_ref, sems.at[0])
    hid_copy.start()
    d_shared = pair_sum(ca_s[...])
    d1, d2, d3 = split3(d_shared.reshape(inner * WIDE, channels))
    last = ((1,), (1,))
    d_stats = dot_t(d1, pool, last) + dot_t(d2, pool, last) + dot_t(d3, pool, last)
    ca_s[...] = (d_stats[:, :channels] * (1.0 / members)).reshape(shape)
    cs_s[...] = d_stats[:, channels:].reshape(shape) / (members * var_s[...])
    r_id = lax.broadcasted_iota(jnp.int32, shape, 0)
    c_id = lax.broadcasted_iota(jnp.int32, shape, 1)
    mine = (r_id >= 1) & (r_id <= rows) & (c_id >= 2) & (c_id < 2 + cols) & (parity == 0)
    e1, e2, e3 = split3(jnp.where(mine, d_shared, 0.0).reshape(inner * WIDE, channels))
    g_pool = dot_rows(s1, e1) + dot_rows(s1, e2) + dot_rows(s2, e1) + dot_rows(s2, e2) + dot_rows(s1, e3) + dot_rows(s3, e1)

    def fourth(s, carry):
        pre = pre_s[s]
        sig = sigmoid(pre)
        d_act = dh_s[s] + ca_s[...] + cs_s[...] * (act_s[s] - sum_s[...])
        dp = jnp.where(inside, d_act * (sig * (1.0 + pre * (1.0 - sig))), 0.0).astype(BF).astype(F32)
        dpre_s[s] = dp[:, :width].astype(BF)
        dpo_s[s] = up(dp, 2)[1 : 1 + rows, :cols].astype(BF)
        return carry

    lax.fori_loop(0, srcs, fourth, 0)
    dpre_copy = pltpu.make_async_copy(dpre_s, dpre_ref, sems.at[1])
    dpre_copy.start()

    total = srcs * rows * cols
    dpo = dpo_s[...].reshape(total, channels)
    own = xo_s[:, 1 : 1 + rows, :, 128:256].reshape(total, 128)
    half = channels // 2
    for p in range(3):
        g_in = dot_rows(dpo, xo_s[:, p : p + rows].reshape(total, 384))
        g_out = dot_rows(own, hq_s[:, p : p + rows].reshape(total, 384))
        for q in range(3):
            t = 3 * p + q
            grads_ref[t * half : (t + 1) * half, :] = g_in[:, q * 128 : (q + 1) * 128].T[:half].astype(BF)
            grads_ref[(9 + t) * half : (10 + t) * half, :] = g_out[half:, q * 128 : (q + 1) * 128].astype(BF)
    used = 18 * half + 2 * channels
    grads_ref[18 * half : used, :] = g_pool.astype(BF)
    if used < grads_ref.shape[0]:
        grads_ref[used:, :] = jnp.zeros((grads_ref.shape[0] - used, 128), BF)
    hid_copy.wait()
    dpre_copy.wait()


def output_kernel(t0, t1, t2, t3, hid_ref, dpre_ref, w2_ref, *out_refs):
    _, inner, width, _ = hid_ref.shape
    rows = inner - 2
    cols = out_refs[0].shape[2]

    def shifts(ref, s):
        v = ref[s].astype(F32)
        return [(pltpu.roll(v, width - 2 * q, 1) if q else v)[:, :cols] for q in range(3)]

    for d, (tile, out_ref) in enumerate(zip((t0, t1, t2, t3), out_refs)):

        def piece(j, carry):
            both = jnp.concatenate(shifts(hid_ref, 2 * d + j) + shifts(dpre_ref, 2 * d + j), axis=-1).astype(BF)
            depth = both.shape[-1]
            acc = dot(both[0:rows].reshape(rows * cols, depth), w2_ref[0])
            acc += dot(both[1 : 1 + rows].reshape(rows * cols, depth), w2_ref[1])
            acc += dot(both[2 : 2 + rows].reshape(rows * cols, depth), w2_ref[2])
            own = pltpu.roll(tile[j].astype(F32), width - 4, 1)[:, :cols]
            out_ref[j] = (own + acc.reshape(rows, cols, 128)).astype(BF)
            return carry

        lax.fori_loop(0, 2, piece, 0)


def sum_kernel(parts_ref, out_ref):
    total = jnp.sum(parts_ref[...].astype(F32), axis=0)
    out_ref[...] = jnp.broadcast_to(total[None], out_ref.shape).astype(out_ref.dtype)


def finish_kernel(scale, full_ref, in_ref, out_ref, pool_ref):
    start = 0
    for ref in (in_ref, out_ref, pool_ref):
        size = ref.shape[0]
        ref[...] = full_ref[start : start + size].astype(F32) * scale
        start += size


def block(ensemble, cotangent, conv_in, pool_weight, conv_out):
    mem_local, _, rows, lon = ensemble.shape
    groups = lax.axis_size("member")
    bands = lax.axis_size("lat")
    channels = conv_in.shape[-1]
    cols = lon // groups
    width = (cols + 4) * mem_local
    vspec = pl.BlockSpec(memory_space=pltpu.VMEM)
    sspec = pl.BlockSpec(memory_space=pltpu.SMEM)
    vm = pltpu.VMEM
    me = lax.axis_index("member").astype(jnp.int32).reshape(1)
    chips = groups // 2
    keep, give = pl.pallas_call(
        pack_kernel,
        out_shape=[vm((chips, rows, width, 128), BF)] * 2,
        in_specs=[sspec, vspec, vspec],
        out_specs=[vspec] * 2,
        scratch_shapes=[vm((rows, 2 * lon + 8, 128), F32)],
        name="pack",
    )(me, ensemble, cotangent)
    got = swap(give, 0, 1, groups)
    tiles = pl.pallas_call(
        pair_kernel,
        out_shape=[vm((2, rows, width, 128), BF)] * chips,
        in_specs=[vspec] * 2,
        out_specs=[vspec] * chips,
        name="pair",
    )(*near(keep, got))
    tiles = [tiles[0]] + [swap(tiles[d], d, 0, groups) for d in range(1, chips)]
    head, tail = pl.pallas_call(
        edges_kernel,
        out_shape=[vm((groups, 2, width, 128), BF)] * 2,
        in_specs=[vspec] * chips,
        out_specs=[vspec] * 2,
        name="edges",
    )(*near(*tiles))
    top = lax.ppermute(tail, "lat", [(i, i + 1) for i in range(bands - 1)])
    bot = lax.ppermute(head, "lat", [(i + 1, i) for i in range(bands - 1)])

    flip_in = jnp.transpose(conv_in[::-1, ::-1], (0, 1, 3, 2))
    flip_out = jnp.transpose(conv_out[::-1, ::-1], (0, 1, 3, 2))
    z1 = jnp.zeros_like(conv_in)
    z2 = jnp.zeros_like(conv_out)
    w1 = jnp.concatenate(
        [jnp.concatenate([conv_in, z1], axis=3), jnp.concatenate([z1, flip_out], axis=3)], axis=2
    ).reshape(3, 384, 256)
    w2 = jnp.concatenate(
        [
            jnp.concatenate([conv_out, z2], axis=3).reshape(3, 384, 128),
            jnp.concatenate([z2, flip_in], axis=3).reshape(3, 384, 128),
        ],
        axis=1,
    )
    lat = jnp.stack([lax.axis_index("lat"), jnp.int32(bands * rows)]).astype(jnp.int32)
    inner = rows + 2
    plane = (inner, WIDE, channels)
    used = 18 * (channels // 2) + 2 * channels
    per = -(-used // (8 * bands)) * 8
    shifted = (groups, inner, cols * mem_local, 384)
    compact = pltpu.HBM((groups, inner, width, channels), BF)
    hspec = pl.BlockSpec(memory_space=pltpu.HBM)
    grads, hid, dpre = pl.pallas_call(
        tile_kernel,
        out_shape=[vm((bands * per, channels), BF), compact, compact],
        in_specs=[sspec] + [vspec] * (chips + 4) + [hspec],
        out_specs=[vspec, hspec, hspec],
        scratch_shapes=[
            vm((groups, rows, width, 128), BF),
            vm((groups,) + plane, F32),
            vm((groups,) + plane, F32),
            vm((groups,) + plane, F32),
            vm(shifted, BF),
            vm(shifted, BF),
            vm((groups, rows, cols * mem_local, channels), BF),
            vm(compact.shape, BF),
            vm(compact.shape, BF),
            vm(plane, F32),
            vm(plane, F32),
            vm(plane, F32),
            vm(plane, F32),
            vm(plane, F32),
            pltpu.SemaphoreType.DMA((2,)),
        ],
        compiler_params=pltpu.CompilerParams(vmem_limit_bytes=48 * 1024 * 1024),
        name="tile",
    )(lat, *near(*tiles, top, bot, w1, pool_weight), w2)
    pieces = list(pl.pallas_call(
        output_kernel,
        out_shape=[vm((2, rows, cols * mem_local, 128), BF)] * chips,
        in_specs=[vspec] * (chips + 3),
        out_specs=[vspec] * chips,
        name="output",
    )(*near(*tiles), hid, dpre, w2))

    def exchange(value, axis):
        return lax.all_to_all(value, axis, split_axis=0, concat_axis=0, tiled=True)

    def add_up(parts, copies, dtype):
        return pl.pallas_call(
            sum_kernel,
            out_shape=vm((copies,) + parts.shape[1:], dtype),
            in_specs=[vspec],
            out_specs=vspec,
            name="total",
        )(*near(parts))

    parts = exchange(grads.reshape(bands, per, channels), "lat")
    far = swap(pieces[2], chips - 2, 0, groups)
    parts, pieces[1], pieces[3] = lax.optimization_barrier((parts, pieces[1], pieces[3]))
    pieces = [pieces[0]] + [far if d == 2 else swap(pieces[d], chips - d, 0, groups) for d in range(1, chips)]
    parts = add_up(parts, groups, F32)
    parts = exchange(parts, "member")
    parts, pieces[1], pieces[3] = lax.optimization_barrier((parts, pieces[1], pieces[3]))
    other = pl.pallas_call(
        other_kernel,
        out_shape=vm((chips, rows, cols * mem_local, 128), BF),
        in_specs=[vspec] * chips,
        out_specs=vspec,
        name="other",
    )(*near(*pieces))
    theirs = swap(other, 0, 1, groups)
    full = exchange(add_up(parts, bands, BF), "lat").reshape(bands * per, channels)
    members = mem_local * groups
    scale = 1.0 / math.sqrt(members * bands * rows * lon)
    half = channels // 2
    grad_in, grad_out, grad_pool = pl.pallas_call(
        functools.partial(finish_kernel, scale),
        out_shape=[jax.ShapeDtypeStruct((n, channels), F32) for n in (9 * half, 9 * half, 2 * channels)],
        in_specs=[vspec],
        out_specs=[vspec] * 3,
        name="finish",
    )(*near(full))
    grad_in = grad_in.reshape(3, 3, half, channels)
    grad_out = grad_out.reshape(3, 3, half, channels).transpose(0, 1, 3, 2)

    encoded, d_input = pl.pallas_call(
        unpack_kernel,
        out_shape=[jax.ShapeDtypeStruct(ensemble.shape, BF)] * 2,
        in_specs=[sspec] + [vspec] * (chips + 1),
        out_specs=[vspec] * 2,
        scratch_shapes=[vm((rows, 2 * lon, 128), F32)],
        name="unpack",
    )(me, *near(*pieces, theirs))
    return encoded, d_input, grad_in, grad_pool, grad_out


def solution(mesh):
    return jax.shard_map(
        block,
        mesh=mesh,
        in_specs=(P("member", None, "lat", None), P("member", None, "lat", None), P(), P(), P()),
        out_specs=(P("member", None, "lat", None), P("member", None, "lat", None), P(), P(), P()),
        check_vma=False,
    )
```

profile of v0, /device:TPU:1, one launch (start us, length us, event | category | flops | bytes accessed | tf_op | source)
XLA Modules:
  0.0 114.9 jit_solution(5779658381290110573)
XLA Ops:
  0.7 2.0 %pack.1 = (bf16[4,4,72,128]{3,2,1,0:T(8,128)(2,1)S(1)}, bf16[4,4,72,128]{3,2,1,0:T(8,128)(2,1)S(1)}) custom-call(s32[1]{0:T(128)} %bitcast.me_ref, bf16[2,64,4,256]{3,2,1,0:T(4,128)(2,1)} %ens_ref.1, bf16[2,64,4,256]{3,2,1,0:T(4,128)(2,1)} %cot_ref.1), custom_call_target="tpu_custom_call" | custom-call | tf_op jit(solution)/shard_map/pack/pallas_call | solution.py:282
  2.7 3.3 %collective-permute-start = (bf16[4,4,72,128]{3,2,1,0:T(8,128)(2,1)S(1)}, bf16[4,4,72,128]{3,2,1,0:T(8,128)(2,1)S(1)}, u32[]{:S(2)}, u32[]{:S(2)}) collective-permute-start(bf16[4,4,72,128]{3,2,1,0:T(8,128)(2,1)S(1)} %get-tuple-element.32), channel_id=1, source_target_pairs={{0,32},{32,0},{64,96},{96,64},{128,160},{160,128},{192,224},{224,1... | collective-permute-start | bytes 884744 | tf_op jit(solution)/shard_map/ppermute | solution.py:22
  6.0 1.2 %collective-permute-done.got_ref = bf16[4,4,72,128]{3,2,1,0:T(8,128)(2,1)S(1)} collective-permute-done((bf16[4,4,72,128]{3,2,1,0:T(8,128)(2,1)S(1)}, bf16[4,4,72,128]{3,2,1,0:T(8,128)(2,1)S(1)}, u32[]{:S(2)}, u32[]{:S(2)}) %collective-permute-start) | collective-permute-done | bytes 294944 | tf_op jit(solution)/shard_map/ppermute | solution.py:22
  7.2 1.4 %collective-permute-start.1 = (bf16[2,4,72,128]{3,2,1,0:T(8,128)(2,1)S(1)}, bf16[2,4,72,128]{3,2,1,0:T(8,128)(2,1)S(1)}, u32[]{:S(2)}, u32[]{:S(2)}) collective-permute-start(bf16[2,4,72,128]{3,2,1,0:T(8,128)(2,1)S(1)} %get-tuple-element.34), channel_id=1, source_target_pairs={{0,64},{32,96},{64,128},{96,160},{128,192},{160,224},{192,0},{224,... | collective-permute-start | bytes 442376 | tf_op jit(solution)/shard_map/ppermute | solution.py:22
  8.6 5.1 %collective-permute-start.2 = (bf16[2,4,72,128]{3,2,1,0:T(8,128)(2,1)S(1)}, bf16[2,4,72,128]{3,2,1,0:T(8,128)(2,1)S(1)}, u32[]{:S(2)}, u32[]{:S(2)}) collective-permute-start(bf16[2,4,72,128]{3,2,1,0:T(8,128)(2,1)S(1)} %get-tuple-element.35), channel_id=1, source_target_pairs={{0,128},{32,160},{64,192},{96,224},{128,0},{160,32},{192,64},{224,... | collective-permute-start | bytes 442376 | tf_op jit(solution)/shard_map/ppermute | solution.py:22
  13.7 2.4 %collective-permute-start.3 = (bf16[2,4,72,128]{3,2,1,0:T(8,128)(2,1)S(1)}, bf16[2,4,72,128]{3,2,1,0:T(8,128)(2,1)S(1)}, u32[]{:S(2)}, u32[]{:S(2)}) collective-permute-start(bf16[2,4,72,128]{3,2,1,0:T(8,128)(2,1)S(1)} %get-tuple-element.36), channel_id=1, source_target_pairs={{0,192},{32,224},{64,0},{96,32},{128,64},{160,96},{192,128},{224,1... | collective-permute-start | bytes 442376 | tf_op jit(solution)/shard_map/ppermute | solution.py:22
  16.1 7.5 %collective-permute-done.2.refs_2_.t2 = bf16[2,4,72,128]{3,2,1,0:T(8,128)(2,1)S(1)} collective-permute-done((bf16[2,4,72,128]{3,2,1,0:T(8,128)(2,1)S(1)}, bf16[2,4,72,128]{3,2,1,0:T(8,128)(2,1)S(1)}, u32[]{:S(2)}, u32[]{:S(2)}) %collective-permute-start.2) | collective-permute-done | bytes 147488 | tf_op jit(solution)/shard_map/ppermute | solution.py:22
  23.6 4.4 %collective-permute-done.3.refs_3_.t3 = bf16[2,4,72,128]{3,2,1,0:T(8,128)(2,1)S(1)} collective-permute-done((bf16[2,4,72,128]{3,2,1,0:T(8,128)(2,1)S(1)}, bf16[2,4,72,128]{3,2,1,0:T(8,128)(2,1)S(1)}, u32[]{:S(2)}, u32[]{:S(2)}) %collective-permute-start.3) | collective-permute-done | bytes 147488 | tf_op jit(solution)/shard_map/ppermute | solution.py:22
  28.1 3.1 %collective-permute-start.4 = (bf16[8,2,72,128]{3,2,1,0:T(8,128)(2,1)S(1)}, bf16[8,2,72,128]{3,2,1,0:T(8,128)(2,1)S(1)}, u32[]{:S(2)}, u32[]{:S(2)}) collective-permute-start(bf16[8,2,72,128]{3,2,1,0:T(8,128)(2,1)S(1)} %get-tuple-element.37), channel_id=1, source_target_pairs={{0,1},{1,2},{2,3},{3,4},{4,5},{5,6},{6,7},{7,8},{8,9},{9,10},{10,1... | collective-permute-start | bytes 884744 | tf_op jit(solution)/shard_map/ppermute | solution.py:306
  31.2 1.3 %collective-permute-start.5 = (bf16[8,2,72,128]{3,2,1,0:T(8,128)(2,1)S(1)}, bf16[8,2,72,128]{3,2,1,0:T(8,128)(2,1)S(1)}, u32[]{:S(2)}, u32[]{:S(2)}) collective-permute-start(bf16[8,2,72,128]{3,2,1,0:T(8,128)(2,1)S(1)} %get-tuple-element.38), channel_id=1, source_target_pairs={{1,0},{2,1},{3,2},{4,3},{5,4},{6,5},{7,6},{8,7},{9,8},{10,9},{11,1... | collective-permute-start | bytes 884744 | tf_op jit(solution)/shard_map/ppermute | solution.py:307
  32.5 0.1 pad_add_fusion.lat_ref
  32.6 0.2 copy.12
  32.8 0.2 copy.13
  33.1 0.2 concatenate.22.clone
  33.5 3.6 %collective-permute-done.4.top_ref = bf16[8,2,72,128]{3,2,1,0:T(8,128)(2,1)S(1)} collective-permute-done((bf16[8,2,72,128]{3,2,1,0:T(8,128)(2,1)S(1)}, bf16[8,2,72,128]{3,2,1,0:T(8,128)(2,1)S(1)}, u32[]{:S(2)}, u32[]{:S(2)}) %collective-permute-start.4) | collective-permute-done | bytes 294944 | tf_op jit(solution)/shard_map/ppermute | solution.py:306
  37.1 3.8 %collective-permute-done.5.bot_ref = bf16[8,2,72,128]{3,2,1,0:T(8,128)(2,1)S(1)} collective-permute-done((bf16[8,2,72,128]{3,2,1,0:T(8,128)(2,1)S(1)}, bf16[8,2,72,128]{3,2,1,0:T(8,128)(2,1)S(1)}, u32[]{:S(2)}, u32[]{:S(2)}) %collective-permute-start.5) | collective-permute-done | bytes 294944 | tf_op jit(solution)/shard_map/ppermute | solution.py:307
  40.9 11.9 %tile.1 = (bf16[1536,128]{1,0:T(8,128)(2,1)}, bf16[8,6,72,128]{3,2,1,0:T(8,128)(2,1)}, bf16[8,6,72,128]{3,2,1,0:T(8,128)(2,1)}) custom-call(s32[2]{0:T(128)S(1)} %pad_add_fusion.lat_ref, bf16[2,4,72,128]{3,2,1,0:T(8,128)(2,1)S(1)} %get-tuple-element.33.refs_0_.t0, bf16[2,4,72,128]{3,2,1,0:T(8,128)(2,1)S(1)} %collective-permute-done.1.refs_1_.t1, ...), custom_call_target="tpu_custom_call" | custom-call | tf_op jit(solution)/shard_map/tile/pallas_call | solution.py:331
  52.8 10.4 %all-to-all-start = ((bf16[32,48,128]{2,1,0:T(8,128)(2,1)}), bf16[32,48,128]{2,1,0:T(8,128)(2,1)S(1)}, u32[]{:S(2)}, u32[]{:S(2)}) async-start(bf16[32,48,128]{2,1,0:T(8,128)(2,1)} %bitcast.7), calls=%async_computation | async-start | bytes 786432 | tf_op jit(solution)/shard_map/all_to_all | solution.py:365
  63.2 5.4 %output.1 = (bf16[2,4,64,128]{3,2,1,0:T(8,128)(2,1)S(1)}, bf16[2,4,64,128]{3,2,1,0:T(8,128)(2,1)S(1)}, bf16[2,4,64,128]{3,2,1,0:T(8,128)(2,1)S(1)}, bf16[2,4,64,128]{3,2,1,0:T(8,128)(2,1)S(1)}) custom-call(bf16[2,4,72,128]{3,2,1,0:T(8,128)(2,1)S(1)} %get-tuple-element.33.refs_0_.t0, bf16[2,4,72,128]{3,2,1,0:T(8,128)(2,1)S(1)} %collective-permute-done.1.refs_1_.t1, ...), custom_call_target="tpu_custom_call" | custom-call | tf_op jit(solution)/shard_map/output/pallas_call | solution.py:356
  68.6 3.1 %all-to-all-done.parts_ref = bf16[32,48,128]{2,1,0:T(8,128)(2,1)S(1)} async-done(((bf16[32,48,128]{2,1,0:T(8,128)(2,1)}), bf16[32,48,128]{2,1,0:T(8,128)(2,1)S(1)}, u32[]{:S(2)}, u32[]{:S(2)}) %all-to-all-start) | async-done | bytes 393248 | tf_op jit(solution)/shard_map/all_to_all | solution.py:365
  71.7 0.8 total.2
  72.4 8.1 %all-to-all-start.1 = ((f32[8,48,128]{2,1,0:T(8,128)}), f32[8,48,128]{2,1,0:T(8,128)S(1)}, u32[]{:S(2)}, u32[]{:S(2)}) async-start(f32[8,48,128]{2,1,0:T(8,128)} %total.2), calls=%async_computation.1 | async-start | bytes 393216 | tf_op jit(solution)/shard_map/all_to_all | solution.py:365
  80.5 3.5 %collective-permute-start.6 = (bf16[2,4,64,128]{3,2,1,0:T(8,128)(2,1)S(1)}, bf16[2,4,64,128]{3,2,1,0:T(8,128)(2,1)S(1)}, u32[]{:S(2)}, u32[]{:S(2)}) collective-permute-start(bf16[2,4,64,128]{3,2,1,0:T(8,128)(2,1)S(1)} %get-tuple-element.46), channel_id=1, source_target_pairs={{0,192},{32,224},{64,0},{96,32},{128,64},{160,96},{192,128},{224,1... | collective-permute-start | bytes 393224 | tf_op jit(solution)/shard_map/ppermute | solution.py:22
  84.0 9.7 %collective-permute-done.6.refs_1_ = bf16[2,4,64,128]{3,2,1,0:T(8,128)(2,1)S(1)} collective-permute-done((bf16[2,4,64,128]{3,2,1,0:T(8,128)(2,1)S(1)}, bf16[2,4,64,128]{3,2,1,0:T(8,128)(2,1)S(1)}, u32[]{:S(2)}, u32[]{:S(2)}) %collective-permute-start.6) | collective-permute-done | bytes 131104 | tf_op jit(solution)/shard_map/ppermute | solution.py:22
  93.7 0.8 total.3
  94.5 5.5 %all-to-all-start.2 = ((bf16[32,48,128]{2,1,0:T(8,128)(2,1)}), bf16[32,48,128]{2,1,0:T(8,128)(2,1)S(1)}, u32[]{:S(2)}, u32[]{:S(2)}) async-start(bf16[32,48,128]{2,1,0:T(8,128)(2,1)} %total.3), calls=%async_computation.2 | async-start | bytes 786432 | tf_op jit(solution)/shard_map/all_to_all | solution.py:365
  99.9 2.2 %collective-permute-start.8 = (bf16[2,4,64,128]{3,2,1,0:T(8,128)(2,1)S(1)}, bf16[2,4,64,128]{3,2,1,0:T(8,128)(2,1)S(1)}, u32[]{:S(2)}, u32[]{:S(2)}) collective-permute-start(bf16[2,4,64,128]{3,2,1,0:T(8,128)(2,1)S(1)} %get-tuple-element.49), channel_id=1, source_target_pairs={{0,128},{32,160},{64,192},{96,224},{128,0},{160,32},{192,64},{224,... | collective-permute-start | bytes 393224 | tf_op jit(solution)/shard_map/ppermute | solution.py:22
  102.1 7.6 %collective-permute-done.8.refs_2_ = bf16[2,4,64,128]{3,2,1,0:T(8,128)(2,1)S(1)} collective-permute-done((bf16[2,4,64,128]{3,2,1,0:T(8,128)(2,1)S(1)}, bf16[2,4,64,128]{3,2,1,0:T(8,128)(2,1)S(1)}, u32[]{:S(2)}, u32[]{:S(2)}) %collective-permute-start.8) | collective-permute-done | bytes 131104 | tf_op jit(solution)/shard_map/ppermute | solution.py:22
  109.7 1.6 %collective-permute-start.9 = (bf16[4,4,64,128]{3,2,1,0:T(8,128)(2,1)S(1)}, bf16[4,4,64,128]{3,2,1,0:T(8,128)(2,1)S(1)}, u32[]{:S(2)}, u32[]{:S(2)}) collective-permute-start(bf16[4,4,64,128]{3,2,1,0:T(8,128)(2,1)S(1)} %other.1), channel_id=1, source_target_pairs={{0,32},{32,0},{64,96},{96,64},{128,160},{160,128},{192,224},{224,1... | collective-permute-start | bytes 786440 | tf_op jit(solution)/shard_map/ppermute | solution.py:22
  111.3 1.2 %collective-permute-done.9.refs_4_ = bf16[4,4,64,128]{3,2,1,0:T(8,128)(2,1)S(1)} collective-permute-done((bf16[4,4,64,128]{3,2,1,0:T(8,128)(2,1)S(1)}, bf16[4,4,64,128]{3,2,1,0:T(8,128)(2,1)S(1)}, u32[]{:S(2)}, u32[]{:S(2)}) %collective-permute-start.9) | collective-permute-done | bytes 262176 | tf_op jit(solution)/shard_map/ppermute | solution.py:22
  112.4 1.5 %unpack.1 = (bf16[2,64,4,256]{3,2,1,0:T(4,128)(2,1)}, bf16[2,64,4,256]{3,2,1,0:T(4,128)(2,1)}) custom-call(s32[1]{0:T(128)} %bitcast.me_ref, bf16[2,4,64,128]{3,2,1,0:T(8,128)(2,1)S(1)} %get-tuple-element.41.refs_0_, bf16[2,4,64,128]{3,2,1,0:T(8,128)(2,1)S(1)} %collective-permute-done.6.refs_1_, bf16[2,4,64,128]{3,2,1,0:T(8,128)(2,1)S(1)} %collective-permute-done.8.refs_2_, ...), custom_call_target="tpu_custom_call" | custom-call | tf_op jit(solution)/shard_map/unpack/pallas_call | solution.py:405
  114.0 0.9 finish.1
  (21 shorter events, 0.3 us)
Async XLA Ops:
  0.6 15.5 %copy-start.3 = (bf16[3,3,64,128]{3,2,1,0:T(8,128)(2,1)S(1)}, bf16[3,3,64,128]{3,2,1,0:T(8,128)(2,1)}, u32[]{:S(2)}) copy-start(bf16[3,3,64,128]{3,2,1,0:T(8,128)(2,1)} %param.7) | copy-start | bytes 442372
  0.6 15.5 %copy-start.2 = (bf16[3,3,128,64]{2,3,1,0:T(8,128)(2,1)S(1)}, bf16[3,3,128,64]{2,3,1,0:T(8,128)(2,1)}, u32[]{:S(2)}) copy-start(bf16[3,3,128,64]{2,3,1,0:T(8,128)(2,1)} %param.9) | copy-start | bytes 442372
  2.7 4.5 %collective-permute-start = (bf16[4,4,72,128]{3,2,1,0:T(8,128)(2,1)S(1)}, bf16[4,4,72,128]{3,2,1,0:T(8,128)(2,1)S(1)}, u32[]{:S(2)}, u32[]{:S(2)}) collective-permute-start(bf16[4,4,72,128]{3,2,1,0:T(8,128)(2,1)S(1)} %get-tuple-element.32), channel_id=1, source_target_pairs={{0,32},{32,0},{64,96},{96,64},{128,160},{160,128},{192,224},{224,1... | collective-permute-start | bytes 884744 | tf_op jit(solution)/shard_map/ppermute | solution.py:22
  7.2 8.9 %collective-permute-start.1 = (bf16[2,4,72,128]{3,2,1,0:T(8,128)(2,1)S(1)}, bf16[2,4,72,128]{3,2,1,0:T(8,128)(2,1)S(1)}, u32[]{:S(2)}, u32[]{:S(2)}) collective-permute-start(bf16[2,4,72,128]{3,2,1,0:T(8,128)(2,1)S(1)} %get-tuple-element.34), channel_id=1, source_target_pairs={{0,64},{32,96},{64,128},{96,160},{128,192},{160,224},{192,0},{224,... | collective-permute-start | bytes 442376 | tf_op jit(solution)/shard_map/ppermute | solution.py:22
  8.6 15.0 %collective-permute-start.2 = (bf16[2,4,72,128]{3,2,1,0:T(8,128)(2,1)S(1)}, bf16[2,4,72,128]{3,2,1,0:T(8,128)(2,1)S(1)}, u32[]{:S(2)}, u32[]{:S(2)}) collective-permute-start(bf16[2,4,72,128]{3,2,1,0:T(8,128)(2,1)S(1)} %get-tuple-element.35), channel_id=1, source_target_pairs={{0,128},{32,160},{64,192},{96,224},{128,0},{160,32},{192,64},{224,... | collective-permute-start | bytes 442376 | tf_op jit(solution)/shard_map/ppermute | solution.py:22
  13.7 14.3 %collective-permute-start.3 = (bf16[2,4,72,128]{3,2,1,0:T(8,128)(2,1)S(1)}, bf16[2,4,72,128]{3,2,1,0:T(8,128)(2,1)S(1)}, u32[]{:S(2)}, u32[]{:S(2)}) collective-permute-start(bf16[2,4,72,128]{3,2,1,0:T(8,128)(2,1)S(1)} %get-tuple-element.36), channel_id=1, source_target_pairs={{0,192},{32,224},{64,0},{96,32},{128,64},{160,96},{192,128},{224,1... | collective-permute-start | bytes 442376 | tf_op jit(solution)/shard_map/ppermute | solution.py:22
  28.1 9.0 %collective-permute-start.4 = (bf16[8,2,72,128]{3,2,1,0:T(8,128)(2,1)S(1)}, bf16[8,2,72,128]{3,2,1,0:T(8,128)(2,1)S(1)}, u32[]{:S(2)}, u32[]{:S(2)}) collective-permute-start(bf16[8,2,72,128]{3,2,1,0:T(8,128)(2,1)S(1)} %get-tuple-element.37), channel_id=1, source_target_pairs={{0,1},{1,2},{2,3},{3,4},{4,5},{5,6},{6,7},{7,8},{8,9},{9,10},{10,1... | collective-permute-start | bytes 884744 | tf_op jit(solution)/shard_map/ppermute | solution.py:306
  31.2 9.7 %collective-permute-start.5 = (bf16[8,2,72,128]{3,2,1,0:T(8,128)(2,1)S(1)}, bf16[8,2,72,128]{3,2,1,0:T(8,128)(2,1)S(1)}, u32[]{:S(2)}, u32[]{:S(2)}) collective-permute-start(bf16[8,2,72,128]{3,2,1,0:T(8,128)(2,1)S(1)} %get-tuple-element.38), channel_id=1, source_target_pairs={{1,0},{2,1},{3,2},{4,3},{5,4},{6,5},{7,6},{8,7},{9,8},{10,9},{11,1... | collective-permute-start | bytes 884744 | tf_op jit(solution)/shard_map/ppermute | solution.py:307
  33.3 7.6 %copy-start.1 = (bf16[256,128]{1,0:T(8,128)(2,1)S(1)}, bf16[256,128]{1,0:T(8,128)(2,1)}, u32[]{:S(2)}) copy-start(bf16[256,128]{1,0:T(8,128)(2,1)} %pool_ref.1) | copy-start | bytes 196612
  33.4 19.3 %copy-start = (bf16[3,768,128]{2,1,0:T(8,128)(2,1)}, bf16[3,768,128]{2,1,0:T(8,128)(2,1)S(1)}, u32[]{:S(2)}) copy-start(bf16[3,768,128]{2,1,0:T(8,128)(2,1)S(1)} %pad_maximum_fusion._.w2_ref) | copy-start | bytes 1769476
  52.8 18.9 %all-to-all-start = ((bf16[32,48,128]{2,1,0:T(8,128)(2,1)}), bf16[32,48,128]{2,1,0:T(8,128)(2,1)S(1)}, u32[]{:S(2)}, u32[]{:S(2)}) async-start(bf16[32,48,128]{2,1,0:T(8,128)(2,1)} %bitcast.7), calls=%async_computation | async-start | bytes 786432 | tf_op jit(solution)/shard_map/all_to_all | solution.py:365
  72.4 21.3 %all-to-all-start.1 = ((f32[8,48,128]{2,1,0:T(8,128)}), f32[8,48,128]{2,1,0:T(8,128)S(1)}, u32[]{:S(2)}, u32[]{:S(2)}) async-start(f32[8,48,128]{2,1,0:T(8,128)} %total.2), calls=%async_computation.1 | async-start | bytes 393216 | tf_op jit(solution)/shard_map/all_to_all | solution.py:365
  80.5 13.2 %collective-permute-start.6 = (bf16[2,4,64,128]{3,2,1,0:T(8,128)(2,1)S(1)}, bf16[2,4,64,128]{3,2,1,0:T(8,128)(2,1)S(1)}, u32[]{:S(2)}, u32[]{:S(2)}) collective-permute-start(bf16[2,4,64,128]{3,2,1,0:T(8,128)(2,1)S(1)} %get-tuple-element.46), channel_id=1, source_target_pairs={{0,192},{32,224},{64,0},{96,32},{128,64},{160,96},{192,128},{224,1... | collective-permute-start | bytes 393224 | tf_op jit(solution)/shard_map/ppermute | solution.py:22
  84.0 9.7 %collective-permute-start.7 = (bf16[2,4,64,128]{3,2,1,0:T(8,128)(2,1)S(1)}, bf16[2,4,64,128]{3,2,1,0:T(8,128)(2,1)S(1)}, u32[]{:S(2)}, u32[]{:S(2)}) collective-permute-start(bf16[2,4,64,128]{3,2,1,0:T(8,128)(2,1)S(1)} %get-tuple-element.47), channel_id=1, source_target_pairs={{0,64},{32,96},{64,128},{96,160},{128,192},{160,224},{192,0},{224,... | collective-permute-start | bytes 393224 | tf_op jit(solution)/shard_map/ppermute | solution.py:22
  94.5 19.5 %all-to-all-start.2 = ((bf16[32,48,128]{2,1,0:T(8,128)(2,1)}), bf16[32,48,128]{2,1,0:T(8,128)(2,1)S(1)}, u32[]{:S(2)}, u32[]{:S(2)}) async-start(bf16[32,48,128]{2,1,0:T(8,128)(2,1)} %total.3), calls=%async_computation.2 | async-start | bytes 786432 | tf_op jit(solution)/shard_map/all_to_all | solution.py:365
  99.9 9.7 %collective-permute-start.8 = (bf16[2,4,64,128]{3,2,1,0:T(8,128)(2,1)S(1)}, bf16[2,4,64,128]{3,2,1,0:T(8,128)(2,1)S(1)}, u32[]{:S(2)}, u32[]{:S(2)}) collective-permute-start(bf16[2,4,64,128]{3,2,1,0:T(8,128)(2,1)S(1)} %get-tuple-element.49), channel_id=1, source_target_pairs={{0,128},{32,160},{64,192},{96,224},{128,0},{160,32},{192,64},{224,... | collective-permute-start | bytes 393224 | tf_op jit(solution)/shard_map/ppermute | solution.py:22
  109.7 2.7 %collective-permute-start.9 = (bf16[4,4,64,128]{3,2,1,0:T(8,128)(2,1)S(1)}, bf16[4,4,64,128]{3,2,1,0:T(8,128)(2,1)S(1)}, u32[]{:S(2)}, u32[]{:S(2)}) collective-permute-start(bf16[4,4,64,128]{3,2,1,0:T(8,128)(2,1)S(1)} %other.1), channel_id=1, source_target_pairs={{0,32},{32,0},{64,96},{96,64},{128,160},{160,128},{192,224},{224,1... | collective-permute-start | bytes 786440 | tf_op jit(solution)/shard_map/ppermute | solution.py:22
where the time goes:
time: 116 us; the launch traced here: 115 us
  starting transfers between devices  47.7 us (41%)
  waiting for transfers between devices  42.1 us (36%)
  Pallas kernels  23.3 us (20%)
    ppermute x8, waiting for transfers between devices, swap(): return lax.ppermute(value, 'member', pairs)  31.5 us
    all_to_all x3, starting transfers between devices, exchange(): return lax.all_to_all(value, axis, split_axis=0, concat_axis=0, tiled=True)  23.9 us
    ppermute x8, starting transfers between devices, swap(): return lax.ppermute(value, 'member', pairs)  19.4 us
    pallas_call x1, Pallas kernels, block(): pl.pallas_call(tile_kernel, out_shape=[vm((bands * per, channels), BF), c...  11.9 us
    pallas_call x1, Pallas kernels, block(): pl.pallas_call(output_kernel, out_shape=[vm((2, rows, cols * mem_local, 1...  5.36 us
    ppermute x1, waiting for transfers between devices, block(): bot = lax.ppermute(head, 'lat', [(i + 1, i) for i in range(bands - 1)])  3.85 us
    ppermute x1, waiting for transfers between devices, block(): top = lax.ppermute(tail, 'lat', [(i, i + 1) for i in range(bands - 1)])  3.6 us
    ppermute x1, starting transfers between devices, block(): top = lax.ppermute(tail, 'lat', [(i, i + 1) for i in range(bands - 1)])  3.13 us
  transfers between devices with their start and end apart: 13, of which 9 were waited for; matrix products, arithmetic and copies ran while one was open for 1% of the time, Pallas kernels for 6%

commit v1 on v0

--- a/solution.py
+++ b/solution.py
@@ -12,6 +12,9 @@
 BF = jnp.bfloat16
 F32 = jnp.float32
 WIDE = 80
+
+
+ORDER = (0, 1, 3, 2)
 
 
 def swap(value, steps, cross, groups):
@@ -66,7 +69,7 @@
             plane[r, pl.ds(4 + 2 * lon + m, 2, stride=2), :] = both[:2]
     for d in range(chips):
         for cross, ref in enumerate((keep_ref, give_ref)):
-            k = column_block(me_ref[0], d, cross, 2 * chips)
+            k = column_block(me_ref[0], ORDER[d], cross, 2 * chips)
             for r in range(rows):
                 ref[d, r] = plane[r, pl.ds(pl.multiple_of(k * (width - 8), 8), width), :].astype(BF)
 
@@ -97,7 +100,7 @@
     width = theirs_ref.shape[2]
     for d in range(chips):
         for cross in range(2):
-            k = column_block(me_ref[0], d, cross, 2 * chips)
+            k = column_block(me_ref[0], ORDER[d], cross, 2 * chips)
             for r in range(rows):
                 piece = theirs_ref[d, r] if cross else tiles[d][0, r]
                 plane[r, pl.ds(pl.multiple_of(k * width, 8), width), :] = piece.astype(F32)
@@ -109,9 +112,9 @@
 
 
 def tile_kernel(
-    lat_ref, t0, t1, t2, t3, top_ref, bot_ref, w1_ref, pool_ref, _,
+    lat_ref, t0, t1, t2, t3, top0, top1, bot0, bot1, w1_ref, pool_ref, _,
     grads_ref, hid_ref, dpre_ref,
-    own_ref, pre_s, dh_s, act_s, xo_s, hq_s, dpo_s, hid_s, dpre_s, sum_s, var_s, shared_s, ca_s, cs_s, sems,
+    own_ref, top_ref, bot_ref, pre_s, dh_s, act_s, xo_s, oc_s, hq_s, dpo_s, hid_s, dpre_s, sum_s, var_s, shared_s, ca_s, cs_s, sems,
 ):
     srcs, rows, width, _ = own_ref.shape
     inner = rows + 2
@@ -119,6 +122,11 @@
     nlat = lat_ref[1]
     for d, tile in enumerate((t0, t1, t2, t3)):
         own_ref[2 * d : 2 * d + 2] = tile[...]
+    split = top0.shape[0]
+    top_ref[:split] = top0[...]
+    top_ref[split:] = top1[...]
+    bot_ref[:split] = bot0[...]
+    bot_ref[split:] = bot1[...]
     members = 2 * srcs
     channels = pre_s.shape[-1]
     shape = (inner, WIDE, channels)
@@ -141,10 +149,12 @@
         x = jnp.concatenate([x, jnp.zeros((rows + 4, WIDE - width, 128), F32)], axis=1)
         x1, x2, x3 = up(x, 2), up(x, 4), up(x, 6)
         xs = jnp.concatenate([x, x1, x2], axis=-1).astype(BF)
-        xo_s[s] = jnp.concatenate([v[1 : 1 + inner, :cols] for v in (x1, x2, x3)], axis=-1).astype(BF)
-        acc = dot(xs[0:inner].reshape(inner * WIDE, 384), w1_ref[0])
-        acc += dot(xs[1 : 1 + inner].reshape(inner * WIDE, 384), w1_ref[1])
-        acc += dot(xs[2 : 2 + inner].reshape(inner * WIDE, 384), w1_ref[2])
+        own = [v[1 : 1 + inner, :cols] for v in (x1, x2, x3)]
+        half = channels // 2
+        xo_s[s] = jnp.concatenate([v[..., :half] for v in own], axis=-1).astype(BF)
+        oc_s[s] = own[1][1 : 1 + rows].astype(BF)
+        xs = jnp.concatenate([xs[p : p + inner] for p in range(3)], axis=-1)
+        acc = dot(xs.reshape(inner * WIDE, 1152), w1_ref[...])
         pre = acc[:, :channels].reshape(shape)
         pre_s[s] = pre
         dh_s[s] = acc[:, channels:].reshape(shape)
@@ -213,15 +223,16 @@
 
     total = srcs * rows * cols
     dpo = dpo_s[...].reshape(total, channels)
-    own = xo_s[:, 1 : 1 + rows, :, 128:256].reshape(total, 128)
+    own = oc_s[...].reshape(total, 128)
     half = channels // 2
+    taps = 3 * half
     for p in range(3):
-        g_in = dot_rows(dpo, xo_s[:, p : p + rows].reshape(total, 384))
-        g_out = dot_rows(own, hq_s[:, p : p + rows].reshape(total, 384))
-        for q in range(3):
-            t = 3 * p + q
-            grads_ref[t * half : (t + 1) * half, :] = g_in[:, q * 128 : (q + 1) * 128].T[:half].astype(BF)
-            grads_ref[(9 + t) * half : (10 + t) * half, :] = g_out[half:, q * 128 : (q + 1) * 128].astype(BF)
+        g_in = dot_rows(dpo, xo_s[:, p : p + rows].reshape(total, taps))
+        grads_ref[p * taps : (p + 1) * taps, :] = g_in.T.astype(BF)
+    hqs = jnp.concatenate([hq_s[:, p : p + rows].reshape(total, 384) for p in range(3)], axis=-1)
+    g_out = dot_rows(own, hqs)
+    for t in range(9):
+        grads_ref[(9 + t) * half : (10 + t) * half, :] = g_out[half:, t * 128 : (t + 1) * 128].astype(BF)
     used = 18 * half + 2 * channels
     grads_ref[18 * half : used, :] = g_pool.astype(BF)
     if used < grads_ref.shape[0]:
@@ -295,16 +306,26 @@
         out_specs=[vspec] * chips,
         name="pair",
     )(*near(keep, got))
-    tiles = [tiles[0]] + [swap(tiles[d], d, 0, groups) for d in range(1, chips)]
-    head, tail = pl.pallas_call(
-        edges_kernel,
-        out_shape=[vm((groups, 2, width, 128), BF)] * 2,
-        in_specs=[vspec] * chips,
-        out_specs=[vspec] * 2,
-        name="edges",
-    )(*near(*tiles))
-    top = lax.ppermute(tail, "lat", [(i, i + 1) for i in range(bands - 1)])
-    bot = lax.ppermute(head, "lat", [(i + 1, i) for i in range(bands - 1)])
+    tiles = [tiles[0]] + [swap(tiles[i], ORDER[i], 0, groups) for i in range(1, chips)]
+
+    def edges(*sources):
+        return pl.pallas_call(
+            edges_kernel,
+            out_shape=[vm((2 * len(sources), 2, width, 128), BF)] * 2,
+            in_specs=[vspec] * len(sources),
+            out_specs=[vspec] * 2,
+            name="edges",
+        )(*near(*sources))
+
+    def to_bands(head, tail):
+        top = lax.ppermute(tail, "lat", [(i, i + 1) for i in range(bands - 1)])
+        bot = lax.ppermute(head, "lat", [(i + 1, i) for i in range(bands - 1)])
+        return top, bot
+
+    first_edges = edges(*tiles[:3])
+    top0, bot0 = to_bands(*first_edges)
+    last_edges = edges(*tiles[3:])
+    top1, bot1 = to_bands(*last_edges)
 
     flip_in = jnp.transpose(conv_in[::-1, ::-1], (0, 1, 3, 2))
     flip_out = jnp.transpose(conv_out[::-1, ::-1], (0, 1, 3, 2))
@@ -312,7 +333,7 @@
     z2 = jnp.zeros_like(conv_out)
     w1 = jnp.concatenate(
         [jnp.concatenate([conv_in, z1], axis=3), jnp.concatenate([z1, flip_out], axis=3)], axis=2
-    ).reshape(3, 384, 256)
+    ).reshape(1152, 256)
     w2 = jnp.concatenate(
         [
             jnp.concatenate([conv_out, z2], axis=3).reshape(3, 384, 128),
@@ -331,14 +352,17 @@
     grads, hid, dpre = pl.pallas_call(
         tile_kernel,
         out_shape=[vm((bands * per, channels), BF), compact, compact],
-        in_specs=[sspec] + [vspec] * (chips + 4) + [hspec],
+        in_specs=[sspec] + [vspec] * (chips + 6) + [hspec],
         out_specs=[vspec, hspec, hspec],
         scratch_shapes=[
             vm((groups, rows, width, 128), BF),
+            vm((groups, 2, width, 128), BF),
+            vm((groups, 2, width, 128), BF),
             vm((groups,) + plane, F32),
             vm((groups,) + plane, F32),
             vm((groups,) + plane, F32),
-            vm(shifted, BF),
+            vm(shifted[:3] + (192,), BF),
+            vm((groups, rows, cols * mem_local, 128), BF),
             vm(shifted, BF),
             vm((groups, rows, cols * mem_local, channels), BF),
             vm(compact.shape, BF),
@@ -352,7 +376,7 @@
         ],
         compiler_params=pltpu.CompilerParams(vmem_limit_bytes=48 * 1024 * 1024),
         name="tile",
-    )(lat, *near(*tiles, top, bot, w1, pool_weight), w2)
+    )(lat, *near(*tiles, top0, top1, bot0, bot1, w1, pool_weight), w2)
     pieces = list(pl.pallas_call(
         output_kernel,
         out_shape=[vm((2, rows, cols * mem_local, 128), BF)] * chips,
@@ -374,12 +398,13 @@
         )(*near(parts))
 
     parts = exchange(grads.reshape(bands, per, channels), "lat")
-    far = swap(pieces[2], chips - 2, 0, groups)
-    parts, pieces[1], pieces[3] = lax.optimization_barrier((parts, pieces[1], pieces[3]))
-    pieces = [pieces[0]] + [far if d == 2 else swap(pieces[d], chips - d, 0, groups) for d in range(1, chips)]
+    far = swap(pieces[3], chips - ORDER[3], 0, groups)
+    parts, pieces[1], pieces[2] = lax.optimization_barrier((parts, pieces[1], pieces[2]))
+    pieces[1:3] = [swap(piece, chips - d, 0, groups) for d, piece in zip(ORDER[1:3], pieces[1:3])]
+    pieces[3] = far
     parts = add_up(parts, groups, F32)
     parts = exchange(parts, "member")
-    parts, pieces[1], pieces[3] = lax.optimization_barrier((parts, pieces[1], pieces[3]))
+    parts = add_up(parts, bands, BF)
     other = pl.pallas_call(
         other_kernel,
         out_shape=vm((chips, rows, cols * mem_local, 128), BF),
@@ -388,7 +413,7 @@
         name="other",
     )(*near(*pieces))
     theirs = swap(other, 0, 1, groups)
-    full = exchange(add_up(parts, bands, BF), "lat").reshape(bands * per, channels)
+    full = exchange(parts, "lat").reshape(bands * per, channels)
     members = mem_local * groups
     scale = 1.0 / math.sqrt(members * bands * rows * lon)
     half = channels // 2

time: 116 us -> 117 us (level)
  blocking collectives: 0 us -> 20.7 us
  waiting for transfers between devices: 42.1 us -> 25.8 us
  starting transfers between devices: 47.7 us -> 45.5 us
  Pallas kernels: 23.3 us -> 21.8 us
    all_to_all x0 -> x1, blocking collectives: none -> 20.7 us  [exchange(): return lax.all_to_all(value, axis, split_axis=0, concat_axis=0, tiled=True)]
    ppermute x8, waiting for transfers between devices: 31.5 us -> 19 us  [swap(): return lax.ppermute(value, 'member', pairs)]
    all_to_all x3 -> x2, starting transfers between devices: 23.9 us -> 17.8 us  [exchange(): return lax.all_to_all(value, axis, split_axis=0, concat_axis=0, tiled=True)]
    ppermute x2 -> x4, starting transfers between devices: 4.43 us -> 9.7 us  [the longest x2 7.12 us: to_bands(): top = lax.ppermute(tail, 'lat', [(i, i + 1) for i in range(bands - 1)])]
    ppermute x2 -> x4, waiting for transfers between devices: 7.45 us -> 3.72 us  [the longest x2 3.71 us: to_bands(): bot = lax.ppermute(head, 'lat', [(i + 1, i) for i in range(bands - 1)])]
    ppermute x8, starting transfers between devices: 19.4 us -> 18 us  [swap(): return lax.ppermute(value, 'member', pairs)]
    all_to_all x3 -> x2, waiting for transfers between devices: 3.11 us -> 3.09 us  [exchange(): return lax.all_to_all(value, axis, split_axis=0, concat_axis=0, tiled=True)]
  transfers between devices with their start and end apart: 13 -> 14, of which waited for: 9 -> 7; matrix products, arithmetic and copies ran while one was open for 1% -> 2% of each run, Pallas kernels for 6% -> 6%
where the time goes in v1:
time: 117 us; the launch traced here: 116 us
  starting transfers between devices  45.5 us (39%)
  waiting for transfers between devices  25.8 us (22%)
  Pallas kernels  21.8 us (19%)
  blocking collectives  20.7 us (18%)
  local copies, waits for them, and re-layouts  1.63 us (1%)
    all_to_all x1, blocking collectives, exchange(): return lax.all_to_all(value, axis, split_axis=0, concat_axis=0, tiled=True)  20.7 us
    ppermute x8, waiting for transfers between devices, swap(): return lax.ppermute(value, 'member', pairs)  19 us
    ppermute x8, starting transfers between devices, swap(): return lax.ppermute(value, 'member', pairs)  18 us
    all_to_all x2, starting transfers between devices, exchange(): return lax.all_to_all(value, axis, split_axis=0, concat_axis=0, tiled=True)  17.8 us
    pallas_call x1, Pallas kernels, block(): pl.pallas_call(tile_kernel, out_shape=[vm((bands * per, channels), BF), c...  10.9 us
    ppermute x2, starting transfers between devices, to_bands(): top = lax.ppermute(tail, 'lat', [(i, i + 1) for i in range(bands - 1)])  7.12 us
    pallas_call x1, Pallas kernels, block(): pl.pallas_call(output_kernel, out_shape=[vm((2, rows, cols * mem_local, 1...  5.43 us
    ppermute x2, waiting for transfers between devices, to_bands(): bot = lax.ppermute(head, 'lat', [(i + 1, i) for i in range(bands - 1)])  3.71 us
  transfers between devices with their start and end apart: 14, of which 7 were waited for; matrix products, arithmetic and copies ran while one was open for 2% of the time, Pallas kernels for 6%

profile of v1, /device:TPU:1, one launch (start us, length us, event | category | flops | bytes accessed | tf_op | source)
XLA Modules:
  0.0 116.4 jit_solution(6419443506815233429)
XLA Ops:
  0.6 2.0 %pack.1 = (bf16[4,4,72,128]{3,2,1,0:T(8,128)(2,1)S(1)}, bf16[4,4,72,128]{3,2,1,0:T(8,128)(2,1)S(1)}) custom-call(s32[1]{0:T(128)} %bitcast.me_ref, bf16[2,64,4,256]{3,2,1,0:T(4,128)(2,1)} %ens_ref.1, bf16[2,64,4,256]{3,2,1,0:T(4,128)(2,1)} %cot_ref.1), custom_call_target="tpu_custom_call" | custom-call | tf_op jit(solution)/shard_map/pack/pallas_call | solution.py:293
  2.7 3.3 %collective-permute-start = (bf16[4,4,72,128]{3,2,1,0:T(8,128)(2,1)S(1)}, bf16[4,4,72,128]{3,2,1,0:T(8,128)(2,1)S(1)}, u32[]{:S(2)}, u32[]{:S(2)}) collective-permute-start(bf16[4,4,72,128]{3,2,1,0:T(8,128)(2,1)S(1)} %get-tuple-element.31), channel_id=1, source_target_pairs={{0,32},{32,0},{64,96},{96,64},{128,160},{160,128},{192,224},{224,1... | collective-permute-start | bytes 884744 | tf_op jit(solution)/shard_map/ppermute | solution.py:25
  6.0 0.9 reverse_bitcast_fusion.1
  6.9 0.3 collective-permute-done.got_ref
  7.2 1.4 %collective-permute-start.1 = (bf16[2,4,72,128]{3,2,1,0:T(8,128)(2,1)S(1)}, bf16[2,4,72,128]{3,2,1,0:T(8,128)(2,1)S(1)}, u32[]{:S(2)}, u32[]{:S(2)}) collective-permute-start(bf16[2,4,72,128]{3,2,1,0:T(8,128)(2,1)S(1)} %get-tuple-element.33), channel_id=1, source_target_pairs={{0,64},{32,96},{64,128},{96,160},{128,192},{160,224},{192,0},{224,... | collective-permute-start | bytes 442376 | tf_op jit(solution)/shard_map/ppermute | solution.py:25
  8.6 3.1 %collective-permute-start.2 = (bf16[2,4,72,128]{3,2,1,0:T(8,128)(2,1)S(1)}, bf16[2,4,72,128]{3,2,1,0:T(8,128)(2,1)S(1)}, u32[]{:S(2)}, u32[]{:S(2)}) collective-permute-start(bf16[2,4,72,128]{3,2,1,0:T(8,128)(2,1)S(1)} %get-tuple-element.34), channel_id=1, source_target_pairs={{0,192},{32,224},{64,0},{96,32},{128,64},{160,96},{192,128},{224,1... | collective-permute-start | bytes 442376 | tf_op jit(solution)/shard_map/ppermute | solution.py:25
  11.8 4.5 %collective-permute-start.3 = (bf16[2,4,72,128]{3,2,1,0:T(8,128)(2,1)S(1)}, bf16[2,4,72,128]{3,2,1,0:T(8,128)(2,1)S(1)}, u32[]{:S(2)}, u32[]{:S(2)}) collective-permute-start(bf16[2,4,72,128]{3,2,1,0:T(8,128)(2,1)S(1)} %get-tuple-element.35), channel_id=1, source_target_pairs={{0,128},{32,160},{64,192},{96,224},{128,0},{160,32},{192,64},{224,... | collective-permute-start | bytes 442376 | tf_op jit(solution)/shard_map/ppermute | solution.py:25
  16.2 0.2 copy.12
  16.5 0.2 copy.13
  16.7 0.2 concatenate.22.clone
  17.0 6.2 %collective-permute-done.2.refs_2_.t2 = bf16[2,4,72,128]{3,2,1,0:T(8,128)(2,1)S(1)} collective-permute-done((bf16[2,4,72,128]{3,2,1,0:T(8,128)(2,1)S(1)}, bf16[2,4,72,128]{3,2,1,0:T(8,128)(2,1)S(1)}, u32[]{:S(2)}, u32[]{:S(2)}) %collective-permute-start.2) | collective-permute-done | bytes 147488 | tf_op jit(solution)/shard_map/ppermute | solution.py:25
  23.2 3.1 %collective-permute-start.4 = (bf16[6,2,72,128]{3,2,1,0:T(8,128)(2,1)S(1)}, bf16[6,2,72,128]{3,2,1,0:T(8,128)(2,1)S(1)}, u32[]{:S(2)}, u32[]{:S(2)}) collective-permute-start(bf16[6,2,72,128]{3,2,1,0:T(8,128)(2,1)S(1)} %get-tuple-element.36), channel_id=1, source_target_pairs={{0,1},{1,2},{2,3},{3,4},{4,5},{5,6},{6,7},{7,8},{8,9},{9,10},{10,1... | collective-permute-start | bytes 663560 | tf_op jit(solution)/shard_map/ppermute | solution.py:321
  26.4 1.3 %collective-permute-start.6 = (bf16[6,2,72,128]{3,2,1,0:T(8,128)(2,1)S(1)}, bf16[6,2,72,128]{3,2,1,0:T(8,128)(2,1)S(1)}, u32[]{:S(2)}, u32[]{:S(2)}) collective-permute-start(bf16[6,2,72,128]{3,2,1,0:T(8,128)(2,1)S(1)} %get-tuple-element.38), channel_id=1, source_target_pairs={{1,0},{2,1},{3,2},{4,3},{5,4},{6,5},{7,6},{8,7},{9,8},{10,9},{11,1... | collective-permute-start | bytes 663560 | tf_op jit(solution)/shard_map/ppermute | solution.py:322
  27.7 4.0 %collective-permute-start.5 = (bf16[2,2,72,128]{3,2,1,0:T(8,128)(2,1)S(1)}, bf16[2,2,72,128]{3,2,1,0:T(8,128)(2,1)S(1)}, u32[]{:S(2)}, u32[]{:S(2)}) collective-permute-start(bf16[2,2,72,128]{3,2,1,0:T(8,128)(2,1)S(1)} %get-tuple-element.37), channel_id=1, source_target_pairs={{0,1},{1,2},{2,3},{3,4},{4,5},{5,6},{6,7},{7,8},{8,9},{9,10},{10,1... | collective-permute-start | bytes 221192 | tf_op jit(solution)/shard_map/ppermute | solution.py:321
  31.7 1.3 %collective-permute-start.7 = (bf16[2,2,72,128]{3,2,1,0:T(8,128)(2,1)S(1)}, bf16[2,2,72,128]{3,2,1,0:T(8,128)(2,1)S(1)}, u32[]{:S(2)}, u32[]{:S(2)}) collective-permute-start(bf16[2,2,72,128]{3,2,1,0:T(8,128)(2,1)S(1)} %get-tuple-element.39), channel_id=1, source_target_pairs={{1,0},{2,1},{3,2},{4,3},{5,4},{6,5},{7,6},{8,7},{9,8},{10,9},{11,1... | collective-permute-start | bytes 221192 | tf_op jit(solution)/shard_map/ppermute | solution.py:322
  33.0 0.1 pad_add_fusion.lat_ref
  33.1 3.7 %collective-permute-done.7.bot1 = bf16[2,2,72,128]{3,2,1,0:T(8,128)(2,1)S(1)} collective-permute-done((bf16[2,2,72,128]{3,2,1,0:T(8,128)(2,1)S(1)}, bf16[2,2,72,128]{3,2,1,0:T(8,128)(2,1)S(1)}, u32[]{:S(2)}, u32[]{:S(2)}) %collective-permute-start.7) | collective-permute-done | bytes 73760 | tf_op jit(solution)/shard_map/ppermute | solution.py:322
  36.9 10.9 %tile.1 = (bf16[1536,128]{1,0:T(8,128)(2,1)}, bf16[8,6,72,128]{3,2,1,0:T(8,128)(2,1)}, bf16[8,6,72,128]{3,2,1,0:T(8,128)(2,1)}) custom-call(s32[2]{0:T(128)S(1)} %pad_add_fusion.lat_ref, bf16[2,4,72,128]{3,2,1,0:T(8,128)(2,1)S(1)} %get-tuple-element.32.refs_0_.t0, bf16[2,4,72,128]{3,2,1,0:T(8,128)(2,1)S(1)} %collective-permute-done.1.refs_1_.t1, ...), custom_call_target="tpu_custom_call" | custom-call | tf_op jit(solution)/shard_map/tile/pallas_call | solution.py:352
  47.8 13.4 %all-to-all-start = ((bf16[32,48,128]{2,1,0:T(8,128)(2,1)}), bf16[32,48,128]{2,1,0:T(8,128)(2,1)S(1)}, u32[]{:S(2)}, u32[]{:S(2)}) async-start(bf16[32,48,128]{2,1,0:T(8,128)(2,1)} %bitcast.7), calls=%async_computation | async-start | bytes 786432 | tf_op jit(solution)/shard_map/all_to_all | solution.py:389
  61.2 5.4 %output.1 = (bf16[2,4,64,128]{3,2,1,0:T(8,128)(2,1)S(1)}, bf16[2,4,64,128]{3,2,1,0:T(8,128)(2,1)S(1)}, bf16[2,4,64,128]{3,2,1,0:T(8,128)(2,1)S(1)}, bf16[2,4,64,128]{3,2,1,0:T(8,128)(2,1)S(1)}) custom-call(bf16[2,4,72,128]{3,2,1,0:T(8,128)(2,1)S(1)} %get-tuple-element.32.refs_0_.t0, bf16[2,4,72,128]{3,2,1,0:T(8,128)(2,1)S(1)} %collective-permute-done.1.refs_1_.t1, ...), custom_call_target="tpu_custom_call" | custom-call | tf_op jit(solution)/shard_map/output/pallas_call | solution.py:380
  66.7 3.1 %all-to-all-done.parts_ref = bf16[32,48,128]{2,1,0:T(8,128)(2,1)S(1)} async-done(((bf16[32,48,128]{2,1,0:T(8,128)(2,1)}), bf16[32,48,128]{2,1,0:T(8,128)(2,1)S(1)}, u32[]{:S(2)}, u32[]{:S(2)}) %all-to-all-start) | async-done | bytes 393248 | tf_op jit(solution)/shard_map/all_to_all | solution.py:389
  69.8 20.7 %all_to_all.15.parts_ref = f32[8,48,128]{2,1,0:T(8,128)S(1)} all-to-all(f32[8,48,128]{2,1,0:T(8,128)S(1)} %total.2), channel_id=1, replica_groups=mesh['member'=8,'lat'=32] {'member'}, dimensions={0} | all-to-all | bytes 393216 | tf_op jit(solution)/shard_map/all_to_all | solution.py:389
  90.6 0.8 total.3
  91.3 4.4 %all-to-all-start.2 = ((bf16[32,48,128]{2,1,0:T(8,128)(2,1)}), bf16[32,48,128]{2,1,0:T(8,128)(2,1)S(1)}, u32[]{:S(2)}, u32[]{:S(2)}) async-start(bf16[32,48,128]{2,1,0:T(8,128)(2,1)} %total.3), calls=%async_computation.2 | async-start | bytes 786432 | tf_op jit(solution)/shard_map/all_to_all | solution.py:389
  95.8 1.0 collective-permute-start.10
  96.8 3.3 %collective-permute-start.8 = (bf16[2,4,64,128]{3,2,1,0:T(8,128)(2,1)S(1)}, bf16[2,4,64,128]{3,2,1,0:T(8,128)(2,1)S(1)}, u32[]{:S(2)}, u32[]{:S(2)}) collective-permute-start(bf16[2,4,64,128]{3,2,1,0:T(8,128)(2,1)S(1)} %get-tuple-element.46), channel_id=1, source_target_pairs={{0,192},{32,224},{64,0},{96,32},{128,64},{160,96},{192,128},{224,1... | collective-permute-start | bytes 393224 | tf_op jit(solution)/shard_map/ppermute | solution.py:25
  100.0 4.0 %collective-permute-done.10.refs_3_ = bf16[2,4,64,128]{3,2,1,0:T(8,128)(2,1)S(1)} collective-permute-done((bf16[2,4,64,128]{3,2,1,0:T(8,128)(2,1)S(1)}, bf16[2,4,64,128]{3,2,1,0:T(8,128)(2,1)S(1)}, u32[]{:S(2)}, u32[]{:S(2)}) %collective-permute-start.10) | collective-permute-done | bytes 131104 | tf_op jit(solution)/shard_map/ppermute | solution.py:25
  104.0 7.3 %collective-permute-done.9.refs_2_ = bf16[2,4,64,128]{3,2,1,0:T(8,128)(2,1)S(1)} collective-permute-done((bf16[2,4,64,128]{3,2,1,0:T(8,128)(2,1)S(1)}, bf16[2,4,64,128]{3,2,1,0:T(8,128)(2,1)S(1)}, u32[]{:S(2)}, u32[]{:S(2)}) %collective-permute-start.9) | collective-permute-done | bytes 131104 | tf_op jit(solution)/shard_map/ppermute | solution.py:25
  111.3 1.5 %collective-permute-start.11 = (bf16[4,4,64,128]{3,2,1,0:T(8,128)(2,1)S(1)}, bf16[4,4,64,128]{3,2,1,0:T(8,128)(2,1)S(1)}, u32[]{:S(2)}, u32[]{:S(2)}) collective-permute-start(bf16[4,4,64,128]{3,2,1,0:T(8,128)(2,1)S(1)} %other.1), channel_id=1, source_target_pairs={{0,32},{32,0},{64,96},{96,64},{128,160},{160,128},{192,224},{224,1... | collective-permute-start | bytes 786440 | tf_op jit(solution)/shard_map/ppermute | solution.py:25
  112.8 1.2 collective-permute-done.11.refs_4_
  114.0 1.5 %unpack.1 = (bf16[2,64,4,256]{3,2,1,0:T(4,128)(2,1)}, bf16[2,64,4,256]{3,2,1,0:T(4,128)(2,1)}) custom-call(s32[1]{0:T(128)} %bitcast.me_ref, bf16[2,4,64,128]{3,2,1,0:T(8,128)(2,1)S(1)} %get-tuple-element.42.refs_0_, bf16[2,4,64,128]{3,2,1,0:T(8,128)(2,1)S(1)} %collective-permute-done.8.refs_1_, bf16[2,4,64,128]{3,2,1,0:T(8,128)(2,1)S(1)} %collective-permute-done.9.refs_2_, ...), custom_call_target="tpu_custom_call" | custom-call | tf_op jit(solution)/shard_map/unpack/pallas_call | solution.py:430
  115.5 0.9 finish.1
  (25 shorter events, 0.4 us)
Async XLA Ops:
  0.6 11.1 %copy-start.2 = (bf16[3,3,64,128]{3,2,1,0:T(8,128)(2,1)S(1)}, bf16[3,3,64,128]{3,2,1,0:T(8,128)(2,1)}, u32[]{:S(2)}) copy-start(bf16[3,3,64,128]{3,2,1,0:T(8,128)(2,1)} %param.7) | copy-start | bytes 442372
  2.7 4.5 %collective-permute-start = (bf16[4,4,72,128]{3,2,1,0:T(8,128)(2,1)S(1)}, bf16[4,4,72,128]{3,2,1,0:T(8,128)(2,1)S(1)}, u32[]{:S(2)}, u32[]{:S(2)}) collective-permute-start(bf16[4,4,72,128]{3,2,1,0:T(8,128)(2,1)S(1)} %get-tuple-element.31), channel_id=1, source_target_pairs={{0,32},{32,0},{64,96},{96,64},{128,160},{160,128},{192,224},{224,1... | collective-permute-start | bytes 884744 | tf_op jit(solution)/shard_map/ppermute | solution.py:25
  7.2 9.1 %copy-start.3 = (bf16[3,3,128,64]{2,3,1,0:T(8,128)(2,1)S(1)}, bf16[3,3,128,64]{2,3,1,0:T(8,128)(2,1)}, u32[]{:S(2)}) copy-start(bf16[3,3,128,64]{2,3,1,0:T(8,128)(2,1)} %param.9) | copy-start | bytes 442372
  7.2 9.7 %collective-permute-start.1 = (bf16[2,4,72,128]{3,2,1,0:T(8,128)(2,1)S(1)}, bf16[2,4,72,128]{3,2,1,0:T(8,128)(2,1)S(1)}, u32[]{:S(2)}, u32[]{:S(2)}) collective-permute-start(bf16[2,4,72,128]{3,2,1,0:T(8,128)(2,1)S(1)} %get-tuple-element.33), channel_id=1, source_target_pairs={{0,64},{32,96},{64,128},{96,160},{128,192},{160,224},{192,0},{224,... | collective-permute-start | bytes 442376 | tf_op jit(solution)/shard_map/ppermute | solution.py:25
  8.6 14.6 %collective-permute-start.2 = (bf16[2,4,72,128]{3,2,1,0:T(8,128)(2,1)S(1)}, bf16[2,4,72,128]{3,2,1,0:T(8,128)(2,1)S(1)}, u32[]{:S(2)}, u32[]{:S(2)}) collective-permute-start(bf16[2,4,72,128]{3,2,1,0:T(8,128)(2,1)S(1)} %get-tuple-element.34), channel_id=1, source_target_pairs={{0,192},{32,224},{64,0},{96,32},{128,64},{160,96},{192,128},{224,1... | collective-permute-start | bytes 442376 | tf_op jit(solution)/shard_map/ppermute | solution.py:25
  11.8 16.0 %collective-permute-start.3 = (bf16[2,4,72,128]{3,2,1,0:T(8,128)(2,1)S(1)}, bf16[2,4,72,128]{3,2,1,0:T(8,128)(2,1)S(1)}, u32[]{:S(2)}, u32[]{:S(2)}) collective-permute-start(bf16[2,4,72,128]{3,2,1,0:T(8,128)(2,1)S(1)} %get-tuple-element.35), channel_id=1, source_target_pairs={{0,128},{32,160},{64,192},{96,224},{128,0},{160,32},{192,64},{224,... | collective-permute-start | bytes 442376 | tf_op jit(solution)/shard_map/ppermute | solution.py:25
  23.2 13.7 %copy-start.1 = (bf16[256,128]{1,0:T(8,128)(2,1)S(1)}, bf16[256,128]{1,0:T(8,128)(2,1)}, u32[]{:S(2)}) copy-start(bf16[256,128]{1,0:T(8,128)(2,1)} %pool_ref.1) | copy-start | bytes 196612
  23.2 13.6 %collective-permute-start.4 = (bf16[6,2,72,128]{3,2,1,0:T(8,128)(2,1)S(1)}, bf16[6,2,72,128]{3,2,1,0:T(8,128)(2,1)S(1)}, u32[]{:S(2)}, u32[]{:S(2)}) collective-permute-start(bf16[6,2,72,128]{3,2,1,0:T(8,128)(2,1)S(1)} %get-tuple-element.36), channel_id=1, source_target_pairs={{0,1},{1,2},{2,3},{3,4},{4,5},{5,6},{6,7},{7,8},{8,9},{9,10},{10,1... | collective-permute-start | bytes 663560 | tf_op jit(solution)/shard_map/ppermute | solution.py:321
  26.4 10.5 %collective-permute-start.6 = (bf16[6,2,72,128]{3,2,1,0:T(8,128)(2,1)S(1)}, bf16[6,2,72,128]{3,2,1,0:T(8,128)(2,1)S(1)}, u32[]{:S(2)}, u32[]{:S(2)}) collective-permute-start(bf16[6,2,72,128]{3,2,1,0:T(8,128)(2,1)S(1)} %get-tuple-element.38), channel_id=1, source_target_pairs={{1,0},{2,1},{3,2},{4,3},{5,4},{6,5},{7,6},{8,7},{9,8},{10,9},{11,1... | collective-permute-start | bytes 663560 | tf_op jit(solution)/shard_map/ppermute | solution.py:322
  27.7 20.1 %copy-start = (bf16[3,768,128]{2,1,0:T(8,128)(2,1)}, bf16[3,768,128]{2,1,0:T(8,128)(2,1)S(1)}, u32[]{:S(2)}) copy-start(bf16[3,768,128]{2,1,0:T(8,128)(2,1)S(1)} %pad_maximum_fusion._.w2_ref) | copy-start | bytes 1769476
  27.7 5.4 %collective-permute-start.5 = (bf16[2,2,72,128]{3,2,1,0:T(8,128)(2,1)S(1)}, bf16[2,2,72,128]{3,2,1,0:T(8,128)(2,1)S(1)}, u32[]{:S(2)}, u32[]{:S(2)}) collective-permute-start(bf16[2,2,72,128]{3,2,1,0:T(8,128)(2,1)S(1)} %get-tuple-element.37), channel_id=1, source_target_pairs={{0,1},{1,2},{2,3},{3,4},{4,5},{5,6},{6,7},{7,8},{8,9},{9,10},{10,1... | collective-permute-start | bytes 221192 | tf_op jit(solution)/shard_map/ppermute | solution.py:321
  31.7 5.1 %collective-permute-start.7 = (bf16[2,2,72,128]{3,2,1,0:T(8,128)(2,1)S(1)}, bf16[2,2,72,128]{3,2,1,0:T(8,128)(2,1)S(1)}, u32[]{:S(2)}, u32[]{:S(2)}) collective-permute-start(bf16[2,2,72,128]{3,2,1,0:T(8,128)(2,1)S(1)} %get-tuple-element.39), channel_id=1, source_target_pairs={{1,0},{2,1},{3,2},{4,3},{5,4},{6,5},{7,6},{8,7},{9,8},{10,9},{11,1... | collective-permute-start | bytes 221192 | tf_op jit(solution)/shard_map/ppermute | solution.py:322
  47.8 21.9 %all-to-all-start = ((bf16[32,48,128]{2,1,0:T(8,128)(2,1)}), bf16[32,48,128]{2,1,0:T(8,128)(2,1)S(1)}, u32[]{:S(2)}, u32[]{:S(2)}) async-start(bf16[32,48,128]{2,1,0:T(8,128)(2,1)} %bitcast.7), calls=%async_computation | async-start | bytes 786432 | tf_op jit(solution)/shard_map/all_to_all | solution.py:389
  91.3 24.2 %all-to-all-start.2 = ((bf16[32,48,128]{2,1,0:T(8,128)(2,1)}), bf16[32,48,128]{2,1,0:T(8,128)(2,1)S(1)}, u32[]{:S(2)}, u32[]{:S(2)}) async-start(bf16[32,48,128]{2,1,0:T(8,128)(2,1)} %total.3), calls=%async_computation.2 | async-start | bytes 786432 | tf_op jit(solution)/shard_map/all_to_all | solution.py:389
  95.8 8.2 %collective-permute-start.10 = (bf16[2,4,64,128]{3,2,1,0:T(8,128)(2,1)S(1)}, bf16[2,4,64,128]{3,2,1,0:T(8,128)(2,1)S(1)}, u32[]{:S(2)}, u32[]{:S(2)}) collective-permute-start(bf16[2,4,64,128]{3,2,1,0:T(8,128)(2,1)S(1)} %get-tuple-element.48), channel_id=1, source_target_pairs={{0,128},{32,160},{64,192},{96,224},{128,0},{160,32},{192,64},{224,... | collective-permute-start | bytes 393224 | tf_op jit(solution)/shard_map/ppermute | solution.py:25
  96.8 7.2 %collective-permute-start.8 = (bf16[2,4,64,128]{3,2,1,0:T(8,128)(2,1)S(1)}, bf16[2,4,64,128]{3,2,1,0:T(8,128)(2,1)S(1)}, u32[]{:S(2)}, u32[]{:S(2)}) collective-permute-start(bf16[2,4,64,128]{3,2,1,0:T(8,128)(2,1)S(1)} %get-tuple-element.46), channel_id=1, source_target_pairs={{0,192},{32,224},{64,0},{96,32},{128,64},{160,96},{192,128},{224,1... | collective-permute-start | bytes 393224 | tf_op jit(solution)/shard_map/ppermute | solution.py:25
  100.0 11.3 %collective-permute-start.9 = (bf16[2,4,64,128]{3,2,1,0:T(8,128)(2,1)S(1)}, bf16[2,4,64,128]{3,2,1,0:T(8,128)(2,1)S(1)}, u32[]{:S(2)}, u32[]{:S(2)}) collective-permute-start(bf16[2,4,64,128]{3,2,1,0:T(8,128)(2,1)S(1)} %get-tuple-element.47), channel_id=1, source_target_pairs={{0,64},{32,96},{64,128},{96,160},{128,192},{160,224},{192,0},{224,... | collective-permute-start | bytes 393224 | tf_op jit(solution)/shard_map/ppermute | solution.py:25
  111.3 2.7 %collective-permute-start.11 = (bf16[4,4,64,128]{3,2,1,0:T(8,128)(2,1)S(1)}, bf16[4,4,64,128]{3,2,1,0:T(8,128)(2,1)S(1)}, u32[]{:S(2)}, u32[]{:S(2)}) collective-permute-start(bf16[4,4,64,128]{3,2,1,0:T(8,128)(2,1)S(1)} %other.1), channel_id=1, source_target_pairs={{0,32},{32,0},{64,96},{96,64},{128,160},{160,128},{192,224},{224,1... | collective-permute-start | bytes 786440 | tf_op jit(solution)/shard_map/ppermute | solution.py:25

commit v2 on v1

--- a/solution.py
+++ b/solution.py
@@ -6,6 +6,7 @@
 from jax import lax
 from jax.experimental import pallas as pl
 from jax.experimental.pallas import tpu as pltpu
+from jax.sharding import Mesh
 from jax.sharding import PartitionSpec as P
 
 
@@ -14,6 +15,10 @@
 WIDE = 80
 
 
+MEMBER = ("zh", "core")
+LAT = ("y", "zl", "x")
+PLANE = ("y", "x")
+REST = ("zh", "core", "zl")
 ORDER = (0, 1, 3, 2)
 
 
@@ -22,7 +27,7 @@
     pairs = [
         (2 * z + c, 2 * ((z + steps) % chips) + (c + cross) % 2) for z in range(chips) for c in range(2)
     ]
-    return lax.ppermute(value, "member", pairs)
+    return lax.ppermute(value, MEMBER, pairs)
 
 
 def column_block(device, steps, cross, groups):
@@ -112,9 +117,9 @@
 
 
 def tile_kernel(
-    lat_ref, t0, t1, t2, t3, top0, top1, bot0, bot1, w1_ref, pool_ref, _,
+    lat_ref, t0, t1, t2, t3, top_ref, bot_ref, w1_ref, pool_ref, _,
     grads_ref, hid_ref, dpre_ref,
-    own_ref, top_ref, bot_ref, pre_s, dh_s, act_s, xo_s, oc_s, hq_s, dpo_s, hid_s, dpre_s, sum_s, var_s, shared_s, ca_s, cs_s, sems,
+    own_ref, pre_s, dh_s, act_s, xo_s, oc_s, hq_s, dpo_s, hid_s, dpre_s, sum_s, var_s, shared_s, ca_s, cs_s, sems,
 ):
     srcs, rows, width, _ = own_ref.shape
     inner = rows + 2
@@ -122,11 +127,6 @@
     nlat = lat_ref[1]
     for d, tile in enumerate((t0, t1, t2, t3)):
         own_ref[2 * d : 2 * d + 2] = tile[...]
-    split = top0.shape[0]
-    top_ref[:split] = top0[...]
-    top_ref[split:] = top1[...]
-    bot_ref[:split] = bot0[...]
-    bot_ref[split:] = bot1[...]
     members = 2 * srcs
     channels = pre_s.shape[-1]
     shape = (inner, WIDE, channels)
@@ -280,15 +280,15 @@
 
 def block(ensemble, cotangent, conv_in, pool_weight, conv_out):
     mem_local, _, rows, lon = ensemble.shape
-    groups = lax.axis_size("member")
-    bands = lax.axis_size("lat")
+    groups = lax.axis_size(MEMBER)
+    bands = lax.axis_size(LAT)
     channels = conv_in.shape[-1]
     cols = lon // groups
     width = (cols + 4) * mem_local
     vspec = pl.BlockSpec(memory_space=pltpu.VMEM)
     sspec = pl.BlockSpec(memory_space=pltpu.SMEM)
     vm = pltpu.VMEM
-    me = lax.axis_index("member").astype(jnp.int32).reshape(1)
+    me = lax.axis_index(MEMBER).astype(jnp.int32).reshape(1)
     chips = groups // 2
     keep, give = pl.pallas_call(
         pack_kernel,
@@ -307,25 +307,15 @@
         name="pair",
     )(*near(keep, got))
     tiles = [tiles[0]] + [swap(tiles[i], ORDER[i], 0, groups) for i in range(1, chips)]
-
-    def edges(*sources):
-        return pl.pallas_call(
-            edges_kernel,
-            out_shape=[vm((2 * len(sources), 2, width, 128), BF)] * 2,
-            in_specs=[vspec] * len(sources),
-            out_specs=[vspec] * 2,
-            name="edges",
-        )(*near(*sources))
-
-    def to_bands(head, tail):
-        top = lax.ppermute(tail, "lat", [(i, i + 1) for i in range(bands - 1)])
-        bot = lax.ppermute(head, "lat", [(i + 1, i) for i in range(bands - 1)])
-        return top, bot
-
-    first_edges = edges(*tiles[:3])
-    top0, bot0 = to_bands(*first_edges)
-    last_edges = edges(*tiles[3:])
-    top1, bot1 = to_bands(*last_edges)
+    head, tail = pl.pallas_call(
+        edges_kernel,
+        out_shape=[vm((groups, 2, width, 128), BF)] * 2,
+        in_specs=[vspec] * chips,
+        out_specs=[vspec] * 2,
+        name="edges",
+    )(*near(*tiles))
+    top = lax.ppermute(tail, LAT, [(i, i + 1) for i in range(bands - 1)])
+    bot = lax.ppermute(head, LAT, [(i + 1, i) for i in range(bands - 1)])
 
     flip_in = jnp.transpose(conv_in[::-1, ::-1], (0, 1, 3, 2))
     flip_out = jnp.transpose(conv_out[::-1, ::-1], (0, 1, 3, 2))
@@ -341,23 +331,22 @@
         ],
         axis=1,
     )
-    lat = jnp.stack([lax.axis_index("lat"), jnp.int32(bands * rows)]).astype(jnp.int32)
+    lat = jnp.stack([lax.axis_index(LAT), jnp.int32(bands * rows)]).astype(jnp.int32)
     inner = rows + 2
     plane = (inner, WIDE, channels)
     used = 18 * (channels // 2) + 2 * channels
-    per = -(-used // (8 * bands)) * 8
+    slices, copies = lax.axis_size(PLANE), lax.axis_size(REST)
+    per = -(-used // (8 * slices)) * 8
     shifted = (groups, inner, cols * mem_local, 384)
     compact = pltpu.HBM((groups, inner, width, channels), BF)
     hspec = pl.BlockSpec(memory_space=pltpu.HBM)
     grads, hid, dpre = pl.pallas_call(
         tile_kernel,
-        out_shape=[vm((bands * per, channels), BF), compact, compact],
-        in_specs=[sspec] + [vspec] * (chips + 6) + [hspec],
+        out_shape=[vm((slices * per, channels), BF), compact, compact],
+        in_specs=[sspec] + [vspec] * (chips + 4) + [hspec],
         out_specs=[vspec, hspec, hspec],
         scratch_shapes=[
             vm((groups, rows, width, 128), BF),
-            vm((groups, 2, width, 128), BF),
-            vm((groups, 2, width, 128), BF),
             vm((groups,) + plane, F32),
             vm((groups,) + plane, F32),
             vm((groups,) + plane, F32),
@@ -376,7 +365,7 @@
         ],
         compiler_params=pltpu.CompilerParams(vmem_limit_bytes=48 * 1024 * 1024),
         name="tile",
-    )(lat, *near(*tiles, top0, top1, bot0, bot1, w1, pool_weight), w2)
+    )(lat, *near(*tiles, top, bot, w1, pool_weight), w2)
     pieces = list(pl.pallas_call(
         output_kernel,
         out_shape=[vm((2, rows, cols * mem_local, 128), BF)] * chips,
@@ -388,23 +377,23 @@
     def exchange(value, axis):
         return lax.all_to_all(value, axis, split_axis=0, concat_axis=0, tiled=True)
 
-    def add_up(parts, copies, dtype):
+    def add_up(parts, count):
         return pl.pallas_call(
             sum_kernel,
-            out_shape=vm((copies,) + parts.shape[1:], dtype),
+            out_shape=vm((count,) + parts.shape[1:], BF),
             in_specs=[vspec],
             out_specs=vspec,
             name="total",
         )(*near(parts))
 
-    parts = exchange(grads.reshape(bands, per, channels), "lat")
+    parts = exchange(grads.reshape(slices, per, channels), PLANE)
     far = swap(pieces[3], chips - ORDER[3], 0, groups)
     parts, pieces[1], pieces[2] = lax.optimization_barrier((parts, pieces[1], pieces[2]))
     pieces[1:3] = [swap(piece, chips - d, 0, groups) for d, piece in zip(ORDER[1:3], pieces[1:3])]
     pieces[3] = far
-    parts = add_up(parts, groups, F32)
-    parts = exchange(parts, "member")
-    parts = add_up(parts, bands, BF)
+    parts = add_up(parts, copies)
+    parts = exchange(parts, REST)
+    parts = add_up(parts, slices)
     other = pl.pallas_call(
         other_kernel,
         out_shape=vm((chips, rows, cols * mem_local, 128), BF),
@@ -413,7 +402,7 @@
         name="other",
     )(*near(*pieces))
     theirs = swap(other, 0, 1, groups)
-    full = exchange(parts, "lat").reshape(bands * per, channels)
+    full = exchange(parts, PLANE).reshape(slices * per, channels)
     members = mem_local * groups
     scale = 1.0 / math.sqrt(members * bands * rows * lon)
     half = channels // 2
@@ -439,10 +428,14 @@
 
 
 def solution(mesh):
+    groups, bands = mesh.devices.shape
+    lat = (4, 2, 4) if bands == 32 else (1, bands, 1)
+    fine = Mesh(mesh.devices.reshape((groups // 2, 2) + lat), MEMBER + LAT)
+    fields = P(MEMBER, None, LAT, None)
     return jax.shard_map(
         block,
-        mesh=mesh,
-        in_specs=(P("member", None, "lat", None), P("member", None, "lat", None), P(), P(), P()),
-        out_specs=(P("member", None, "lat", None), P("member", None, "lat", None), P(), P(), P()),
+        mesh=fine,
+        in_specs=(fields, fields, P(), P(), P()),
+        out_specs=(fields, fields, P(), P(), P()),
         check_vma=False,
     )

time: 117 us -> 105 us (0.90)
  blocking collectives: 20.7 us -> 0 us
  waiting for transfers between devices: 25.8 us -> 31.9 us
  starting transfers between devices: 45.5 us -> 48.9 us
    all_to_all x1 -> x0, blocking collectives: 20.7 us -> none  [exchange(): return lax.all_to_all(value, axis, split_axis=0, concat_axis=0, tiled=True)]
    all_to_all x2 -> x3, waiting for transfers between devices: 3.09 us -> 11.4 us  [exchange(): return lax.all_to_all(value, axis, split_axis=0, concat_axis=0, tiled=True)]
    all_to_all x2 -> x3, starting transfers between devices: 17.8 us -> 23.6 us  [exchange(): return lax.all_to_all(value, axis, split_axis=0, concat_axis=0, tiled=True)]
    ppermute x12 -> x10, starting transfers between devices: 27.7 us -> 25.3 us  [the longest x8 20.9 us: swap(): return lax.ppermute(value, MEMBER, pairs)]
    ppermute x12 -> x10, waiting for transfers between devices: 22.7 us -> 20.5 us  [the longest x8 14.5 us: swap(): return lax.ppermute(value, MEMBER, pairs)]
    pallas_call x5 -> x4, Pallas kernels: 11.8 us -> 12.6 us  [the longest x1 10.9 us: block(): pl.pallas_call(tile_kernel, out_shape=[vm((slices * per, channels), BF),...]
  transfers between devices with their start and end apart: 14 -> 13, of which waited for: 7 -> 10; matrix products, arithmetic and copies ran while one was open for 2% -> 1% of each run, Pallas kernels for 6% -> 7%
where the time goes in v2:
time: 105 us
  starting transfers between devices  48.9 us (47%)
  waiting for transfers between devices  31.9 us (30%)
  Pallas kernels  22.4 us (21%)
    all_to_all x3, starting transfers between devices, exchange(): return lax.all_to_all(value, axis, split_axis=0, concat_axis=0, tiled=True)  23.6 us
    ppermute x8, starting transfers between devices, swap(): return lax.ppermute(value, MEMBER, pairs)  20.9 us
    ppermute x8, waiting for transfers between devices, swap(): return lax.ppermute(value, MEMBER, pairs)  14.5 us
    all_to_all x3, waiting for transfers between devices, exchange(): return lax.all_to_all(value, axis, split_axis=0, concat_axis=0, tiled=True)  11.4 us
    pallas_call x1, Pallas kernels, block(): pl.pallas_call(tile_kernel, out_shape=[vm((slices * per, channels), BF),...  10.9 us
    pallas_call x1, Pallas kernels, block(): pl.pallas_call(output_kernel, out_shape=[vm((2, rows, cols * mem_local, 1...  5.36 us
    ppermute x1, waiting for transfers between devices, block(): bot = lax.ppermute(head, LAT, [(i + 1, i) for i in range(bands - 1)])  3.85 us
    ppermute x1, starting transfers between devices, block(): top = lax.ppermute(tail, LAT, [(i, i + 1) for i in range(bands - 1)])  3.13 us
  transfers between devices with their start and end apart: 13, of which 10 were waited for; matrix products, arithmetic and copies ran while one was open for 1% of the time, Pallas kernels for 7%

profile of v2, /device:TPU:1, one launch (start us, length us, event | category | flops | bytes accessed | tf_op | source)
XLA Modules:
  0.0 105.0 jit_solution(15863859882672246699)
XLA Ops:
  0.7 2.0 %pack.1 = (bf16[4,4,72,128]{3,2,1,0:T(8,128)(2,1)S(1)}, bf16[4,4,72,128]{3,2,1,0:T(8,128)(2,1)S(1)}) custom-call(s32[1]{0:T(128)} %bitcast.me_ref, bf16[2,64,4,256]{3,2,1,0:T(4,128)(2,1)} %ens_ref.1, bf16[2,64,4,256]{3,2,1,0:T(4,128)(2,1)} %cot_ref.1), custom_call_target="tpu_custom_call" | custom-call | tf_op jit(solution)/shard_map/pack/pallas_call | solution.py:293
  2.7 3.3 %collective-permute-start = (bf16[4,4,72,128]{3,2,1,0:T(8,128)(2,1)S(1)}, bf16[4,4,72,128]{3,2,1,0:T(8,128)(2,1)S(1)}, u32[]{:S(2)}, u32[]{:S(2)}) collective-permute-start(bf16[4,4,72,128]{3,2,1,0:T(8,128)(2,1)S(1)} %get-tuple-element.29), channel_id=1, source_target_pairs={{0,32},{32,0},{64,96},{96,64},{128,160},{160,128},{192,224},{224,1... | collective-permute-start | bytes 884744 | tf_op jit(solution)/shard_map/ppermute | solution.py:30
  6.0 1.2 %collective-permute-done.got_ref = bf16[4,4,72,128]{3,2,1,0:T(8,128)(2,1)S(1)} collective-permute-done((bf16[4,4,72,128]{3,2,1,0:T(8,128)(2,1)S(1)}, bf16[4,4,72,128]{3,2,1,0:T(8,128)(2,1)S(1)}, u32[]{:S(2)}, u32[]{:S(2)}) %collective-permute-start) | collective-permute-done | bytes 294944 | tf_op jit(solution)/shard_map/ppermute | solution.py:30
  7.2 1.4 %collective-permute-start.1 = (bf16[2,4,72,128]{3,2,1,0:T(8,128)(2,1)S(1)}, bf16[2,4,72,128]{3,2,1,0:T(8,128)(2,1)S(1)}, u32[]{:S(2)}, u32[]{:S(2)}) collective-permute-start(bf16[2,4,72,128]{3,2,1,0:T(8,128)(2,1)S(1)} %get-tuple-element.31), channel_id=1, source_target_pairs={{0,64},{32,96},{64,128},{96,160},{128,192},{160,224},{192,0},{224,... | collective-permute-start | bytes 442376 | tf_op jit(solution)/shard_map/ppermute | solution.py:30
  8.6 3.1 %collective-permute-start.2 = (bf16[2,4,72,128]{3,2,1,0:T(8,128)(2,1)S(1)}, bf16[2,4,72,128]{3,2,1,0:T(8,128)(2,1)S(1)}, u32[]{:S(2)}, u32[]{:S(2)}) collective-permute-start(bf16[2,4,72,128]{3,2,1,0:T(8,128)(2,1)S(1)} %get-tuple-element.32), channel_id=1, source_target_pairs={{0,192},{32,224},{64,0},{96,32},{128,64},{160,96},{192,128},{224,1... | collective-permute-start | bytes 442376 | tf_op jit(solution)/shard_map/ppermute | solution.py:30
  11.7 4.4 %collective-permute-start.3 = (bf16[2,4,72,128]{3,2,1,0:T(8,128)(2,1)S(1)}, bf16[2,4,72,128]{3,2,1,0:T(8,128)(2,1)S(1)}, u32[]{:S(2)}, u32[]{:S(2)}) collective-permute-start(bf16[2,4,72,128]{3,2,1,0:T(8,128)(2,1)S(1)} %get-tuple-element.33), channel_id=1, source_target_pairs={{0,128},{32,160},{64,192},{96,224},{128,0},{160,32},{192,64},{224,... | collective-permute-start | bytes 442376 | tf_op jit(solution)/shard_map/ppermute | solution.py:30
  16.1 7.0 %collective-permute-done.2.refs_2_.t2 = bf16[2,4,72,128]{3,2,1,0:T(8,128)(2,1)S(1)} collective-permute-done((bf16[2,4,72,128]{3,2,1,0:T(8,128)(2,1)S(1)}, bf16[2,4,72,128]{3,2,1,0:T(8,128)(2,1)S(1)}, u32[]{:S(2)}, u32[]{:S(2)}) %collective-permute-start.2) | collective-permute-done | bytes 147488 | tf_op jit(solution)/shard_map/ppermute | solution.py:30
  23.2 1.7 %collective-permute-done.3.refs_3_.t3 = bf16[2,4,72,128]{3,2,1,0:T(8,128)(2,1)S(1)} collective-permute-done((bf16[2,4,72,128]{3,2,1,0:T(8,128)(2,1)S(1)}, bf16[2,4,72,128]{3,2,1,0:T(8,128)(2,1)S(1)}, u32[]{:S(2)}, u32[]{:S(2)}) %collective-permute-start.3) | collective-permute-done | bytes 147488 | tf_op jit(solution)/shard_map/ppermute | solution.py:30
  24.9 3.1 %collective-permute-start.4 = (bf16[8,2,72,128]{3,2,1,0:T(8,128)(2,1)S(1)}, bf16[8,2,72,128]{3,2,1,0:T(8,128)(2,1)S(1)}, u32[]{:S(2)}, u32[]{:S(2)}) collective-permute-start(bf16[8,2,72,128]{3,2,1,0:T(8,128)(2,1)S(1)} %get-tuple-element.34), channel_id=1, source_target_pairs={{0,1},{1,2},{2,3},{3,4},{4,5},{5,6},{6,7},{7,8},{8,9},{9,10},{10,1... | collective-permute-start | bytes 884744 | tf_op jit(solution)/shard_map/ppermute | solution.py:317
  28.1 1.3 %collective-permute-start.5 = (bf16[8,2,72,128]{3,2,1,0:T(8,128)(2,1)S(1)}, bf16[8,2,72,128]{3,2,1,0:T(8,128)(2,1)S(1)}, u32[]{:S(2)}, u32[]{:S(2)}) collective-permute-start(bf16[8,2,72,128]{3,2,1,0:T(8,128)(2,1)S(1)} %get-tuple-element.35), channel_id=1, source_target_pairs={{1,0},{2,1},{3,2},{4,3},{5,4},{6,5},{7,6},{8,7},{9,8},{10,9},{11,1... | collective-permute-start | bytes 884744 | tf_op jit(solution)/shard_map/ppermute | solution.py:318
  29.4 0.2 copy.12
  29.7 0.2 copy.13
  30.3 2.2 %collective-permute-done.4.top_ref = bf16[8,2,72,128]{3,2,1,0:T(8,128)(2,1)S(1)} collective-permute-done((bf16[8,2,72,128]{3,2,1,0:T(8,128)(2,1)S(1)}, bf16[8,2,72,128]{3,2,1,0:T(8,128)(2,1)S(1)}, u32[]{:S(2)}, u32[]{:S(2)}) %collective-permute-start.4) | collective-permute-done | bytes 294944 | tf_op jit(solution)/shard_map/ppermute | solution.py:317
  32.5 3.8 %collective-permute-done.5.bot_ref = bf16[8,2,72,128]{3,2,1,0:T(8,128)(2,1)S(1)} collective-permute-done((bf16[8,2,72,128]{3,2,1,0:T(8,128)(2,1)S(1)}, bf16[8,2,72,128]{3,2,1,0:T(8,128)(2,1)S(1)}, u32[]{:S(2)}, u32[]{:S(2)}) %collective-permute-start.5) | collective-permute-done | bytes 294944 | tf_op jit(solution)/shard_map/ppermute | solution.py:318
  36.3 10.9 %tile.1 = (bf16[1408,128]{1,0:T(8,128)(2,1)}, bf16[8,6,72,128]{3,2,1,0:T(8,128)(2,1)}, bf16[8,6,72,128]{3,2,1,0:T(8,128)(2,1)}) custom-call(s32[2]{0:T(128)S(1)} %pad_add_fusion.lat_ref, bf16[2,4,72,128]{3,2,1,0:T(8,128)(2,1)S(1)} %get-tuple-element.30.refs_0_.t0, bf16[2,4,72,128]{3,2,1,0:T(8,128)(2,1)S(1)} %collective-permute-done.1.refs_1_.t1, ...), custom_call_target="tpu_custom_call" | custom-call | tf_op jit(solution)/shard_map/tile/pallas_call | solution.py:343
  47.3 13.0 %all-to-all-start = ((bf16[16,88,128]{2,1,0:T(8,128)(2,1)}), bf16[16,88,128]{2,1,0:T(8,128)(2,1)S(1)}, u32[]{:S(2)}, u32[]{:S(2)}) async-start(bf16[16,88,128]{2,1,0:T(8,128)(2,1)} %bitcast.7), calls=%async_computation | async-start | bytes 720896 | tf_op jit(solution)/shard_map/all_to_all | solution.py:378
  60.3 5.4 %output.1 = (bf16[2,4,64,128]{3,2,1,0:T(8,128)(2,1)S(1)}, bf16[2,4,64,128]{3,2,1,0:T(8,128)(2,1)S(1)}, bf16[2,4,64,128]{3,2,1,0:T(8,128)(2,1)S(1)}, bf16[2,4,64,128]{3,2,1,0:T(8,128)(2,1)S(1)}) custom-call(bf16[2,4,72,128]{3,2,1,0:T(8,128)(2,1)S(1)} %get-tuple-element.30.refs_0_.t0, bf16[2,4,72,128]{3,2,1,0:T(8,128)(2,1)S(1)} %collective-permute-done.1.refs_1_.t1, ...), custom_call_target="tpu_custom_call" | custom-call | tf_op jit(solution)/shard_map/output/pallas_call | solution.py:369
  65.6 2.7 %all-to-all-done.parts_ref = bf16[16,88,128]{2,1,0:T(8,128)(2,1)S(1)} async-done(((bf16[16,88,128]{2,1,0:T(8,128)(2,1)}), bf16[16,88,128]{2,1,0:T(8,128)(2,1)S(1)}, u32[]{:S(2)}, u32[]{:S(2)}) %all-to-all-start) | async-done | bytes 360480 | tf_op jit(solution)/shard_map/all_to_all | solution.py:378
  68.3 0.8 total.2
  69.1 7.1 %all-to-all-start.1 = ((bf16[16,88,128]{2,1,0:T(8,128)(2,1)}), bf16[16,88,128]{2,1,0:T(8,128)(2,1)S(1)}, u32[]{:S(2)}, u32[]{:S(2)}) async-start(bf16[16,88,128]{2,1,0:T(8,128)(2,1)} %total.2), calls=%async_computation.1 | async-start | bytes 720896 | tf_op jit(solution)/shard_map/all_to_all | solution.py:378
  76.2 5.3 %collective-permute-start.8 = (bf16[2,4,64,128]{3,2,1,0:T(8,128)(2,1)S(1)}, bf16[2,4,64,128]{3,2,1,0:T(8,128)(2,1)S(1)}, u32[]{:S(2)}, u32[]{:S(2)}) collective-permute-start(bf16[2,4,64,128]{3,2,1,0:T(8,128)(2,1)S(1)} %get-tuple-element.44), channel_id=1, source_target_pairs={{0,128},{32,160},{64,192},{96,224},{128,0},{160,32},{192,64},{224,... | collective-permute-start | bytes 393224 | tf_op jit(solution)/shard_map/ppermute | solution.py:30
  81.4 0.3 collective-permute-start.6
  81.7 2.1 %collective-permute-start.7 = (bf16[2,4,64,128]{3,2,1,0:T(8,128)(2,1)S(1)}, bf16[2,4,64,128]{3,2,1,0:T(8,128)(2,1)S(1)}, u32[]{:S(2)}, u32[]{:S(2)}) collective-permute-start(bf16[2,4,64,128]{3,2,1,0:T(8,128)(2,1)S(1)} %get-tuple-element.43), channel_id=1, source_target_pairs={{0,64},{32,96},{64,128},{96,160},{128,192},{160,224},{192,0},{224,... | collective-permute-start | bytes 393224 | tf_op jit(solution)/shard_map/ppermute | solution.py:30
  83.8 7.9 %all-to-all-done.1.parts_ref = bf16[16,88,128]{2,1,0:T(8,128)(2,1)S(1)} async-done(((bf16[16,88,128]{2,1,0:T(8,128)(2,1)}), bf16[16,88,128]{2,1,0:T(8,128)(2,1)S(1)}, u32[]{:S(2)}, u32[]{:S(2)}) %all-to-all-start.1) | async-done | bytes 360480 | tf_op jit(solution)/shard_map/all_to_all | solution.py:378
  91.7 0.8 total.3
  92.5 3.5 %all-to-all-start.2 = ((bf16[16,88,128]{2,1,0:T(8,128)(2,1)}), bf16[16,88,128]{2,1,0:T(8,128)(2,1)S(1)}, u32[]{:S(2)}, u32[]{:S(2)}) async-start(bf16[16,88,128]{2,1,0:T(8,128)(2,1)} %total.3), calls=%async_computation.2 | async-start | bytes 720896 | tf_op jit(solution)/shard_map/all_to_all | solution.py:378
  96.1 3.4 %collective-permute-done.7.refs_2_ = bf16[2,4,64,128]{3,2,1,0:T(8,128)(2,1)S(1)} collective-permute-done((bf16[2,4,64,128]{3,2,1,0:T(8,128)(2,1)S(1)}, bf16[2,4,64,128]{3,2,1,0:T(8,128)(2,1)S(1)}, u32[]{:S(2)}, u32[]{:S(2)}) %collective-permute-start.7) | collective-permute-done | bytes 131104 | tf_op jit(solution)/shard_map/ppermute | solution.py:30
  99.4 1.1 %collective-permute-start.9 = (bf16[4,4,64,128]{3,2,1,0:T(8,128)(2,1)S(1)}, bf16[4,4,64,128]{3,2,1,0:T(8,128)(2,1)S(1)}, u32[]{:S(2)}, u32[]{:S(2)}) collective-permute-start(bf16[4,4,64,128]{3,2,1,0:T(8,128)(2,1)S(1)} %other.1), channel_id=1, source_target_pairs={{0,32},{32,0},{64,96},{96,64},{128,160},{160,128},{192,224},{224,1... | collective-permute-start | bytes 786440 | tf_op jit(solution)/shard_map/ppermute | solution.py:30
  100.5 1.2 %collective-permute-done.9.refs_4_ = bf16[4,4,64,128]{3,2,1,0:T(8,128)(2,1)S(1)} collective-permute-done((bf16[4,4,64,128]{3,2,1,0:T(8,128)(2,1)S(1)}, bf16[4,4,64,128]{3,2,1,0:T(8,128)(2,1)S(1)}, u32[]{:S(2)}, u32[]{:S(2)}) %collective-permute-start.9) | collective-permute-done | bytes 262176 | tf_op jit(solution)/shard_map/ppermute | solution.py:30
  101.7 1.5 %unpack.1 = (bf16[2,64,4,256]{3,2,1,0:T(4,128)(2,1)}, bf16[2,64,4,256]{3,2,1,0:T(4,128)(2,1)}) custom-call(s32[1]{0:T(128)} %bitcast.me_ref, bf16[2,4,64,128]{3,2,1,0:T(8,128)(2,1)S(1)} %get-tuple-element.38.refs_0_, bf16[2,4,64,128]{3,2,1,0:T(8,128)(2,1)S(1)} %collective-permute-done.6.refs_1_, bf16[2,4,64,128]{3,2,1,0:T(8,128)(2,1)S(1)} %collective-permute-done.7.refs_2_, ...), custom_call_target="tpu_custom_call" | custom-call | tf_op jit(solution)/shard_map/unpack/pallas_call | solution.py:419
  103.2 0.8 all-to-all-done.2
  104.1 0.9 finish.1
  (21 shorter events, 0.5 us)
Async XLA Ops:
  0.6 15.5 %copy-start.3 = (bf16[3,3,64,128]{3,2,1,0:T(8,128)(2,1)S(1)}, bf16[3,3,64,128]{3,2,1,0:T(8,128)(2,1)}, u32[]{:S(2)}) copy-start(bf16[3,3,64,128]{3,2,1,0:T(8,128)(2,1)} %param.7) | copy-start | bytes 442372
  0.6 15.5 %copy-start.2 = (bf16[3,3,128,64]{2,3,1,0:T(8,128)(2,1)S(1)}, bf16[3,3,128,64]{2,3,1,0:T(8,128)(2,1)}, u32[]{:S(2)}) copy-start(bf16[3,3,128,64]{2,3,1,0:T(8,128)(2,1)} %param.9) | copy-start | bytes 442372
  2.7 4.5 %collective-permute-start = (bf16[4,4,72,128]{3,2,1,0:T(8,128)(2,1)S(1)}, bf16[4,4,72,128]{3,2,1,0:T(8,128)(2,1)S(1)}, u32[]{:S(2)}, u32[]{:S(2)}) collective-permute-start(bf16[4,4,72,128]{3,2,1,0:T(8,128)(2,1)S(1)} %get-tuple-element.29), channel_id=1, source_target_pairs={{0,32},{32,0},{64,96},{96,64},{128,160},{160,128},{192,224},{224,1... | collective-permute-start | bytes 884744 | tf_op jit(solution)/shard_map/ppermute | solution.py:30
  7.2 8.9 %collective-permute-start.1 = (bf16[2,4,72,128]{3,2,1,0:T(8,128)(2,1)S(1)}, bf16[2,4,72,128]{3,2,1,0:T(8,128)(2,1)S(1)}, u32[]{:S(2)}, u32[]{:S(2)}) collective-permute-start(bf16[2,4,72,128]{3,2,1,0:T(8,128)(2,1)S(1)} %get-tuple-element.31), channel_id=1, source_target_pairs={{0,64},{32,96},{64,128},{96,160},{128,192},{160,224},{192,0},{224,... | collective-permute-start | bytes 442376 | tf_op jit(solution)/shard_map/ppermute | solution.py:30
  8.6 14.6 %collective-permute-start.2 = (bf16[2,4,72,128]{3,2,1,0:T(8,128)(2,1)S(1)}, bf16[2,4,72,128]{3,2,1,0:T(8,128)(2,1)S(1)}, u32[]{:S(2)}, u32[]{:S(2)}) collective-permute-start(bf16[2,4,72,128]{3,2,1,0:T(8,128)(2,1)S(1)} %get-tuple-element.32), channel_id=1, source_target_pairs={{0,192},{32,224},{64,0},{96,32},{128,64},{160,96},{192,128},{224,1... | collective-permute-start | bytes 442376 | tf_op jit(solution)/shard_map/ppermute | solution.py:30
  11.7 13.2 %collective-permute-start.3 = (bf16[2,4,72,128]{3,2,1,0:T(8,128)(2,1)S(1)}, bf16[2,4,72,128]{3,2,1,0:T(8,128)(2,1)S(1)}, u32[]{:S(2)}, u32[]{:S(2)}) collective-permute-start(bf16[2,4,72,128]{3,2,1,0:T(8,128)(2,1)S(1)} %get-tuple-element.33), channel_id=1, source_target_pairs={{0,128},{32,160},{64,192},{96,224},{128,0},{160,32},{192,64},{224,... | collective-permute-start | bytes 442376 | tf_op jit(solution)/shard_map/ppermute | solution.py:30
  24.9 7.6 %collective-permute-start.4 = (bf16[8,2,72,128]{3,2,1,0:T(8,128)(2,1)S(1)}, bf16[8,2,72,128]{3,2,1,0:T(8,128)(2,1)S(1)}, u32[]{:S(2)}, u32[]{:S(2)}) collective-permute-start(bf16[8,2,72,128]{3,2,1,0:T(8,128)(2,1)S(1)} %get-tuple-element.34), channel_id=1, source_target_pairs={{0,1},{1,2},{2,3},{3,4},{4,5},{5,6},{6,7},{7,8},{8,9},{9,10},{10,1... | collective-permute-start | bytes 884744 | tf_op jit(solution)/shard_map/ppermute | solution.py:317
  28.1 8.3 %collective-permute-start.5 = (bf16[8,2,72,128]{3,2,1,0:T(8,128)(2,1)S(1)}, bf16[8,2,72,128]{3,2,1,0:T(8,128)(2,1)S(1)}, u32[]{:S(2)}, u32[]{:S(2)}) collective-permute-start(bf16[8,2,72,128]{3,2,1,0:T(8,128)(2,1)S(1)} %get-tuple-element.35), channel_id=1, source_target_pairs={{1,0},{2,1},{3,2},{4,3},{5,4},{6,5},{7,6},{8,7},{9,8},{10,9},{11,1... | collective-permute-start | bytes 884744 | tf_op jit(solution)/shard_map/ppermute | solution.py:318
  30.2 6.2 %copy-start.1 = (bf16[256,128]{1,0:T(8,128)(2,1)S(1)}, bf16[256,128]{1,0:T(8,128)(2,1)}, u32[]{:S(2)}) copy-start(bf16[256,128]{1,0:T(8,128)(2,1)} %pool_ref.1) | copy-start | bytes 196612
  30.3 17.0 %copy-start = (bf16[3,768,128]{2,1,0:T(8,128)(2,1)}, bf16[3,768,128]{2,1,0:T(8,128)(2,1)S(1)}, u32[]{:S(2)}) copy-start(bf16[3,768,128]{2,1,0:T(8,128)(2,1)S(1)} %pad_maximum_fusion._.w2_ref) | copy-start | bytes 1769476
  47.3 21.0 %all-to-all-start = ((bf16[16,88,128]{2,1,0:T(8,128)(2,1)}), bf16[16,88,128]{2,1,0:T(8,128)(2,1)S(1)}, u32[]{:S(2)}, u32[]{:S(2)}) async-start(bf16[16,88,128]{2,1,0:T(8,128)(2,1)} %bitcast.7), calls=%async_computation | async-start | bytes 720896 | tf_op jit(solution)/shard_map/all_to_all | solution.py:378
  69.1 22.6 %all-to-all-start.1 = ((bf16[16,88,128]{2,1,0:T(8,128)(2,1)}), bf16[16,88,128]{2,1,0:T(8,128)(2,1)S(1)}, u32[]{:S(2)}, u32[]{:S(2)}) async-start(bf16[16,88,128]{2,1,0:T(8,128)(2,1)} %total.2), calls=%async_computation.1 | async-start | bytes 720896 | tf_op jit(solution)/shard_map/all_to_all | solution.py:378
  76.2 19.9 %collective-permute-start.8 = (bf16[2,4,64,128]{3,2,1,0:T(8,128)(2,1)S(1)}, bf16[2,4,64,128]{3,2,1,0:T(8,128)(2,1)S(1)}, u32[]{:S(2)}, u32[]{:S(2)}) collective-permute-start(bf16[2,4,64,128]{3,2,1,0:T(8,128)(2,1)S(1)} %get-tuple-element.44), channel_id=1, source_target_pairs={{0,128},{32,160},{64,192},{96,224},{128,0},{160,32},{192,64},{224,... | collective-permute-start | bytes 393224 | tf_op jit(solution)/shard_map/ppermute | solution.py:30
  81.4 14.6 %collective-permute-start.6 = (bf16[2,4,64,128]{3,2,1,0:T(8,128)(2,1)S(1)}, bf16[2,4,64,128]{3,2,1,0:T(8,128)(2,1)S(1)}, u32[]{:S(2)}, u32[]{:S(2)}) collective-permute-start(bf16[2,4,64,128]{3,2,1,0:T(8,128)(2,1)S(1)} %get-tuple-element.42), channel_id=1, source_target_pairs={{0,192},{32,224},{64,0},{96,32},{128,64},{160,96},{192,128},{224,1... | collective-permute-start | bytes 393224 | tf_op jit(solution)/shard_map/ppermute | solution.py:30
  81.7 17.7 %collective-permute-start.7 = (bf16[2,4,64,128]{3,2,1,0:T(8,128)(2,1)S(1)}, bf16[2,4,64,128]{3,2,1,0:T(8,128)(2,1)S(1)}, u32[]{:S(2)}, u32[]{:S(2)}) collective-permute-start(bf16[2,4,64,128]{3,2,1,0:T(8,128)(2,1)S(1)} %get-tuple-element.43), channel_id=1, source_target_pairs={{0,64},{32,96},{64,128},{96,160},{128,192},{160,224},{192,0},{224,... | collective-permute-start | bytes 393224 | tf_op jit(solution)/shard_map/ppermute | solution.py:30
  92.5 11.6 %all-to-all-start.2 = ((bf16[16,88,128]{2,1,0:T(8,128)(2,1)}), bf16[16,88,128]{2,1,0:T(8,128)(2,1)S(1)}, u32[]{:S(2)}, u32[]{:S(2)}) async-start(bf16[16,88,128]{2,1,0:T(8,128)(2,1)} %total.3), calls=%async_computation.2 | async-start | bytes 720896 | tf_op jit(solution)/shard_map/all_to_all | solution.py:378
  99.4 2.3 %collective-permute-start.9 = (bf16[4,4,64,128]{3,2,1,0:T(8,128)(2,1)S(1)}, bf16[4,4,64,128]{3,2,1,0:T(8,128)(2,1)S(1)}, u32[]{:S(2)}, u32[]{:S(2)}) collective-permute-start(bf16[4,4,64,128]{3,2,1,0:T(8,128)(2,1)S(1)} %other.1), channel_id=1, source_target_pairs={{0,32},{32,0},{64,96},{96,64},{128,160},{160,128},{192,224},{224,1... | collective-permute-start | bytes 786440 | tf_op jit(solution)/shard_map/ppermute | solution.py:30

commit v3 on v2

--- a/solution.py
+++ b/solution.py
@@ -80,22 +80,28 @@
 
 
 def pair_kernel(keep_ref, got_ref, *out_refs):
-    for d, ref in enumerate(out_refs):
+    last = keep_ref.shape[0] - 1
+    for d, ref in enumerate(out_refs[:last]):
         ref[0] = keep_ref[d]
         ref[1] = got_ref[d]
+    out_refs[last][0] = keep_ref[last]
+    out_refs[last + 1][0] = got_ref[last]
 
 
 def edges_kernel(*refs):
     tiles, (head_ref, tail_ref) = refs[:-2], refs[-2:]
     rows = tiles[0].shape[1]
-    for d, tile in enumerate(tiles):
-        head_ref[2 * d : 2 * d + 2] = tile[:, :2]
-        tail_ref[2 * d : 2 * d + 2] = tile[:, rows - 2 :]
+    at = 0
+    for tile in tiles:
+        n = tile.shape[0]
+        head_ref[at : at + n] = tile[:, :2]
+        tail_ref[at : at + n] = tile[:, rows - 2 :]
+        at += n
 
 
 def other_kernel(*refs):
     for d, tile in enumerate(refs[:-1]):
-        refs[-1][d] = tile[1]
+        refs[-1][d] = tile[tile.shape[0] - 1]
 
 
 def unpack_kernel(me_ref, *refs):
@@ -117,7 +123,7 @@
 
 
 def tile_kernel(
-    lat_ref, t0, t1, t2, t3, top_ref, bot_ref, w1_ref, pool_ref, _,
+    lat_ref, t0, t1, t2, t3, t4, top_ref, bot_ref, w1_ref, pool_ref, _,
     grads_ref, hid_ref, dpre_ref,
     own_ref, pre_s, dh_s, act_s, xo_s, oc_s, hq_s, dpo_s, hid_s, dpre_s, sum_s, var_s, shared_s, ca_s, cs_s, sems,
 ):
@@ -125,8 +131,10 @@
     inner = rows + 2
     cols = xo_s.shape[2]
     nlat = lat_ref[1]
-    for d, tile in enumerate((t0, t1, t2, t3)):
-        own_ref[2 * d : 2 * d + 2] = tile[...]
+    at = 0
+    for tile in (t0, t1, t2, t3, t4):
+        own_ref[at : at + tile.shape[0]] = tile[...]
+        at += tile.shape[0]
     members = 2 * srcs
     channels = pre_s.shape[-1]
     shape = (inner, WIDE, channels)
@@ -241,7 +249,7 @@
     dpre_copy.wait()
 
 
-def output_kernel(t0, t1, t2, t3, hid_ref, dpre_ref, w2_ref, *out_refs):
+def output_kernel(t0, t1, t2, t3, t4, hid_ref, dpre_ref, w2_ref, *out_refs):
     _, inner, width, _ = hid_ref.shape
     rows = inner - 2
     cols = out_refs[0].shape[2]
@@ -250,19 +258,20 @@
         v = ref[s].astype(F32)
         return [(pltpu.roll(v, width - 2 * q, 1) if q else v)[:, :cols] for q in range(3)]
 
-    for d, (tile, out_ref) in enumerate(zip((t0, t1, t2, t3), out_refs)):
-
-        def piece(j, carry):
-            both = jnp.concatenate(shifts(hid_ref, 2 * d + j) + shifts(dpre_ref, 2 * d + j), axis=-1).astype(BF)
-            depth = both.shape[-1]
-            acc = dot(both[0:rows].reshape(rows * cols, depth), w2_ref[0])
-            acc += dot(both[1 : 1 + rows].reshape(rows * cols, depth), w2_ref[1])
-            acc += dot(both[2 : 2 + rows].reshape(rows * cols, depth), w2_ref[2])
-            own = pltpu.roll(tile[j].astype(F32), width - 4, 1)[:, :cols]
-            out_ref[j] = (own + acc.reshape(rows, cols, 128)).astype(BF)
-            return carry
-
-        lax.fori_loop(0, 2, piece, 0)
+    def piece(at, tile, out_ref, j, carry):
+        both = jnp.concatenate(shifts(hid_ref, at + j) + shifts(dpre_ref, at + j), axis=-1).astype(BF)
+        depth = both.shape[-1]
+        acc = dot(both[0:rows].reshape(rows * cols, depth), w2_ref[0])
+        acc += dot(both[1 : 1 + rows].reshape(rows * cols, depth), w2_ref[1])
+        acc += dot(both[2 : 2 + rows].reshape(rows * cols, depth), w2_ref[2])
+        own = pltpu.roll(tile[j].astype(F32), width - 4, 1)[:, :cols]
+        out_ref[j] = (own + acc.reshape(rows, cols, 128)).astype(BF)
+        return carry
+
+    at = 0
+    for tile, out_ref in zip((t0, t1, t2, t3, t4), out_refs):
+        lax.fori_loop(0, tile.shape[0], functools.partial(piece, at, tile, out_ref), 0)
+        at += tile.shape[0]
 
 
 def sum_kernel(parts_ref, out_ref):
@@ -299,18 +308,24 @@
         name="pack",
     )(me, ensemble, cotangent)
     got = swap(give, 0, 1, groups)
+    sizes = [2] * (chips - 1) + [1, 1]
     tiles = pl.pallas_call(
         pair_kernel,
-        out_shape=[vm((2, rows, width, 128), BF)] * chips,
+        out_shape=[vm((n, rows, width, 128), BF) for n in sizes],
         in_specs=[vspec] * 2,
-        out_specs=[vspec] * chips,
+        out_specs=[vspec] * len(sizes),
         name="pair",
     )(*near(keep, got))
-    tiles = [tiles[0]] + [swap(tiles[i], ORDER[i], 0, groups) for i in range(1, chips)]
+    back = chips - 1
+    relay = swap(tiles[4], back, 0, groups)
+    far = swap(tiles[3], 2, 0, groups)
+    beside = [swap(tiles[i], ORDER[i], 0, groups) for i in (2, 1)]
+    relay = swap(relay, back, 0, groups)
+    tiles = [tiles[0], beside[1], beside[0], far, relay]
     head, tail = pl.pallas_call(
         edges_kernel,
         out_shape=[vm((groups, 2, width, 128), BF)] * 2,
-        in_specs=[vspec] * chips,
+        in_specs=[vspec] * len(sizes),
         out_specs=[vspec] * 2,
         name="edges",
     )(*near(*tiles))
@@ -343,7 +358,7 @@
     grads, hid, dpre = pl.pallas_call(
         tile_kernel,
         out_shape=[vm((slices * per, channels), BF), compact, compact],
-        in_specs=[sspec] + [vspec] * (chips + 4) + [hspec],
+        in_specs=[sspec] + [vspec] * (len(sizes) + 4) + [hspec],
         out_specs=[vspec, hspec, hspec],
         scratch_shapes=[
             vm((groups, rows, width, 128), BF),
@@ -368,9 +383,9 @@
     )(lat, *near(*tiles, top, bot, w1, pool_weight), w2)
     pieces = list(pl.pallas_call(
         output_kernel,
-        out_shape=[vm((2, rows, cols * mem_local, 128), BF)] * chips,
-        in_specs=[vspec] * (chips + 3),
-        out_specs=[vspec] * chips,
+        out_shape=[vm((n, rows, cols * mem_local, 128), BF) for n in sizes],
+        in_specs=[vspec] * (len(sizes) + 3),
+        out_specs=[vspec] * len(sizes),
         name="output",
     )(*near(*tiles), hid, dpre, w2))
 
@@ -387,10 +402,12 @@
         )(*near(parts))
 
     parts = exchange(grads.reshape(slices, per, channels), PLANE)
-    far = swap(pieces[3], chips - ORDER[3], 0, groups)
+    relay = swap(pieces[4], back, 0, groups)
+    far = swap(pieces[3], 2, 0, groups)
     parts, pieces[1], pieces[2] = lax.optimization_barrier((parts, pieces[1], pieces[2]))
-    pieces[1:3] = [swap(piece, chips - d, 0, groups) for d, piece in zip(ORDER[1:3], pieces[1:3])]
-    pieces[3] = far
+    beside = [swap(pieces[i], chips - ORDER[i], 0, groups) for i in (1, 2)]
+    relay = swap(relay, back, 0, groups)
+    pieces = [pieces[0], *beside, far]
     parts = add_up(parts, copies)
     parts = exchange(parts, REST)
     parts = add_up(parts, slices)
@@ -400,7 +417,7 @@
         in_specs=[vspec] * chips,
         out_specs=vspec,
         name="other",
-    )(*near(*pieces))
+    )(*near(*pieces[:3], relay))
     theirs = swap(other, 0, 1, groups)
     full = exchange(parts, PLANE).reshape(slices * per, channels)
     members = mem_local * groups

time: 105 us -> 112 us (1.067)
  starting transfers between devices: 48.9 us -> 56 us
    ppermute x8 -> x12, starting transfers between devices: 20.9 us -> 25.8 us  [swap(): return lax.ppermute(value, MEMBER, pairs)]
    all_to_all x3, starting transfers between devices: 23.6 us -> 25.8 us  [exchange(): return lax.all_to_all(value, axis, split_axis=0, concat_axis=0, tiled=True)]
    all_to_all x3, waiting for transfers between devices: 11.4 us -> 10.3 us  [exchange(): return lax.all_to_all(value, axis, split_axis=0, concat_axis=0, tiled=True)]
    ppermute x8 -> x12, waiting for transfers between devices: 14.5 us -> 15.4 us  [swap(): return lax.ppermute(value, MEMBER, pairs)]
  transfers between devices with their start and end apart: 13 -> 17, of which waited for: 10 -> 8; matrix products, arithmetic and copies ran while one was open for 1% -> 1% of each run, Pallas kernels for 7% -> 7%
where the time goes in v3:
time: 112 us; the launch traced here: 111 us
  starting transfers between devices  56 us (50%)
  waiting for transfers between devices  31 us (28%)
  Pallas kernels  22.3 us (20%)
    ppermute x12, starting transfers between devices, swap(): return lax.ppermute(value, MEMBER, pairs)  25.8 us
    all_to_all x3, starting transfers between devices, exchange(): return lax.all_to_all(value, axis, split_axis=0, concat_axis=0, tiled=True)  25.8 us
    ppermute x12, waiting for transfers between devices, swap(): return lax.ppermute(value, MEMBER, pairs)  15.4 us
    pallas_call x1, Pallas kernels, block(): pl.pallas_call(tile_kernel, out_shape=[vm((slices * per, channels), BF),...  11 us
    all_to_all x3, waiting for transfers between devices, exchange(): return lax.all_to_all(value, axis, split_axis=0, concat_axis=0, tiled=True)  10.3 us
    pallas_call x1, Pallas kernels, block(): pl.pallas_call(output_kernel, out_shape=[vm((n, rows, cols * mem_local, 1...  5.19 us
    ppermute x1, waiting for transfers between devices, block(): bot = lax.ppermute(head, LAT, [(i + 1, i) for i in range(bands - 1)])  3.83 us
    ppermute x1, starting transfers between devices, block(): top = lax.ppermute(tail, LAT, [(i, i + 1) for i in range(bands - 1)])  3.13 us
  transfers between devices with their start and end apart: 17, of which 8 were waited for; matrix products, arithmetic and copies ran while one was open for 1% of the time, Pallas kernels for 7%

profile of v3, /device:TPU:1, one launch (start us, length us, event | category | flops | bytes accessed | tf_op | source)
XLA Modules:
  0.0 111.0 jit_solution(14864511112066485057)
XLA Ops:
  0.7 2.0 %pack.1 = (bf16[4,4,72,128]{3,2,1,0:T(8,128)(2,1)S(1)}, bf16[4,4,72,128]{3,2,1,0:T(8,128)(2,1)S(1)}) custom-call(s32[1]{0:T(128)} %bitcast.me_ref, bf16[2,64,4,256]{3,2,1,0:T(4,128)(2,1)} %ens_ref.1, bf16[2,64,4,256]{3,2,1,0:T(4,128)(2,1)} %cot_ref.1), custom_call_target="tpu_custom_call" | custom-call | tf_op jit(solution)/shard_map/pack/pallas_call | solution.py:302
  2.7 3.3 %collective-permute-start = (bf16[4,4,72,128]{3,2,1,0:T(8,128)(2,1)S(1)}, bf16[4,4,72,128]{3,2,1,0:T(8,128)(2,1)S(1)}, u32[]{:S(2)}, u32[]{:S(2)}) collective-permute-start(bf16[4,4,72,128]{3,2,1,0:T(8,128)(2,1)S(1)} %get-tuple-element.31), channel_id=1, source_target_pairs={{0,32},{32,0},{64,96},{96,64},{128,160},{160,128},{192,224},{224,1... | collective-permute-start | bytes 884744 | tf_op jit(solution)/shard_map/ppermute | solution.py:30
  6.0 1.2 %collective-permute-done.got_ref = bf16[4,4,72,128]{3,2,1,0:T(8,128)(2,1)S(1)} collective-permute-done((bf16[4,4,72,128]{3,2,1,0:T(8,128)(2,1)S(1)}, bf16[4,4,72,128]{3,2,1,0:T(8,128)(2,1)S(1)}, u32[]{:S(2)}, u32[]{:S(2)}) %collective-permute-start) | collective-permute-done | bytes 294944 | tf_op jit(solution)/shard_map/ppermute | solution.py:30
  7.2 4.4 %collective-permute-start.4 = (bf16[1,4,72,128]{3,2,1,0:T(8,128)(2,1)S(1)}, bf16[1,4,72,128]{3,2,1,0:T(8,128)(2,1)S(1)}, u32[]{:S(2)}, u32[]{:S(2)}) collective-permute-start(bf16[1,4,72,128]{3,2,1,0:T(8,128)(2,1)S(1)} %get-tuple-element.36), channel_id=1, source_target_pairs={{0,192},{32,224},{64,0},{96,32},{128,64},{160,96},{192,128},{224,1... | collective-permute-start | bytes 221192 | tf_op jit(solution)/shard_map/ppermute | solution.py:30
  11.6 3.6 %collective-permute-start.2 = (bf16[2,4,72,128]{3,2,1,0:T(8,128)(2,1)S(1)}, bf16[2,4,72,128]{3,2,1,0:T(8,128)(2,1)S(1)}, u32[]{:S(2)}, u32[]{:S(2)}) collective-permute-start(bf16[2,4,72,128]{3,2,1,0:T(8,128)(2,1)S(1)} %get-tuple-element.34), channel_id=1, source_target_pairs={{0,192},{32,224},{64,0},{96,32},{128,64},{160,96},{192,128},{224,1... | collective-permute-start | bytes 442376 | tf_op jit(solution)/shard_map/ppermute | solution.py:30
  15.2 1.1 collective-permute-start.3
  16.3 1.1 collective-permute-start.5
  17.4 7.0 %collective-permute-done.3.refs_3_.t3 = bf16[1,4,72,128]{3,2,1,0:T(8,128)(2,1)S(1)} collective-permute-done((bf16[1,4,72,128]{3,2,1,0:T(8,128)(2,1)S(1)}, bf16[1,4,72,128]{3,2,1,0:T(8,128)(2,1)S(1)}, u32[]{:S(2)}, u32[]{:S(2)}) %collective-permute-start.3) | collective-permute-done | bytes 73760 | tf_op jit(solution)/shard_map/ppermute | solution.py:30
  24.5 3.1 %collective-permute-start.6 = (bf16[8,2,72,128]{3,2,1,0:T(8,128)(2,1)S(1)}, bf16[8,2,72,128]{3,2,1,0:T(8,128)(2,1)S(1)}, u32[]{:S(2)}, u32[]{:S(2)}) collective-permute-start(bf16[8,2,72,128]{3,2,1,0:T(8,128)(2,1)S(1)} %get-tuple-element.37), channel_id=1, source_target_pairs={{0,1},{1,2},{2,3},{3,4},{4,5},{5,6},{6,7},{7,8},{8,9},{9,10},{10,1... | collective-permute-start | bytes 884744 | tf_op jit(solution)/shard_map/ppermute | solution.py:332
  27.6 1.3 %collective-permute-start.7 = (bf16[8,2,72,128]{3,2,1,0:T(8,128)(2,1)S(1)}, bf16[8,2,72,128]{3,2,1,0:T(8,128)(2,1)S(1)}, u32[]{:S(2)}, u32[]{:S(2)}) collective-permute-start(bf16[8,2,72,128]{3,2,1,0:T(8,128)(2,1)S(1)} %get-tuple-element.38), channel_id=1, source_target_pairs={{1,0},{2,1},{3,2},{4,3},{5,4},{6,5},{7,6},{8,7},{9,8},{10,9},{11,1... | collective-permute-start | bytes 884744 | tf_op jit(solution)/shard_map/ppermute | solution.py:333
  29.2 0.2 copy.13
  29.9 1.4 %collective-permute-done.6.top_ref = bf16[8,2,72,128]{3,2,1,0:T(8,128)(2,1)S(1)} collective-permute-done((bf16[8,2,72,128]{3,2,1,0:T(8,128)(2,1)S(1)}, bf16[8,2,72,128]{3,2,1,0:T(8,128)(2,1)S(1)}, u32[]{:S(2)}, u32[]{:S(2)}) %collective-permute-start.6) | collective-permute-done | bytes 294944 | tf_op jit(solution)/shard_map/ppermute | solution.py:332
  31.3 3.8 %collective-permute-done.7.bot_ref = bf16[8,2,72,128]{3,2,1,0:T(8,128)(2,1)S(1)} collective-permute-done((bf16[8,2,72,128]{3,2,1,0:T(8,128)(2,1)S(1)}, bf16[8,2,72,128]{3,2,1,0:T(8,128)(2,1)S(1)}, u32[]{:S(2)}, u32[]{:S(2)}) %collective-permute-start.7) | collective-permute-done | bytes 294944 | tf_op jit(solution)/shard_map/ppermute | solution.py:333
  35.1 11.0 %tile.1 = (bf16[1408,128]{1,0:T(8,128)(2,1)}, bf16[8,6,72,128]{3,2,1,0:T(8,128)(2,1)}, bf16[8,6,72,128]{3,2,1,0:T(8,128)(2,1)}) custom-call(s32[2]{0:T(128)S(1)} %pad_add_fusion.lat_ref, bf16[2,4,72,128]{3,2,1,0:T(8,128)(2,1)S(1)} %get-tuple-element.32.refs_0_.t0, bf16[2,4,72,128]{3,2,1,0:T(8,128)(2,1)S(1)} %collective-permute-done.1.refs_1_.t1, ...), custom_call_target="tpu_custom_call" | custom-call | tf_op jit(solution)/shard_map/tile/pallas_call | solution.py:358
  46.1 13.0 %all-to-all-start = ((bf16[16,88,128]{2,1,0:T(8,128)(2,1)}), bf16[16,88,128]{2,1,0:T(8,128)(2,1)S(1)}, u32[]{:S(2)}, u32[]{:S(2)}) async-start(bf16[16,88,128]{2,1,0:T(8,128)(2,1)} %bitcast.7), calls=%async_computation | async-start | bytes 720896 | tf_op jit(solution)/shard_map/all_to_all | solution.py:393
  59.1 5.2 %output.1 = (bf16[2,4,64,128]{3,2,1,0:T(8,128)(2,1)S(1)}, bf16[2,4,64,128]{3,2,1,0:T(8,128)(2,1)S(1)}, bf16[2,4,64,128]{3,2,1,0:T(8,128)(2,1)S(1)}, bf16[1,4,64,...) custom-call(bf16[2,4,72,128]{3,2,1,0:T(8,128)(2,1)S(1)} %get-tuple-element.32.refs_0_.t0, ...), custom_call_target="tpu_custom_call" | custom-call | tf_op jit(solution)/shard_map/output/pallas_call | solution.py:384
  64.3 2.9 %all-to-all-done.parts_ref = bf16[16,88,128]{2,1,0:T(8,128)(2,1)S(1)} async-done(((bf16[16,88,128]{2,1,0:T(8,128)(2,1)}), bf16[16,88,128]{2,1,0:T(8,128)(2,1)S(1)}, u32[]{:S(2)}, u32[]{:S(2)}) %all-to-all-start) | async-done | bytes 360480 | tf_op jit(solution)/shard_map/all_to_all | solution.py:393
  67.2 0.8 total.2
  68.0 9.2 %all-to-all-start.1 = ((bf16[16,88,128]{2,1,0:T(8,128)(2,1)}), bf16[16,88,128]{2,1,0:T(8,128)(2,1)S(1)}, u32[]{:S(2)}, u32[]{:S(2)}) async-start(bf16[16,88,128]{2,1,0:T(8,128)(2,1)} %total.2), calls=%async_computation.1 | async-start | bytes 720896 | tf_op jit(solution)/shard_map/all_to_all | solution.py:393
  77.2 3.5 %collective-permute-start.11 = (bf16[1,4,64,128]{3,2,1,0:T(8,128)(2,1)S(1)}, bf16[1,4,64,128]{3,2,1,0:T(8,128)(2,1)S(1)}, u32[]{:S(2)}, u32[]{:S(2)}) collective-permute-start(bf16[1,4,64,128]{3,2,1,0:T(8,128)(2,1)S(1)} %get-tuple-element.48), channel_id=1, source_target_pairs={{0,192},{32,224},{64,0},{96,32},{128,64},{160,96},{192,128},{224,1... | collective-permute-start | bytes 196616 | tf_op jit(solution)/shard_map/ppermute | solution.py:30
  80.7 2.1 %collective-permute-start.8 = (bf16[2,4,64,128]{3,2,1,0:T(8,128)(2,1)S(1)}, bf16[2,4,64,128]{3,2,1,0:T(8,128)(2,1)S(1)}, u32[]{:S(2)}, u32[]{:S(2)}) collective-permute-start(bf16[2,4,64,128]{3,2,1,0:T(8,128)(2,1)S(1)} %get-tuple-element.45), channel_id=1, source_target_pairs={{0,192},{32,224},{64,0},{96,32},{128,64},{160,96},{192,128},{224,1... | collective-permute-start | bytes 393224 | tf_op jit(solution)/shard_map/ppermute | solution.py:30
  82.7 0.3 collective-permute-start.9
  83.0 7.4 %all-to-all-done.1.parts_ref = bf16[16,88,128]{2,1,0:T(8,128)(2,1)S(1)} async-done(((bf16[16,88,128]{2,1,0:T(8,128)(2,1)}), bf16[16,88,128]{2,1,0:T(8,128)(2,1)S(1)}, u32[]{:S(2)}, u32[]{:S(2)}) %all-to-all-start.1) | async-done | bytes 360480 | tf_op jit(solution)/shard_map/all_to_all | solution.py:393
  90.4 0.8 total.3
  91.2 3.5 %all-to-all-start.2 = ((bf16[16,88,128]{2,1,0:T(8,128)(2,1)}), bf16[16,88,128]{2,1,0:T(8,128)(2,1)S(1)}, u32[]{:S(2)}, u32[]{:S(2)}) async-start(bf16[16,88,128]{2,1,0:T(8,128)(2,1)} %total.3), calls=%async_computation.2 | async-start | bytes 720896 | tf_op jit(solution)/shard_map/all_to_all | solution.py:393
  94.8 3.0 %collective-permute-start.12 = (bf16[1,4,64,128]{3,2,1,0:T(8,128)(2,1)S(1)}, bf16[1,4,64,128]{3,2,1,0:T(8,128)(2,1)S(1)}, u32[]{:S(2)}, u32[]{:S(2)}) collective-permute-start(bf16[1,4,64,128]{3,2,1,0:T(8,128)(2,1)S(1)} %collective-permute-done.11), channel_id=1, source_target_pairs={{0,192},{32,224},{64,0},{96,32},{128,64},{160,96},{192,128},{224,1... | collective-permute-start | bytes 196616 | tf_op jit(solution)/shard_map/ppermute | solution.py:30
  97.8 2.2 %collective-permute-done.12.refs_3_ = bf16[1,4,64,128]{3,2,1,0:T(8,128)(2,1)S(1)} collective-permute-done((bf16[1,4,64,128]{3,2,1,0:T(8,128)(2,1)S(1)}, bf16[1,4,64,128]{3,2,1,0:T(8,128)(2,1)S(1)}, u32[]{:S(2)}, u32[]{:S(2)}) %collective-permute-start.12) | collective-permute-done | bytes 65568 | tf_op jit(solution)/shard_map/ppermute | solution.py:30
  100.0 1.1 collective-permute-start.13
  101.1 2.5 %collective-permute-start.10 = (bf16[1,4,64,128]{3,2,1,0:T(8,128)(2,1)S(1)}, bf16[1,4,64,128]{3,2,1,0:T(8,128)(2,1)S(1)}, u32[]{:S(2)}, u32[]{:S(2)}) collective-permute-start(bf16[1,4,64,128]{3,2,1,0:T(8,128)(2,1)S(1)} %get-tuple-element.47), channel_id=1, source_target_pairs={{0,128},{32,160},{64,192},{96,224},{128,0},{160,32},{192,64},{224,... | collective-permute-start | bytes 196616 | tf_op jit(solution)/shard_map/ppermute | solution.py:30
  103.6 5.0 %collective-permute-done.10.refs_3_ = bf16[1,4,64,128]{3,2,1,0:T(8,128)(2,1)S(1)} collective-permute-done((bf16[1,4,64,128]{3,2,1,0:T(8,128)(2,1)S(1)}, bf16[1,4,64,128]{3,2,1,0:T(8,128)(2,1)S(1)}, u32[]{:S(2)}, u32[]{:S(2)}) %collective-permute-start.10) | collective-permute-done | bytes 65568 | tf_op jit(solution)/shard_map/ppermute | solution.py:30
  108.6 1.5 %unpack.1 = (bf16[2,64,4,256]{3,2,1,0:T(4,128)(2,1)}, bf16[2,64,4,256]{3,2,1,0:T(4,128)(2,1)}) custom-call(s32[1]{0:T(128)} %bitcast.me_ref, bf16[2,4,64,128]{3,2,1,0:T(8,128)(2,1)S(1)} %get-tuple-element.41.refs_0_, bf16[2,4,64,128]{3,2,1,0:T(8,128)(2,1)S(1)} %collective-permute-done.8.refs_1_, bf16[2,4,64,128]{3,2,1,0:T(8,128)(2,1)S(1)} %collective-permute-done.9.refs_2_, ...), custom_call_target="tpu_custom_call" | custom-call | tf_op jit(solution)/shard_map/unpack/pallas_call | solution.py:436
  110.1 0.9 finish.1
  (29 shorter events, 0.8 us)
Async XLA Ops:
  0.6 14.6 %copy-start.3 = (bf16[3,3,64,128]{3,2,1,0:T(8,128)(2,1)S(1)}, bf16[3,3,64,128]{3,2,1,0:T(8,128)(2,1)}, u32[]{:S(2)}) copy-start(bf16[3,3,64,128]{3,2,1,0:T(8,128)(2,1)} %param.7) | copy-start | bytes 442372
  0.6 16.8 %copy-start.2 = (bf16[3,3,128,64]{2,3,1,0:T(8,128)(2,1)S(1)}, bf16[3,3,128,64]{2,3,1,0:T(8,128)(2,1)}, u32[]{:S(2)}) copy-start(bf16[3,3,128,64]{2,3,1,0:T(8,128)(2,1)} %param.9) | copy-start | bytes 442372
  2.7 4.5 %collective-permute-start = (bf16[4,4,72,128]{3,2,1,0:T(8,128)(2,1)S(1)}, bf16[4,4,72,128]{3,2,1,0:T(8,128)(2,1)S(1)}, u32[]{:S(2)}, u32[]{:S(2)}) collective-permute-start(bf16[4,4,72,128]{3,2,1,0:T(8,128)(2,1)S(1)} %get-tuple-element.31), channel_id=1, source_target_pairs={{0,32},{32,0},{64,96},{96,64},{128,160},{160,128},{192,224},{224,1... | collective-permute-start | bytes 884744 | tf_op jit(solution)/shard_map/ppermute | solution.py:30
  7.2 9.1 %collective-permute-start.4 = (bf16[1,4,72,128]{3,2,1,0:T(8,128)(2,1)S(1)}, bf16[1,4,72,128]{3,2,1,0:T(8,128)(2,1)S(1)}, u32[]{:S(2)}, u32[]{:S(2)}) collective-permute-start(bf16[1,4,72,128]{3,2,1,0:T(8,128)(2,1)S(1)} %get-tuple-element.36), channel_id=1, source_target_pairs={{0,192},{32,224},{64,0},{96,32},{128,64},{160,96},{192,128},{224,1... | collective-permute-start | bytes 221192 | tf_op jit(solution)/shard_map/ppermute | solution.py:30
  11.6 12.8 %collective-permute-start.1 = (bf16[2,4,72,128]{3,2,1,0:T(8,128)(2,1)S(1)}, bf16[2,4,72,128]{3,2,1,0:T(8,128)(2,1)S(1)}, u32[]{:S(2)}, u32[]{:S(2)}) collective-permute-start(bf16[2,4,72,128]{3,2,1,0:T(8,128)(2,1)S(1)} %get-tuple-element.33), channel_id=1, source_target_pairs={{0,64},{32,96},{64,128},{96,160},{128,192},{160,224},{192,0},{224,... | collective-permute-start | bytes 442376 | tf_op jit(solution)/shard_map/ppermute | solution.py:30
  11.6 12.8 %collective-permute-start.2 = (bf16[2,4,72,128]{3,2,1,0:T(8,128)(2,1)S(1)}, bf16[2,4,72,128]{3,2,1,0:T(8,128)(2,1)S(1)}, u32[]{:S(2)}, u32[]{:S(2)}) collective-permute-start(bf16[2,4,72,128]{3,2,1,0:T(8,128)(2,1)S(1)} %get-tuple-element.34), channel_id=1, source_target_pairs={{0,192},{32,224},{64,0},{96,32},{128,64},{160,96},{192,128},{224,1... | collective-permute-start | bytes 442376 | tf_op jit(solution)/shard_map/ppermute | solution.py:30
  15.2 9.2 %collective-permute-start.3 = (bf16[1,4,72,128]{3,2,1,0:T(8,128)(2,1)S(1)}, bf16[1,4,72,128]{3,2,1,0:T(8,128)(2,1)S(1)}, u32[]{:S(2)}, u32[]{:S(2)}) collective-permute-start(bf16[1,4,72,128]{3,2,1,0:T(8,128)(2,1)S(1)} %get-tuple-element.35), channel_id=1, source_target_pairs={{0,128},{32,160},{64,192},{96,224},{128,0},{160,32},{192,64},{224,... | collective-permute-start | bytes 221192 | tf_op jit(solution)/shard_map/ppermute | solution.py:30
  16.3 8.1 %collective-permute-start.5 = (bf16[1,4,72,128]{3,2,1,0:T(8,128)(2,1)S(1)}, bf16[1,4,72,128]{3,2,1,0:T(8,128)(2,1)S(1)}, u32[]{:S(2)}, u32[]{:S(2)}) collective-permute-start(bf16[1,4,72,128]{3,2,1,0:T(8,128)(2,1)S(1)} %collective-permute-done.4), channel_id=1, source_target_pairs={{0,192},{32,224},{64,0},{96,32},{128,64},{160,96},{192,128},{224,1... | collective-permute-start | bytes 221192 | tf_op jit(solution)/shard_map/ppermute | solution.py:30
  24.5 6.8 %collective-permute-start.6 = (bf16[8,2,72,128]{3,2,1,0:T(8,128)(2,1)S(1)}, bf16[8,2,72,128]{3,2,1,0:T(8,128)(2,1)S(1)}, u32[]{:S(2)}, u32[]{:S(2)}) collective-permute-start(bf16[8,2,72,128]{3,2,1,0:T(8,128)(2,1)S(1)} %get-tuple-element.37), channel_id=1, source_target_pairs={{0,1},{1,2},{2,3},{3,4},{4,5},{5,6},{6,7},{7,8},{8,9},{9,10},{10,1... | collective-permute-start | bytes 884744 | tf_op jit(solution)/shard_map/ppermute | solution.py:332
  27.6 7.5 %collective-permute-start.7 = (bf16[8,2,72,128]{3,2,1,0:T(8,128)(2,1)S(1)}, bf16[8,2,72,128]{3,2,1,0:T(8,128)(2,1)S(1)}, u32[]{:S(2)}, u32[]{:S(2)}) collective-permute-start(bf16[8,2,72,128]{3,2,1,0:T(8,128)(2,1)S(1)} %get-tuple-element.38), channel_id=1, source_target_pairs={{1,0},{2,1},{3,2},{4,3},{5,4},{6,5},{7,6},{8,7},{9,8},{10,9},{11,1... | collective-permute-start | bytes 884744 | tf_op jit(solution)/shard_map/ppermute | solution.py:333
  29.7 5.4 %copy-start.1 = (bf16[256,128]{1,0:T(8,128)(2,1)S(1)}, bf16[256,128]{1,0:T(8,128)(2,1)}, u32[]{:S(2)}) copy-start(bf16[256,128]{1,0:T(8,128)(2,1)} %pool_ref.1) | copy-start | bytes 196612
  29.8 16.2 %copy-start = (bf16[3,768,128]{2,1,0:T(8,128)(2,1)}, bf16[3,768,128]{2,1,0:T(8,128)(2,1)S(1)}, u32[]{:S(2)}) copy-start(bf16[3,768,128]{2,1,0:T(8,128)(2,1)S(1)} %pad_maximum_fusion._.w2_ref) | copy-start | bytes 1769476
  46.1 21.1 %all-to-all-start = ((bf16[16,88,128]{2,1,0:T(8,128)(2,1)}), bf16[16,88,128]{2,1,0:T(8,128)(2,1)S(1)}, u32[]{:S(2)}, u32[]{:S(2)}) async-start(bf16[16,88,128]{2,1,0:T(8,128)(2,1)} %bitcast.7), calls=%async_computation | async-start | bytes 720896 | tf_op jit(solution)/shard_map/all_to_all | solution.py:393
  68.0 22.5 %all-to-all-start.1 = ((bf16[16,88,128]{2,1,0:T(8,128)(2,1)}), bf16[16,88,128]{2,1,0:T(8,128)(2,1)S(1)}, u32[]{:S(2)}, u32[]{:S(2)}) async-start(bf16[16,88,128]{2,1,0:T(8,128)(2,1)} %total.2), calls=%async_computation.1 | async-start | bytes 720896 | tf_op jit(solution)/shard_map/all_to_all | solution.py:393
  77.2 17.6 %collective-permute-start.11 = (bf16[1,4,64,128]{3,2,1,0:T(8,128)(2,1)S(1)}, bf16[1,4,64,128]{3,2,1,0:T(8,128)(2,1)S(1)}, u32[]{:S(2)}, u32[]{:S(2)}) collective-permute-start(bf16[1,4,64,128]{3,2,1,0:T(8,128)(2,1)S(1)} %get-tuple-element.48), channel_id=1, source_target_pairs={{0,192},{32,224},{64,0},{96,32},{128,64},{160,96},{192,128},{224,1... | collective-permute-start | bytes 196616 | tf_op jit(solution)/shard_map/ppermute | solution.py:30
  80.7 19.3 %collective-permute-start.8 = (bf16[2,4,64,128]{3,2,1,0:T(8,128)(2,1)S(1)}, bf16[2,4,64,128]{3,2,1,0:T(8,128)(2,1)S(1)}, u32[]{:S(2)}, u32[]{:S(2)}) collective-permute-start(bf16[2,4,64,128]{3,2,1,0:T(8,128)(2,1)S(1)} %get-tuple-element.45), channel_id=1, source_target_pairs={{0,192},{32,224},{64,0},{96,32},{128,64},{160,96},{192,128},{224,1... | collective-permute-start | bytes 393224 | tf_op jit(solution)/shard_map/ppermute | solution.py:30
  82.7 17.2 %collective-permute-start.9 = (bf16[2,4,64,128]{3,2,1,0:T(8,128)(2,1)S(1)}, bf16[2,4,64,128]{3,2,1,0:T(8,128)(2,1)S(1)}, u32[]{:S(2)}, u32[]{:S(2)}) collective-permute-start(bf16[2,4,64,128]{3,2,1,0:T(8,128)(2,1)S(1)} %get-tuple-element.46), channel_id=1, source_target_pairs={{0,64},{32,96},{64,128},{96,160},{128,192},{160,224},{192,0},{224,... | collective-permute-start | bytes 393224 | tf_op jit(solution)/shard_map/ppermute | solution.py:30
  91.2 18.9 %all-to-all-start.2 = ((bf16[16,88,128]{2,1,0:T(8,128)(2,1)}), bf16[16,88,128]{2,1,0:T(8,128)(2,1)S(1)}, u32[]{:S(2)}, u32[]{:S(2)}) async-start(bf16[16,88,128]{2,1,0:T(8,128)(2,1)} %total.3), calls=%async_computation.2 | async-start | bytes 720896 | tf_op jit(solution)/shard_map/all_to_all | solution.py:393
  94.8 5.2 %collective-permute-start.12 = (bf16[1,4,64,128]{3,2,1,0:T(8,128)(2,1)S(1)}, bf16[1,4,64,128]{3,2,1,0:T(8,128)(2,1)S(1)}, u32[]{:S(2)}, u32[]{:S(2)}) collective-permute-start(bf16[1,4,64,128]{3,2,1,0:T(8,128)(2,1)S(1)} %collective-permute-done.11), channel_id=1, source_target_pairs={{0,192},{32,224},{64,0},{96,32},{128,64},{160,96},{192,128},{224,1... | collective-permute-start | bytes 196616 | tf_op jit(solution)/shard_map/ppermute | solution.py:30
  100.0 8.6 %collective-permute-start.13 = (bf16[4,4,64,128]{3,2,1,0:T(8,128)(2,1)S(1)}, bf16[4,4,64,128]{3,2,1,0:T(8,128)(2,1)S(1)}, u32[]{:S(2)}, u32[]{:S(2)}) collective-permute-start(bf16[4,4,64,128]{3,2,1,0:T(8,128)(2,1)S(1)} %other.1), channel_id=1, source_target_pairs={{0,32},{32,0},{64,96},{96,64},{128,160},{160,128},{192,224},{224,1... | collective-permute-start | bytes 786440 | tf_op jit(solution)/shard_map/ppermute | solution.py:30
  101.1 7.5 %collective-permute-start.10 = (bf16[1,4,64,128]{3,2,1,0:T(8,128)(2,1)S(1)}, bf16[1,4,64,128]{3,2,1,0:T(8,128)(2,1)S(1)}, u32[]{:S(2)}, u32[]{:S(2)}) collective-permute-start(bf16[1,4,64,128]{3,2,1,0:T(8,128)(2,1)S(1)} %get-tuple-element.47), channel_id=1, source_target_pairs={{0,128},{32,160},{64,192},{96,224},{128,0},{160,32},{192,64},{224,... | collective-permute-start | bytes 196616 | tf_op jit(solution)/shard_map/ppermute | solution.py:30

commit v4 on v2

--- a/solution.py
+++ b/solution.py
@@ -17,8 +17,8 @@
 
 MEMBER = ("zh", "core")
 LAT = ("y", "zl", "x")
-PLANE = ("y", "x")
-REST = ("zh", "core", "zl")
+LINE = ("zh", "core", "zl")
+REST = ("y", "x")
 ORDER = (0, 1, 3, 2)
 
 
@@ -335,7 +335,7 @@
     inner = rows + 2
     plane = (inner, WIDE, channels)
     used = 18 * (channels // 2) + 2 * channels
-    slices, copies = lax.axis_size(PLANE), lax.axis_size(REST)
+    slices, copies = lax.axis_size(LINE), lax.axis_size(REST)
     per = -(-used // (8 * slices)) * 8
     shifted = (groups, inner, cols * mem_local, 384)
     compact = pltpu.HBM((groups, inner, width, channels), BF)
@@ -386,7 +386,7 @@
             name="total",
         )(*near(parts))
 
-    parts = exchange(grads.reshape(slices, per, channels), PLANE)
+    parts = exchange(grads.reshape(slices, per, channels), LINE)
     far = swap(pieces[3], chips - ORDER[3], 0, groups)
     parts, pieces[1], pieces[2] = lax.optimization_barrier((parts, pieces[1], pieces[2]))
     pieces[1:3] = [swap(piece, chips - d, 0, groups) for d, piece in zip(ORDER[1:3], pieces[1:3])]
@@ -402,7 +402,7 @@
         name="other",
     )(*near(*pieces))
     theirs = swap(other, 0, 1, groups)
-    full = exchange(parts, PLANE).reshape(slices * per, channels)
+    full = exchange(parts, LINE).reshape(slices * per, channels)
     members = mem_local * groups
     scale = 1.0 / math.sqrt(members * bands * rows * lon)
     half = channels // 2

time: 105 us -> 122 us (1.16)
  blocking collectives: 0 us -> 17.4 us
  starting transfers between devices: 48.9 us -> 40.9 us
  waiting for transfers between devices: 31.9 us -> 39.6 us
    all_to_all x0 -> x1, blocking collectives: none -> 17.4 us  [exchange(): return lax.all_to_all(value, axis, split_axis=0, concat_axis=0, tiled=True)]
    ppermute x8, waiting for transfers between devices: 14.5 us -> 26.7 us  [swap(): return lax.ppermute(value, MEMBER, pairs)]
    all_to_all x3 -> x2, starting transfers between devices: 23.6 us -> 15.6 us  [exchange(): return lax.all_to_all(value, axis, split_axis=0, concat_axis=0, tiled=True)]
    all_to_all x3 -> x2, waiting for transfers between devices: 11.4 us -> 6.81 us  [exchange(): return lax.all_to_all(value, axis, split_axis=0, concat_axis=0, tiled=True)]
  transfers between devices with their start and end apart: 13 -> 12, of which waited for: 10 -> 9; matrix products, arithmetic and copies ran while one was open for 1% -> 1% of each run, Pallas kernels for 7% -> 6%
where the time goes in v4:
time: 122 us; the launch traced here: 121 us
  starting transfers between devices  40.9 us (34%)
  waiting for transfers between devices  39.6 us (32%)
  Pallas kernels  21.7 us (18%)
  blocking collectives  17.4 us (14%)
    ppermute x8, waiting for transfers between devices, swap(): return lax.ppermute(value, MEMBER, pairs)  26.7 us
    ppermute x8, starting transfers between devices, swap(): return lax.ppermute(value, MEMBER, pairs)  20.9 us
    all_to_all x1, blocking collectives, exchange(): return lax.all_to_all(value, axis, split_axis=0, concat_axis=0, tiled=True)  17.4 us
    all_to_all x2, starting transfers between devices, exchange(): return lax.all_to_all(value, axis, split_axis=0, concat_axis=0, tiled=True)  15.6 us
    pallas_call x1, Pallas kernels, block(): pl.pallas_call(tile_kernel, out_shape=[vm((slices * per, channels), BF),...  10.9 us
    all_to_all x2, waiting for transfers between devices, exchange(): return lax.all_to_all(value, axis, split_axis=0, concat_axis=0, tiled=True)  6.81 us
    pallas_call x1, Pallas kernels, block(): pl.pallas_call(output_kernel, out_shape=[vm((2, rows, cols * mem_local, 1...  5.41 us
    ppermute x1, waiting for transfers between devices, block(): bot = lax.ppermute(head, LAT, [(i + 1, i) for i in range(bands - 1)])  3.85 us
  transfers between devices with their start and end apart: 12, of which 9 were waited for; matrix products, arithmetic and copies ran while one was open for 1% of the time, Pallas kernels for 6%

profile of v4, /device:TPU:1, one launch (start us, length us, event | category | flops | bytes accessed | tf_op | source)
XLA Modules:
  0.0 121.3 jit_solution(10237508488196918441)
XLA Ops:
  0.7 2.0 %pack.1 = (bf16[4,4,72,128]{3,2,1,0:T(8,128)(2,1)S(1)}, bf16[4,4,72,128]{3,2,1,0:T(8,128)(2,1)S(1)}) custom-call(s32[1]{0:T(128)} %bitcast.me_ref, bf16[2,64,4,256]{3,2,1,0:T(4,128)(2,1)} %ens_ref.1, bf16[2,64,4,256]{3,2,1,0:T(4,128)(2,1)} %cot_ref.1), custom_call_target="tpu_custom_call" | custom-call | tf_op jit(solution)/shard_map/pack/pallas_call | solution.py:293
  2.7 3.3 %collective-permute-start = (bf16[4,4,72,128]{3,2,1,0:T(8,128)(2,1)S(1)}, bf16[4,4,72,128]{3,2,1,0:T(8,128)(2,1)S(1)}, u32[]{:S(2)}, u32[]{:S(2)}) collective-permute-start(bf16[4,4,72,128]{3,2,1,0:T(8,128)(2,1)S(1)} %get-tuple-element.29), channel_id=1, source_target_pairs={{0,32},{32,0},{64,96},{96,64},{128,160},{160,128},{192,224},{224,1... | collective-permute-start | bytes 884744 | tf_op jit(solution)/shard_map/ppermute | solution.py:30
  6.0 1.2 collective-permute-done.got_ref
  7.2 1.4 %collective-permute-start.1 = (bf16[2,4,72,128]{3,2,1,0:T(8,128)(2,1)S(1)}, bf16[2,4,72,128]{3,2,1,0:T(8,128)(2,1)S(1)}, u32[]{:S(2)}, u32[]{:S(2)}) collective-permute-start(bf16[2,4,72,128]{3,2,1,0:T(8,128)(2,1)S(1)} %get-tuple-element.31), channel_id=1, source_target_pairs={{0,64},{32,96},{64,128},{96,160},{128,192},{160,224},{192,0},{224,... | collective-permute-start | bytes 442376 | tf_op jit(solution)/shard_map/ppermute | solution.py:30
  8.6 3.1 %collective-permute-start.2 = (bf16[2,4,72,128]{3,2,1,0:T(8,128)(2,1)S(1)}, bf16[2,4,72,128]{3,2,1,0:T(8,128)(2,1)S(1)}, u32[]{:S(2)}, u32[]{:S(2)}) collective-permute-start(bf16[2,4,72,128]{3,2,1,0:T(8,128)(2,1)S(1)} %get-tuple-element.32), channel_id=1, source_target_pairs={{0,192},{32,224},{64,0},{96,32},{128,64},{160,96},{192,128},{224,1... | collective-permute-start | bytes 442376 | tf_op jit(solution)/shard_map/ppermute | solution.py:30
  11.7 4.4 %collective-permute-start.3 = (bf16[2,4,72,128]{3,2,1,0:T(8,128)(2,1)S(1)}, bf16[2,4,72,128]{3,2,1,0:T(8,128)(2,1)S(1)}, u32[]{:S(2)}, u32[]{:S(2)}) collective-permute-start(bf16[2,4,72,128]{3,2,1,0:T(8,128)(2,1)S(1)} %get-tuple-element.33), channel_id=1, source_target_pairs={{0,128},{32,160},{64,192},{96,224},{128,0},{160,32},{192,64},{224,... | collective-permute-start | bytes 442376 | tf_op jit(solution)/shard_map/ppermute | solution.py:30
  16.1 7.0 %collective-permute-done.2.refs_2_.t2 = bf16[2,4,72,128]{3,2,1,0:T(8,128)(2,1)S(1)} collective-permute-done((bf16[2,4,72,128]{3,2,1,0:T(8,128)(2,1)S(1)}, bf16[2,4,72,128]{3,2,1,0:T(8,128)(2,1)S(1)}, u32[]{:S(2)}, u32[]{:S(2)}) %collective-permute-start.2) | collective-permute-done | bytes 147488 | tf_op jit(solution)/shard_map/ppermute | solution.py:30
  23.2 1.7 %collective-permute-done.3.refs_3_.t3 = bf16[2,4,72,128]{3,2,1,0:T(8,128)(2,1)S(1)} collective-permute-done((bf16[2,4,72,128]{3,2,1,0:T(8,128)(2,1)S(1)}, bf16[2,4,72,128]{3,2,1,0:T(8,128)(2,1)S(1)}, u32[]{:S(2)}, u32[]{:S(2)}) %collective-permute-start.3) | collective-permute-done | bytes 147488 | tf_op jit(solution)/shard_map/ppermute | solution.py:30
  24.9 3.1 %collective-permute-start.4 = (bf16[8,2,72,128]{3,2,1,0:T(8,128)(2,1)S(1)}, bf16[8,2,72,128]{3,2,1,0:T(8,128)(2,1)S(1)}, u32[]{:S(2)}, u32[]{:S(2)}) collective-permute-start(bf16[8,2,72,128]{3,2,1,0:T(8,128)(2,1)S(1)} %get-tuple-element.34), channel_id=1, source_target_pairs={{0,1},{1,2},{2,3},{3,4},{4,5},{5,6},{6,7},{7,8},{8,9},{9,10},{10,1... | collective-permute-start | bytes 884744 | tf_op jit(solution)/shard_map/ppermute | solution.py:317
  28.1 1.3 %collective-permute-start.5 = (bf16[8,2,72,128]{3,2,1,0:T(8,128)(2,1)S(1)}, bf16[8,2,72,128]{3,2,1,0:T(8,128)(2,1)S(1)}, u32[]{:S(2)}, u32[]{:S(2)}) collective-permute-start(bf16[8,2,72,128]{3,2,1,0:T(8,128)(2,1)S(1)} %get-tuple-element.35), channel_id=1, source_target_pairs={{1,0},{2,1},{3,2},{4,3},{5,4},{6,5},{7,6},{8,7},{9,8},{10,9},{11,1... | collective-permute-start | bytes 884744 | tf_op jit(solution)/shard_map/ppermute | solution.py:318
  29.4 0.1 pad_add_fusion.lat_ref
  29.4 0.2 copy.12
  29.7 0.2 copy.13
  29.9 0.2 concatenate.22.clone
  30.3 2.2 %collective-permute-done.4.top_ref = bf16[8,2,72,128]{3,2,1,0:T(8,128)(2,1)S(1)} collective-permute-done((bf16[8,2,72,128]{3,2,1,0:T(8,128)(2,1)S(1)}, bf16[8,2,72,128]{3,2,1,0:T(8,128)(2,1)S(1)}, u32[]{:S(2)}, u32[]{:S(2)}) %collective-permute-start.4) | collective-permute-done | bytes 294944 | tf_op jit(solution)/shard_map/ppermute | solution.py:317
  32.5 3.8 %collective-permute-done.5.bot_ref = bf16[8,2,72,128]{3,2,1,0:T(8,128)(2,1)S(1)} collective-permute-done((bf16[8,2,72,128]{3,2,1,0:T(8,128)(2,1)S(1)}, bf16[8,2,72,128]{3,2,1,0:T(8,128)(2,1)S(1)}, u32[]{:S(2)}, u32[]{:S(2)}) %collective-permute-start.5) | collective-permute-done | bytes 294944 | tf_op jit(solution)/shard_map/ppermute | solution.py:318
  36.3 10.9 %tile.1 = (bf16[1408,128]{1,0:T(8,128)(2,1)}, bf16[8,6,72,128]{3,2,1,0:T(8,128)(2,1)}, bf16[8,6,72,128]{3,2,1,0:T(8,128)(2,1)}) custom-call(s32[2]{0:T(128)S(1)} %pad_add_fusion.lat_ref, bf16[2,4,72,128]{3,2,1,0:T(8,128)(2,1)S(1)} %get-tuple-element.30.refs_0_.t0, bf16[2,4,72,128]{3,2,1,0:T(8,128)(2,1)S(1)} %collective-permute-done.1.refs_1_.t1, ...), custom_call_target="tpu_custom_call" | custom-call | tf_op jit(solution)/shard_map/tile/pallas_call | solution.py:343
  47.3 10.2 %all-to-all-start = ((bf16[16,88,128]{2,1,0:T(8,128)(2,1)}), bf16[16,88,128]{2,1,0:T(8,128)(2,1)S(1)}, u32[]{:S(2)}, u32[]{:S(2)}) async-start(bf16[16,88,128]{2,1,0:T(8,128)(2,1)} %bitcast.7), calls=%async_computation | async-start | bytes 720896 | tf_op jit(solution)/shard_map/all_to_all | solution.py:378
  57.5 5.4 %output.1 = (bf16[2,4,64,128]{3,2,1,0:T(8,128)(2,1)S(1)}, bf16[2,4,64,128]{3,2,1,0:T(8,128)(2,1)S(1)}, bf16[2,4,64,128]{3,2,1,0:T(8,128)(2,1)S(1)}, bf16[2,4,64,128]{3,2,1,0:T(8,128)(2,1)S(1)}) custom-call(bf16[2,4,72,128]{3,2,1,0:T(8,128)(2,1)S(1)} %get-tuple-element.30.refs_0_.t0, bf16[2,4,72,128]{3,2,1,0:T(8,128)(2,1)S(1)} %collective-permute-done.1.refs_1_.t1, ...), custom_call_target="tpu_custom_call" | custom-call | tf_op jit(solution)/shard_map/output/pallas_call | solution.py:369
  62.9 6.8 %all-to-all-done.parts_ref = bf16[16,88,128]{2,1,0:T(8,128)(2,1)S(1)} async-done(((bf16[16,88,128]{2,1,0:T(8,128)(2,1)}), bf16[16,88,128]{2,1,0:T(8,128)(2,1)S(1)}, u32[]{:S(2)}, u32[]{:S(2)}) %all-to-all-start) | async-done | bytes 360480 | tf_op jit(solution)/shard_map/all_to_all | solution.py:378
  69.8 17.4 %all_to_all.15.parts_ref = bf16[16,88,128]{2,1,0:T(8,128)(2,1)S(1)} all-to-all(bf16[16,88,128]{2,1,0:T(8,128)(2,1)S(1)} %total.2), channel_id=1, replica_groups=mesh['zh'=4,'core'=2,'y'=4,'zl'=2,'x'=4] {'y','x'}, dimensions={0} | all-to-all | bytes 720896 | tf_op jit(solution)/shard_map/all_to_all | solution.py:378
  87.2 0.8 total.3
  88.0 5.4 %all-to-all-start.2 = ((bf16[16,88,128]{2,1,0:T(8,128)(2,1)}), bf16[16,88,128]{2,1,0:T(8,128)(2,1)S(1)}, u32[]{:S(2)}, u32[]{:S(2)}) async-start(bf16[16,88,128]{2,1,0:T(8,128)(2,1)} %total.3), calls=%async_computation.2 | async-start | bytes 720896 | tf_op jit(solution)/shard_map/all_to_all | solution.py:378
  93.4 5.3 %collective-permute-start.8 = (bf16[2,4,64,128]{3,2,1,0:T(8,128)(2,1)S(1)}, bf16[2,4,64,128]{3,2,1,0:T(8,128)(2,1)S(1)}, u32[]{:S(2)}, u32[]{:S(2)}) collective-permute-start(bf16[2,4,64,128]{3,2,1,0:T(8,128)(2,1)S(1)} %get-tuple-element.44), channel_id=1, source_target_pairs={{0,128},{32,160},{64,192},{96,224},{128,0},{160,32},{192,64},{224,... | collective-permute-start | bytes 393224 | tf_op jit(solution)/shard_map/ppermute | solution.py:30
  98.7 0.3 collective-permute-start.6
  98.9 2.1 %collective-permute-start.7 = (bf16[2,4,64,128]{3,2,1,0:T(8,128)(2,1)S(1)}, bf16[2,4,64,128]{3,2,1,0:T(8,128)(2,1)S(1)}, u32[]{:S(2)}, u32[]{:S(2)}) collective-permute-start(bf16[2,4,64,128]{3,2,1,0:T(8,128)(2,1)S(1)} %get-tuple-element.43), channel_id=1, source_target_pairs={{0,64},{32,96},{64,128},{96,160},{128,192},{160,224},{192,0},{224,... | collective-permute-start | bytes 393224 | tf_op jit(solution)/shard_map/ppermute | solution.py:30
  101.0 10.7 %collective-permute-done.8.refs_3_ = bf16[2,4,64,128]{3,2,1,0:T(8,128)(2,1)S(1)} collective-permute-done((bf16[2,4,64,128]{3,2,1,0:T(8,128)(2,1)S(1)}, bf16[2,4,64,128]{3,2,1,0:T(8,128)(2,1)S(1)}, u32[]{:S(2)}, u32[]{:S(2)}) %collective-permute-start.8) | collective-permute-done | bytes 131104 | tf_op jit(solution)/shard_map/ppermute | solution.py:30
  111.8 4.9 %collective-permute-done.7.refs_2_ = bf16[2,4,64,128]{3,2,1,0:T(8,128)(2,1)S(1)} collective-permute-done((bf16[2,4,64,128]{3,2,1,0:T(8,128)(2,1)S(1)}, bf16[2,4,64,128]{3,2,1,0:T(8,128)(2,1)S(1)}, u32[]{:S(2)}, u32[]{:S(2)}) %collective-permute-start.7) | collective-permute-done | bytes 131104 | tf_op jit(solution)/shard_map/ppermute | solution.py:30
  116.7 1.1 collective-permute-start.9
  117.8 1.2 collective-permute-done.9.refs_4_
  118.9 1.5 %unpack.1 = (bf16[2,64,4,256]{3,2,1,0:T(4,128)(2,1)}, bf16[2,64,4,256]{3,2,1,0:T(4,128)(2,1)}) custom-call(s32[1]{0:T(128)} %bitcast.me_ref, bf16[2,4,64,128]{3,2,1,0:T(8,128)(2,1)S(1)} %get-tuple-element.38.refs_0_, bf16[2,4,64,128]{3,2,1,0:T(8,128)(2,1)S(1)} %collective-permute-done.6.refs_1_, bf16[2,4,64,128]{3,2,1,0:T(8,128)(2,1)S(1)} %collective-permute-done.7.refs_2_, ...), custom_call_target="tpu_custom_call" | custom-call | tf_op jit(solution)/shard_map/unpack/pallas_call | solution.py:419
  120.5 0.9 finish.1
  (20 shorter events, 0.4 us)
Async XLA Ops:
  0.6 15.5 %copy-start.3 = (bf16[3,3,64,128]{3,2,1,0:T(8,128)(2,1)S(1)}, bf16[3,3,64,128]{3,2,1,0:T(8,128)(2,1)}, u32[]{:S(2)}) copy-start(bf16[3,3,64,128]{3,2,1,0:T(8,128)(2,1)} %param.7) | copy-start | bytes 442372
  0.6 15.5 %copy-start.2 = (bf16[3,3,128,64]{2,3,1,0:T(8,128)(2,1)S(1)}, bf16[3,3,128,64]{2,3,1,0:T(8,128)(2,1)}, u32[]{:S(2)}) copy-start(bf16[3,3,128,64]{2,3,1,0:T(8,128)(2,1)} %param.9) | copy-start | bytes 442372
  2.7 4.5 %collective-permute-start = (bf16[4,4,72,128]{3,2,1,0:T(8,128)(2,1)S(1)}, bf16[4,4,72,128]{3,2,1,0:T(8,128)(2,1)S(1)}, u32[]{:S(2)}, u32[]{:S(2)}) collective-permute-start(bf16[4,4,72,128]{3,2,1,0:T(8,128)(2,1)S(1)} %get-tuple-element.29), channel_id=1, source_target_pairs={{0,32},{32,0},{64,96},{96,64},{128,160},{160,128},{192,224},{224,1... | collective-permute-start | bytes 884744 | tf_op jit(solution)/shard_map/ppermute | solution.py:30
  7.2 8.9 %collective-permute-start.1 = (bf16[2,4,72,128]{3,2,1,0:T(8,128)(2,1)S(1)}, bf16[2,4,72,128]{3,2,1,0:T(8,128)(2,1)S(1)}, u32[]{:S(2)}, u32[]{:S(2)}) collective-permute-start(bf16[2,4,72,128]{3,2,1,0:T(8,128)(2,1)S(1)} %get-tuple-element.31), channel_id=1, source_target_pairs={{0,64},{32,96},{64,128},{96,160},{128,192},{160,224},{192,0},{224,... | collective-permute-start | bytes 442376 | tf_op jit(solution)/shard_map/ppermute | solution.py:30
  8.6 14.6 %collective-permute-start.2 = (bf16[2,4,72,128]{3,2,1,0:T(8,128)(2,1)S(1)}, bf16[2,4,72,128]{3,2,1,0:T(8,128)(2,1)S(1)}, u32[]{:S(2)}, u32[]{:S(2)}) collective-permute-start(bf16[2,4,72,128]{3,2,1,0:T(8,128)(2,1)S(1)} %get-tuple-element.32), channel_id=1, source_target_pairs={{0,192},{32,224},{64,0},{96,32},{128,64},{160,96},{192,128},{224,1... | collective-permute-start | bytes 442376 | tf_op jit(solution)/shard_map/ppermute | solution.py:30
  11.7 13.2 %collective-permute-start.3 = (bf16[2,4,72,128]{3,2,1,0:T(8,128)(2,1)S(1)}, bf16[2,4,72,128]{3,2,1,0:T(8,128)(2,1)S(1)}, u32[]{:S(2)}, u32[]{:S(2)}) collective-permute-start(bf16[2,4,72,128]{3,2,1,0:T(8,128)(2,1)S(1)} %get-tuple-element.33), channel_id=1, source_target_pairs={{0,128},{32,160},{64,192},{96,224},{128,0},{160,32},{192,64},{224,... | collective-permute-start | bytes 442376 | tf_op jit(solution)/shard_map/ppermute | solution.py:30
  24.9 7.6 %collective-permute-start.4 = (bf16[8,2,72,128]{3,2,1,0:T(8,128)(2,1)S(1)}, bf16[8,2,72,128]{3,2,1,0:T(8,128)(2,1)S(1)}, u32[]{:S(2)}, u32[]{:S(2)}) collective-permute-start(bf16[8,2,72,128]{3,2,1,0:T(8,128)(2,1)S(1)} %get-tuple-element.34), channel_id=1, source_target_pairs={{0,1},{1,2},{2,3},{3,4},{4,5},{5,6},{6,7},{7,8},{8,9},{9,10},{10,1... | collective-permute-start | bytes 884744 | tf_op jit(solution)/shard_map/ppermute | solution.py:317
  28.1 8.3 %collective-permute-start.5 = (bf16[8,2,72,128]{3,2,1,0:T(8,128)(2,1)S(1)}, bf16[8,2,72,128]{3,2,1,0:T(8,128)(2,1)S(1)}, u32[]{:S(2)}, u32[]{:S(2)}) collective-permute-start(bf16[8,2,72,128]{3,2,1,0:T(8,128)(2,1)S(1)} %get-tuple-element.35), channel_id=1, source_target_pairs={{1,0},{2,1},{3,2},{4,3},{5,4},{6,5},{7,6},{8,7},{9,8},{10,9},{11,1... | collective-permute-start | bytes 884744 | tf_op jit(solution)/shard_map/ppermute | solution.py:318
  30.2 6.2 %copy-start.1 = (bf16[256,128]{1,0:T(8,128)(2,1)S(1)}, bf16[256,128]{1,0:T(8,128)(2,1)}, u32[]{:S(2)}) copy-start(bf16[256,128]{1,0:T(8,128)(2,1)} %pool_ref.1) | copy-start | bytes 196612
  30.3 17.0 %copy-start = (bf16[3,768,128]{2,1,0:T(8,128)(2,1)}, bf16[3,768,128]{2,1,0:T(8,128)(2,1)S(1)}, u32[]{:S(2)}) copy-start(bf16[3,768,128]{2,1,0:T(8,128)(2,1)S(1)} %pad_maximum_fusion._.w2_ref) | copy-start | bytes 1769476
  47.3 22.5 %all-to-all-start = ((bf16[16,88,128]{2,1,0:T(8,128)(2,1)}), bf16[16,88,128]{2,1,0:T(8,128)(2,1)S(1)}, u32[]{:S(2)}, u32[]{:S(2)}) async-start(bf16[16,88,128]{2,1,0:T(8,128)(2,1)} %bitcast.7), calls=%async_computation | async-start | bytes 720896 | tf_op jit(solution)/shard_map/all_to_all | solution.py:378
  88.0 32.4 %all-to-all-start.2 = ((bf16[16,88,128]{2,1,0:T(8,128)(2,1)}), bf16[16,88,128]{2,1,0:T(8,128)(2,1)S(1)}, u32[]{:S(2)}, u32[]{:S(2)}) async-start(bf16[16,88,128]{2,1,0:T(8,128)(2,1)} %total.3), calls=%async_computation.2 | async-start | bytes 720896 | tf_op jit(solution)/shard_map/all_to_all | solution.py:378
  93.4 18.4 %collective-permute-start.8 = (bf16[2,4,64,128]{3,2,1,0:T(8,128)(2,1)S(1)}, bf16[2,4,64,128]{3,2,1,0:T(8,128)(2,1)S(1)}, u32[]{:S(2)}, u32[]{:S(2)}) collective-permute-start(bf16[2,4,64,128]{3,2,1,0:T(8,128)(2,1)S(1)} %get-tuple-element.44), channel_id=1, source_target_pairs={{0,128},{32,160},{64,192},{96,224},{128,0},{160,32},{192,64},{224,... | collective-permute-start | bytes 393224 | tf_op jit(solution)/shard_map/ppermute | solution.py:30
  98.7 13.1 %collective-permute-start.6 = (bf16[2,4,64,128]{3,2,1,0:T(8,128)(2,1)S(1)}, bf16[2,4,64,128]{3,2,1,0:T(8,128)(2,1)S(1)}, u32[]{:S(2)}, u32[]{:S(2)}) collective-permute-start(bf16[2,4,64,128]{3,2,1,0:T(8,128)(2,1)S(1)} %get-tuple-element.42), channel_id=1, source_target_pairs={{0,192},{32,224},{64,0},{96,32},{128,64},{160,96},{192,128},{224,1... | collective-permute-start | bytes 393224 | tf_op jit(solution)/shard_map/ppermute | solution.py:30
  98.9 17.7 %collective-permute-start.7 = (bf16[2,4,64,128]{3,2,1,0:T(8,128)(2,1)S(1)}, bf16[2,4,64,128]{3,2,1,0:T(8,128)(2,1)S(1)}, u32[]{:S(2)}, u32[]{:S(2)}) collective-permute-start(bf16[2,4,64,128]{3,2,1,0:T(8,128)(2,1)S(1)} %get-tuple-element.43), channel_id=1, source_target_pairs={{0,64},{32,96},{64,128},{96,160},{128,192},{160,224},{192,0},{224,... | collective-permute-start | bytes 393224 | tf_op jit(solution)/shard_map/ppermute | solution.py:30
  116.7 2.3 %collective-permute-start.9 = (bf16[4,4,64,128]{3,2,1,0:T(8,128)(2,1)S(1)}, bf16[4,4,64,128]{3,2,1,0:T(8,128)(2,1)S(1)}, u32[]{:S(2)}, u32[]{:S(2)}) collective-permute-start(bf16[4,4,64,128]{3,2,1,0:T(8,128)(2,1)S(1)} %other.1), channel_id=1, source_target_pairs={{0,32},{32,0},{64,96},{96,64},{128,160},{160,128},{192,224},{224,1... | collective-permute-start | bytes 786440 | tf_op jit(solution)/shard_map/ppermute | solution.py:30

commit v5 on v2

--- a/solution.py
+++ b/solution.py
@@ -118,7 +118,7 @@
 
 def tile_kernel(
     lat_ref, t0, t1, t2, t3, top_ref, bot_ref, w1_ref, pool_ref, _,
-    grads_ref, hid_ref, dpre_ref,
+    grads_ref, hid_far, dpre_far, hid_ref, dpre_ref,
     own_ref, pre_s, dh_s, act_s, xo_s, oc_s, hq_s, dpo_s, hid_s, dpre_s, sum_s, var_s, shared_s, ca_s, cs_s, sems,
 ):
     srcs, rows, width, _ = own_ref.shape
@@ -194,7 +194,9 @@
         return carry
 
     lax.fori_loop(0, srcs, third, 0)
-    hid_copy = pltpu.make_async_copy(hid_s, hid_ref, sems.at[0])
+    first = hid_ref.shape[0]
+    hid_far[...] = hid_s[first:]
+    hid_copy = pltpu.make_async_copy(hid_s.at[pl.ds(0, first)], hid_ref, sems.at[0])
     hid_copy.start()
     d_shared = pair_sum(ca_s[...])
     d1, d2, d3 = split3(d_shared.reshape(inner * WIDE, channels))
@@ -218,7 +220,8 @@
         return carry
 
     lax.fori_loop(0, srcs, fourth, 0)
-    dpre_copy = pltpu.make_async_copy(dpre_s, dpre_ref, sems.at[1])
+    dpre_far[...] = dpre_s[first:]
+    dpre_copy = pltpu.make_async_copy(dpre_s.at[pl.ds(0, first)], dpre_ref, sems.at[1])
     dpre_copy.start()
 
     total = srcs * rows * cols
@@ -241,7 +244,9 @@
     dpre_copy.wait()
 
 
-def output_kernel(t0, t1, t2, t3, hid_ref, dpre_ref, w2_ref, *out_refs):
+def output_kernel(*refs):
+    (hid_ref, dpre_ref, w2_ref), refs = refs[:3], refs[3:]
+    tiles, out_refs = refs[: len(refs) // 2], refs[len(refs) // 2 :]
     _, inner, width, _ = hid_ref.shape
     rows = inner - 2
     cols = out_refs[0].shape[2]
@@ -250,10 +255,11 @@
         v = ref[s].astype(F32)
         return [(pltpu.roll(v, width - 2 * q, 1) if q else v)[:, :cols] for q in range(3)]
 
-    for d, (tile, out_ref) in enumerate(zip((t0, t1, t2, t3), out_refs)):
+    for d, (tile, out_ref) in enumerate(zip(tiles, out_refs)):
 
         def piece(j, carry):
-            both = jnp.concatenate(shifts(hid_ref, 2 * d + j) + shifts(dpre_ref, 2 * d + j), axis=-1).astype(BF)
+            s = 2 * d + j
+            both = jnp.concatenate(shifts(hid_ref, s) + shifts(dpre_ref, s), axis=-1).astype(BF)
             depth = both.shape[-1]
             acc = dot(both[0:rows].reshape(rows * cols, depth), w2_ref[0])
             acc += dot(both[1 : 1 + rows].reshape(rows * cols, depth), w2_ref[1])
@@ -338,13 +344,15 @@
     slices, copies = lax.axis_size(PLANE), lax.axis_size(REST)
     per = -(-used // (8 * slices)) * 8
     shifted = (groups, inner, cols * mem_local, 384)
-    compact = pltpu.HBM((groups, inner, width, channels), BF)
+    compact = (groups, inner, width, channels)
+    far_part = vm((2,) + compact[1:], BF)
+    first_part = pltpu.HBM((groups - 2,) + compact[1:], BF)
     hspec = pl.BlockSpec(memory_space=pltpu.HBM)
-    grads, hid, dpre = pl.pallas_call(
+    grads, hid_far, dpre_far, hid, dpre = pl.pallas_call(
         tile_kernel,
-        out_shape=[vm((slices * per, channels), BF), compact, compact],
+        out_shape=[vm((slices * per, channels), BF), far_part, far_part, first_part, first_part],
         in_specs=[sspec] + [vspec] * (chips + 4) + [hspec],
-        out_specs=[vspec, hspec, hspec],
+        out_specs=[vspec] * 3 + [hspec] * 2,
         scratch_shapes=[
             vm((groups, rows, width, 128), BF),
             vm((groups,) + plane, F32),
@@ -354,8 +362,8 @@
             vm((groups, rows, cols * mem_local, 128), BF),
             vm(shifted, BF),
             vm((groups, rows, cols * mem_local, channels), BF),
-            vm(compact.shape, BF),
-            vm(compact.shape, BF),
+            vm(compact, BF),
+            vm(compact, BF),
             vm(plane, F32),
             vm(plane, F32),
             vm(plane, F32),
@@ -366,13 +374,19 @@
         compiler_params=pltpu.CompilerParams(vmem_limit_bytes=48 * 1024 * 1024),
         name="tile",
     )(lat, *near(*tiles, top, bot, w1, pool_weight), w2)
-    pieces = list(pl.pallas_call(
-        output_kernel,
-        out_shape=[vm((2, rows, cols * mem_local, 128), BF)] * chips,
-        in_specs=[vspec] * (chips + 3),
-        out_specs=[vspec] * chips,
-        name="output",
-    )(*near(*tiles), hid, dpre, w2))
+
+    def outputs(hid, dpre, *sources):
+        n = len(sources)
+        return pl.pallas_call(
+            output_kernel,
+            out_shape=[vm((2, rows, cols * mem_local, 128), BF)] * n,
+            in_specs=[vspec] * (n + 3),
+            out_specs=[vspec] * n,
+            name="output",
+        )(hid, dpre, w2, *near(*sources))
+
+    far_piece = outputs(*near(hid_far, dpre_far), tiles[-1])
+    pieces = [*outputs(hid, dpre, *tiles[:-1]), *far_piece]
 
     def exchange(value, axis):
         return lax.all_to_all(value, axis, split_axis=0, concat_axis=0, tiled=True)

time: 105 us -> 105 us (level)
    all_to_all x3, waiting for transfers between devices: 11.4 us -> 9.71 us  [exchange(): return lax.all_to_all(value, axis, split_axis=0, concat_axis=0, tiled=True)]
    pallas_call x1 -> x2, Pallas kernels: 5.36 us -> 6.3 us  [outputs(): pl.pallas_call(output_kernel, out_shape=[vm((2, rows, cols * mem_local, 1...]
  transfers between devices with their start and end apart: 13 -> 13, of which waited for: 10 -> 10; matrix products, arithmetic and copies ran while one was open for 1% -> 1% of each run, Pallas kernels for 7% -> 8%
where the time goes in v5:
time: 105 us
  starting transfers between devices  48.9 us (47%)
  waiting for transfers between devices  30.9 us (29%)
  Pallas kernels  23.3 us (22%)
    all_to_all x3, starting transfers between devices, exchange(): return lax.all_to_all(value, axis, split_axis=0, concat_axis=0, tiled=True)  23.6 us
    ppermute x8, starting transfers between devices, swap(): return lax.ppermute(value, MEMBER, pairs)  20.9 us
    ppermute x8, waiting for transfers between devices, swap(): return lax.ppermute(value, MEMBER, pairs)  15.2 us
    pallas_call x1, Pallas kernels, block(): pl.pallas_call(tile_kernel, out_shape=[vm((slices * per, channels), BF),...  10.9 us
    all_to_all x3, waiting for transfers between devices, exchange(): return lax.all_to_all(value, axis, split_axis=0, concat_axis=0, tiled=True)  9.71 us
    pallas_call x2, Pallas kernels, outputs(): pl.pallas_call(output_kernel, out_shape=[vm((2, rows, cols * mem_local, 1...  6.3 us
    ppermute x1, waiting for transfers between devices, block(): bot = lax.ppermute(head, LAT, [(i + 1, i) for i in range(bands - 1)])  3.85 us
    ppermute x1, starting transfers between devices, block(): top = lax.ppermute(tail, LAT, [(i, i + 1) for i in range(bands - 1)])  3.13 us
  transfers between devices with their start and end apart: 13, of which 10 were waited for; matrix products, arithmetic and copies ran while one was open for 1% of the time, Pallas kernels for 8%

profile of v5, /device:TPU:1, one launch (start us, length us, event | category | flops | bytes accessed | tf_op | source)
XLA Modules:
  0.0 105.0 jit_solution(2885969099684868870)
XLA Ops:
  0.7 2.0 %pack.1 = (bf16[4,4,72,128]{3,2,1,0:T(8,128)(2,1)S(1)}, bf16[4,4,72,128]{3,2,1,0:T(8,128)(2,1)S(1)}) custom-call(s32[1]{0:T(128)} %bitcast.me_ref, bf16[2,64,4,256]{3,2,1,0:T(4,128)(2,1)} %ens_ref.1, bf16[2,64,4,256]{3,2,1,0:T(4,128)(2,1)} %cot_ref.1), custom_call_target="tpu_custom_call" | custom-call | tf_op jit(solution)/shard_map/pack/pallas_call | solution.py:299
  2.7 3.3 %collective-permute-start = (bf16[4,4,72,128]{3,2,1,0:T(8,128)(2,1)S(1)}, bf16[4,4,72,128]{3,2,1,0:T(8,128)(2,1)S(1)}, u32[]{:S(2)}, u32[]{:S(2)}) collective-permute-start(bf16[4,4,72,128]{3,2,1,0:T(8,128)(2,1)S(1)} %get-tuple-element.30), channel_id=1, source_target_pairs={{0,32},{32,0},{64,96},{96,64},{128,160},{160,128},{192,224},{224,1... | collective-permute-start | bytes 884744 | tf_op jit(solution)/shard_map/ppermute | solution.py:30
  6.0 1.2 %collective-permute-done.got_ref = bf16[4,4,72,128]{3,2,1,0:T(8,128)(2,1)S(1)} collective-permute-done((bf16[4,4,72,128]{3,2,1,0:T(8,128)(2,1)S(1)}, bf16[4,4,72,128]{3,2,1,0:T(8,128)(2,1)S(1)}, u32[]{:S(2)}, u32[]{:S(2)}) %collective-permute-start) | collective-permute-done | bytes 294944 | tf_op jit(solution)/shard_map/ppermute | solution.py:30
  7.2 1.4 %collective-permute-start.1 = (bf16[2,4,72,128]{3,2,1,0:T(8,128)(2,1)S(1)}, bf16[2,4,72,128]{3,2,1,0:T(8,128)(2,1)S(1)}, u32[]{:S(2)}, u32[]{:S(2)}) collective-permute-start(bf16[2,4,72,128]{3,2,1,0:T(8,128)(2,1)S(1)} %get-tuple-element.32), channel_id=1, source_target_pairs={{0,64},{32,96},{64,128},{96,160},{128,192},{160,224},{192,0},{224,... | collective-permute-start | bytes 442376 | tf_op jit(solution)/shard_map/ppermute | solution.py:30
  8.6 3.1 %collective-permute-start.2 = (bf16[2,4,72,128]{3,2,1,0:T(8,128)(2,1)S(1)}, bf16[2,4,72,128]{3,2,1,0:T(8,128)(2,1)S(1)}, u32[]{:S(2)}, u32[]{:S(2)}) collective-permute-start(bf16[2,4,72,128]{3,2,1,0:T(8,128)(2,1)S(1)} %get-tuple-element.33), channel_id=1, source_target_pairs={{0,192},{32,224},{64,0},{96,32},{128,64},{160,96},{192,128},{224,1... | collective-permute-start | bytes 442376 | tf_op jit(solution)/shard_map/ppermute | solution.py:30
  11.7 4.4 %collective-permute-start.3 = (bf16[2,4,72,128]{3,2,1,0:T(8,128)(2,1)S(1)}, bf16[2,4,72,128]{3,2,1,0:T(8,128)(2,1)S(1)}, u32[]{:S(2)}, u32[]{:S(2)}) collective-permute-start(bf16[2,4,72,128]{3,2,1,0:T(8,128)(2,1)S(1)} %get-tuple-element.34), channel_id=1, source_target_pairs={{0,128},{32,160},{64,192},{96,224},{128,0},{160,32},{192,64},{224,... | collective-permute-start | bytes 442376 | tf_op jit(solution)/shard_map/ppermute | solution.py:30
  16.1 7.0 %collective-permute-done.2.refs_2_.t2.refs_5_ = bf16[2,4,72,128]{3,2,1,0:T(8,128)(2,1)S(1)} collective-permute-done((bf16[2,4,72,128]{3,2,1,0:T(8,128)(2,1)S(1)}, bf16[2,4,72,128]{3,2,1,0:T(8,128)(2,1)S(1)}, u32[]{:S(2)}, u32[]{:S(2)}) %collective-permute-start.2) | collective-permute-done | bytes 147488 | tf_op jit(solution)/shard_map/ppermute | solution.py:30
  23.2 1.7 %collective-permute-done.3.refs_3_.t3 = bf16[2,4,72,128]{3,2,1,0:T(8,128)(2,1)S(1)} collective-permute-done((bf16[2,4,72,128]{3,2,1,0:T(8,128)(2,1)S(1)}, bf16[2,4,72,128]{3,2,1,0:T(8,128)(2,1)S(1)}, u32[]{:S(2)}, u32[]{:S(2)}) %collective-permute-start.3) | collective-permute-done | bytes 147488 | tf_op jit(solution)/shard_map/ppermute | solution.py:30
  24.9 3.1 %collective-permute-start.4 = (bf16[8,2,72,128]{3,2,1,0:T(8,128)(2,1)S(1)}, bf16[8,2,72,128]{3,2,1,0:T(8,128)(2,1)S(1)}, u32[]{:S(2)}, u32[]{:S(2)}) collective-permute-start(bf16[8,2,72,128]{3,2,1,0:T(8,128)(2,1)S(1)} %get-tuple-element.35), channel_id=1, source_target_pairs={{0,1},{1,2},{2,3},{3,4},{4,5},{5,6},{6,7},{7,8},{8,9},{9,10},{10,1... | collective-permute-start | bytes 884744 | tf_op jit(solution)/shard_map/ppermute | solution.py:323
  28.1 1.3 %collective-permute-start.5 = (bf16[8,2,72,128]{3,2,1,0:T(8,128)(2,1)S(1)}, bf16[8,2,72,128]{3,2,1,0:T(8,128)(2,1)S(1)}, u32[]{:S(2)}, u32[]{:S(2)}) collective-permute-start(bf16[8,2,72,128]{3,2,1,0:T(8,128)(2,1)S(1)} %get-tuple-element.36), channel_id=1, source_target_pairs={{1,0},{2,1},{3,2},{4,3},{5,4},{6,5},{7,6},{8,7},{9,8},{10,9},{11,1... | collective-permute-start | bytes 884744 | tf_op jit(solution)/shard_map/ppermute | solution.py:324
  29.7 0.3 copy.13
  30.3 2.1 %collective-permute-done.4.top_ref = bf16[8,2,72,128]{3,2,1,0:T(8,128)(2,1)S(1)} collective-permute-done((bf16[8,2,72,128]{3,2,1,0:T(8,128)(2,1)S(1)}, bf16[8,2,72,128]{3,2,1,0:T(8,128)(2,1)S(1)}, u32[]{:S(2)}, u32[]{:S(2)}) %collective-permute-start.4) | collective-permute-done | bytes 294944 | tf_op jit(solution)/shard_map/ppermute | solution.py:323
  32.5 3.8 %collective-permute-done.5.bot_ref = bf16[8,2,72,128]{3,2,1,0:T(8,128)(2,1)S(1)} collective-permute-done((bf16[8,2,72,128]{3,2,1,0:T(8,128)(2,1)S(1)}, bf16[8,2,72,128]{3,2,1,0:T(8,128)(2,1)S(1)}, u32[]{:S(2)}, u32[]{:S(2)}) %collective-permute-start.5) | collective-permute-done | bytes 294944 | tf_op jit(solution)/shard_map/ppermute | solution.py:324
  36.3 10.9 %tile.1 = (bf16[1408,128]{1,0:T(8,128)(2,1)}, bf16[2,6,72,128]{3,2,1,0:T(8,128)(2,1)S(1)}, bf16[2,6,72,128]{3,2,1,0:T(8,128)(2,1)S(1)}, bf16[6,6,72,128]{3,2,1,0:T(8,128)(2,1)}, bf16[6,6,72,128]{3,2,1,0:T(8,128)(2,1)}) custom-call(s32[2]{0:T(128)S(1)} %pad_add_fusion.lat_ref, bf16[2,4,72,128]{3,2,1,0:T(8,128)(2,1)S(1)} %get-tuple-element.31.refs_0_.t0.refs_3_, ...), custom_call_target="tpu_custom_call" | custom-call | tf_op jit(solution)/shard_map/tile/pallas_call | solution.py:351
  47.3 13.0 %all-to-all-start = ((bf16[16,88,128]{2,1,0:T(8,128)(2,1)}), bf16[16,88,128]{2,1,0:T(8,128)(2,1)S(1)}, u32[]{:S(2)}, u32[]{:S(2)}) async-start(bf16[16,88,128]{2,1,0:T(8,128)(2,1)} %bitcast.7), calls=%async_computation | async-start | bytes 720896 | tf_op jit(solution)/shard_map/all_to_all | solution.py:392
  60.2 4.3 %output.2 = (bf16[2,4,64,128]{3,2,1,0:T(8,128)(2,1)S(1)}, bf16[2,4,64,128]{3,2,1,0:T(8,128)(2,1)S(1)}, bf16[2,4,64,128]{3,2,1,0:T(8,128)(2,1)S(1)}) custom-call(bf16[6,6,72,128]{3,2,1,0:T(8,128)(2,1)} %get-tuple-element.37.refs_0_, bf16[6,6,72,128]{3,2,1,0:T(8,128)(2,1)} %get-tuple-element.38.refs_1_, bf16[3,768,128]{2,1,0:T(8,128)(2,1)} %copy-done, ...), custom_call_target="tpu_custom_call" | custom-call | tf_op jit(solution)/shard_map/output/pallas_call | solution.py:380
  64.5 3.8 %all-to-all-done.parts_ref = bf16[16,88,128]{2,1,0:T(8,128)(2,1)S(1)} async-done(((bf16[16,88,128]{2,1,0:T(8,128)(2,1)}), bf16[16,88,128]{2,1,0:T(8,128)(2,1)S(1)}, u32[]{:S(2)}, u32[]{:S(2)}) %all-to-all-start) | async-done | bytes 360480 | tf_op jit(solution)/shard_map/all_to_all | solution.py:392
  68.3 0.8 total.2
  69.1 7.1 %all-to-all-start.1 = ((bf16[16,88,128]{2,1,0:T(8,128)(2,1)}), bf16[16,88,128]{2,1,0:T(8,128)(2,1)S(1)}, u32[]{:S(2)}, u32[]{:S(2)}) async-start(bf16[16,88,128]{2,1,0:T(8,128)(2,1)} %total.2), calls=%async_computation.1 | async-start | bytes 720896 | tf_op jit(solution)/shard_map/all_to_all | solution.py:392
  76.2 2.0 %output.3 = bf16[2,4,64,128]{3,2,1,0:T(8,128)(2,1)S(1)} custom-call(bf16[2,6,72,128]{3,2,1,0:T(8,128)(2,1)S(1)} %get-tuple-element.45.refs_0_, bf16[2,6,72,128]{3,2,1,0:T(8,128)(2,1)S(1)} %get-tuple-element.46.refs_1_, bf16[3,768,128]{2,1,0:T(8,128)(2,1)} %copy-done, bf16[2,4,72,128]{3,2,1,0:T(8,128)(2,1)S(1)} %collective-permute-done.3.refs_3_.t3), custom_call_target="tpu_custom_call" | custom-call | tf_op jit(solution)/shard_map/output/pallas_call | solution.py:380
  78.2 5.3 %collective-permute-start.8 = (bf16[2,4,64,128]{3,2,1,0:T(8,128)(2,1)S(1)}, bf16[2,4,64,128]{3,2,1,0:T(8,128)(2,1)S(1)}, u32[]{:S(2)}, u32[]{:S(2)}) collective-permute-start(bf16[2,4,64,128]{3,2,1,0:T(8,128)(2,1)S(1)} %output.3), channel_id=1, source_target_pairs={{0,128},{32,160},{64,192},{96,224},{128,0},{160,32},{192,64},{224,... | collective-permute-start | bytes 393224 | tf_op jit(solution)/shard_map/ppermute | solution.py:30
  83.5 0.3 collective-permute-start.6
  83.8 2.1 %collective-permute-start.7 = (bf16[2,4,64,128]{3,2,1,0:T(8,128)(2,1)S(1)}, bf16[2,4,64,128]{3,2,1,0:T(8,128)(2,1)S(1)}, u32[]{:S(2)}, u32[]{:S(2)}) collective-permute-start(bf16[2,4,64,128]{3,2,1,0:T(8,128)(2,1)S(1)} %get-tuple-element.44), channel_id=1, source_target_pairs={{0,64},{32,96},{64,128},{96,160},{128,192},{160,224},{192,0},{224,... | collective-permute-start | bytes 393224 | tf_op jit(solution)/shard_map/ppermute | solution.py:30
  85.9 5.1 %all-to-all-done.1.parts_ref = bf16[16,88,128]{2,1,0:T(8,128)(2,1)S(1)} async-done(((bf16[16,88,128]{2,1,0:T(8,128)(2,1)}), bf16[16,88,128]{2,1,0:T(8,128)(2,1)S(1)}, u32[]{:S(2)}, u32[]{:S(2)}) %all-to-all-start.1) | async-done | bytes 360480 | tf_op jit(solution)/shard_map/all_to_all | solution.py:392
  91.0 0.8 total.3
  91.8 3.5 %all-to-all-start.2 = ((bf16[16,88,128]{2,1,0:T(8,128)(2,1)}), bf16[16,88,128]{2,1,0:T(8,128)(2,1)S(1)}, u32[]{:S(2)}, u32[]{:S(2)}) async-start(bf16[16,88,128]{2,1,0:T(8,128)(2,1)} %total.3), calls=%async_computation.2 | async-start | bytes 720896 | tf_op jit(solution)/shard_map/all_to_all | solution.py:392
  95.3 4.1 %collective-permute-done.7.refs_2_ = bf16[2,4,64,128]{3,2,1,0:T(8,128)(2,1)S(1)} collective-permute-done((bf16[2,4,64,128]{3,2,1,0:T(8,128)(2,1)S(1)}, bf16[2,4,64,128]{3,2,1,0:T(8,128)(2,1)S(1)}, u32[]{:S(2)}, u32[]{:S(2)}) %collective-permute-start.7) | collective-permute-done | bytes 131104 | tf_op jit(solution)/shard_map/ppermute | solution.py:30
  99.5 1.1 %collective-permute-start.9 = (bf16[4,4,64,128]{3,2,1,0:T(8,128)(2,1)S(1)}, bf16[4,4,64,128]{3,2,1,0:T(8,128)(2,1)S(1)}, u32[]{:S(2)}, u32[]{:S(2)}) collective-permute-start(bf16[4,4,64,128]{3,2,1,0:T(8,128)(2,1)S(1)} %other.1), channel_id=1, source_target_pairs={{0,32},{32,0},{64,96},{96,64},{128,160},{160,128},{192,224},{224,1... | collective-permute-start | bytes 786440 | tf_op jit(solution)/shard_map/ppermute | solution.py:30
  100.5 1.2 %collective-permute-done.9.refs_4_ = bf16[4,4,64,128]{3,2,1,0:T(8,128)(2,1)S(1)} collective-permute-done((bf16[4,4,64,128]{3,2,1,0:T(8,128)(2,1)S(1)}, bf16[4,4,64,128]{3,2,1,0:T(8,128)(2,1)S(1)}, u32[]{:S(2)}, u32[]{:S(2)}) %collective-permute-start.9) | collective-permute-done | bytes 262176 | tf_op jit(solution)/shard_map/ppermute | solution.py:30
  101.7 1.5 %unpack.1 = (bf16[2,64,4,256]{3,2,1,0:T(4,128)(2,1)}, bf16[2,64,4,256]{3,2,1,0:T(4,128)(2,1)}) custom-call(s32[1]{0:T(128)} %bitcast.me_ref, bf16[2,4,64,128]{3,2,1,0:T(8,128)(2,1)S(1)} %get-tuple-element.39.refs_0_, bf16[2,4,64,128]{3,2,1,0:T(8,128)(2,1)S(1)} %collective-permute-done.6.refs_1_, bf16[2,4,64,128]{3,2,1,0:T(8,128)(2,1)S(1)} %collective-permute-done.7.refs_2_, ...), custom_call_target="tpu_custom_call" | custom-call | tf_op jit(solution)/shard_map/unpack/pallas_call | solution.py:433
  103.2 0.8 all-to-all-done.2
  104.1 0.9 finish.1
  (22 shorter events, 0.8 us)
Async XLA Ops:
  0.6 15.5 %copy-start.3 = (bf16[3,3,64,128]{3,2,1,0:T(8,128)(2,1)S(1)}, bf16[3,3,64,128]{3,2,1,0:T(8,128)(2,1)}, u32[]{:S(2)}) copy-start(bf16[3,3,64,128]{3,2,1,0:T(8,128)(2,1)} %param.7) | copy-start | bytes 442372
  0.7 15.5 %copy-start.2 = (bf16[3,3,128,64]{2,3,1,0:T(8,128)(2,1)S(1)}, bf16[3,3,128,64]{2,3,1,0:T(8,128)(2,1)}, u32[]{:S(2)}) copy-start(bf16[3,3,128,64]{2,3,1,0:T(8,128)(2,1)} %param.9) | copy-start | bytes 442372
  2.7 4.5 %collective-permute-start = (bf16[4,4,72,128]{3,2,1,0:T(8,128)(2,1)S(1)}, bf16[4,4,72,128]{3,2,1,0:T(8,128)(2,1)S(1)}, u32[]{:S(2)}, u32[]{:S(2)}) collective-permute-start(bf16[4,4,72,128]{3,2,1,0:T(8,128)(2,1)S(1)} %get-tuple-element.30), channel_id=1, source_target_pairs={{0,32},{32,0},{64,96},{96,64},{128,160},{160,128},{192,224},{224,1... | collective-permute-start | bytes 884744 | tf_op jit(solution)/shard_map/ppermute | solution.py:30
  7.2 8.9 %collective-permute-start.1 = (bf16[2,4,72,128]{3,2,1,0:T(8,128)(2,1)S(1)}, bf16[2,4,72,128]{3,2,1,0:T(8,128)(2,1)S(1)}, u32[]{:S(2)}, u32[]{:S(2)}) collective-permute-start(bf16[2,4,72,128]{3,2,1,0:T(8,128)(2,1)S(1)} %get-tuple-element.32), channel_id=1, source_target_pairs={{0,64},{32,96},{64,128},{96,160},{128,192},{160,224},{192,0},{224,... | collective-permute-start | bytes 442376 | tf_op jit(solution)/shard_map/ppermute | solution.py:30
  8.6 14.6 %collective-permute-start.2 = (bf16[2,4,72,128]{3,2,1,0:T(8,128)(2,1)S(1)}, bf16[2,4,72,128]{3,2,1,0:T(8,128)(2,1)S(1)}, u32[]{:S(2)}, u32[]{:S(2)}) collective-permute-start(bf16[2,4,72,128]{3,2,1,0:T(8,128)(2,1)S(1)} %get-tuple-element.33), channel_id=1, source_target_pairs={{0,192},{32,224},{64,0},{96,32},{128,64},{160,96},{192,128},{224,1... | collective-permute-start | bytes 442376 | tf_op jit(solution)/shard_map/ppermute | solution.py:30
  11.7 13.2 %collective-permute-start.3 = (bf16[2,4,72,128]{3,2,1,0:T(8,128)(2,1)S(1)}, bf16[2,4,72,128]{3,2,1,0:T(8,128)(2,1)S(1)}, u32[]{:S(2)}, u32[]{:S(2)}) collective-permute-start(bf16[2,4,72,128]{3,2,1,0:T(8,128)(2,1)S(1)} %get-tuple-element.34), channel_id=1, source_target_pairs={{0,128},{32,160},{64,192},{96,224},{128,0},{160,32},{192,64},{224,... | collective-permute-start | bytes 442376 | tf_op jit(solution)/shard_map/ppermute | solution.py:30
  24.9 7.6 %collective-permute-start.4 = (bf16[8,2,72,128]{3,2,1,0:T(8,128)(2,1)S(1)}, bf16[8,2,72,128]{3,2,1,0:T(8,128)(2,1)S(1)}, u32[]{:S(2)}, u32[]{:S(2)}) collective-permute-start(bf16[8,2,72,128]{3,2,1,0:T(8,128)(2,1)S(1)} %get-tuple-element.35), channel_id=1, source_target_pairs={{0,1},{1,2},{2,3},{3,4},{4,5},{5,6},{6,7},{7,8},{8,9},{9,10},{10,1... | collective-permute-start | bytes 884744 | tf_op jit(solution)/shard_map/ppermute | solution.py:323
  28.1 8.3 %collective-permute-start.5 = (bf16[8,2,72,128]{3,2,1,0:T(8,128)(2,1)S(1)}, bf16[8,2,72,128]{3,2,1,0:T(8,128)(2,1)S(1)}, u32[]{:S(2)}, u32[]{:S(2)}) collective-permute-start(bf16[8,2,72,128]{3,2,1,0:T(8,128)(2,1)S(1)} %get-tuple-element.36), channel_id=1, source_target_pairs={{1,0},{2,1},{3,2},{4,3},{5,4},{6,5},{7,6},{8,7},{9,8},{10,9},{11,1... | collective-permute-start | bytes 884744 | tf_op jit(solution)/shard_map/ppermute | solution.py:324
  30.3 6.1 %copy-start.1 = (bf16[256,128]{1,0:T(8,128)(2,1)S(1)}, bf16[256,128]{1,0:T(8,128)(2,1)}, u32[]{:S(2)}) copy-start(bf16[256,128]{1,0:T(8,128)(2,1)} %pool_ref.1) | copy-start | bytes 196612
  30.3 16.9 %copy-start = (bf16[3,768,128]{2,1,0:T(8,128)(2,1)}, bf16[3,768,128]{2,1,0:T(8,128)(2,1)S(1)}, u32[]{:S(2)}) copy-start(bf16[3,768,128]{2,1,0:T(8,128)(2,1)S(1)} %pad_maximum_fusion._.refs_2_) | copy-start | bytes 1769476
  47.3 21.0 %all-to-all-start = ((bf16[16,88,128]{2,1,0:T(8,128)(2,1)}), bf16[16,88,128]{2,1,0:T(8,128)(2,1)S(1)}, u32[]{:S(2)}, u32[]{:S(2)}) async-start(bf16[16,88,128]{2,1,0:T(8,128)(2,1)} %bitcast.7), calls=%async_computation | async-start | bytes 720896 | tf_op jit(solution)/shard_map/all_to_all | solution.py:392
  69.1 21.9 %all-to-all-start.1 = ((bf16[16,88,128]{2,1,0:T(8,128)(2,1)}), bf16[16,88,128]{2,1,0:T(8,128)(2,1)S(1)}, u32[]{:S(2)}, u32[]{:S(2)}) async-start(bf16[16,88,128]{2,1,0:T(8,128)(2,1)} %total.2), calls=%async_computation.1 | async-start | bytes 720896 | tf_op jit(solution)/shard_map/all_to_all | solution.py:392
  78.2 17.2 %collective-permute-start.8 = (bf16[2,4,64,128]{3,2,1,0:T(8,128)(2,1)S(1)}, bf16[2,4,64,128]{3,2,1,0:T(8,128)(2,1)S(1)}, u32[]{:S(2)}, u32[]{:S(2)}) collective-permute-start(bf16[2,4,64,128]{3,2,1,0:T(8,128)(2,1)S(1)} %output.3), channel_id=1, source_target_pairs={{0,128},{32,160},{64,192},{96,224},{128,0},{160,32},{192,64},{224,... | collective-permute-start | bytes 393224 | tf_op jit(solution)/shard_map/ppermute | solution.py:30
  83.5 11.8 %collective-permute-start.6 = (bf16[2,4,64,128]{3,2,1,0:T(8,128)(2,1)S(1)}, bf16[2,4,64,128]{3,2,1,0:T(8,128)(2,1)S(1)}, u32[]{:S(2)}, u32[]{:S(2)}) collective-permute-start(bf16[2,4,64,128]{3,2,1,0:T(8,128)(2,1)S(1)} %get-tuple-element.43), channel_id=1, source_target_pairs={{0,192},{32,224},{64,0},{96,32},{128,64},{160,96},{192,128},{224,1... | collective-permute-start | bytes 393224 | tf_op jit(solution)/shard_map/ppermute | solution.py:30
  83.8 15.7 %collective-permute-start.7 = (bf16[2,4,64,128]{3,2,1,0:T(8,128)(2,1)S(1)}, bf16[2,4,64,128]{3,2,1,0:T(8,128)(2,1)S(1)}, u32[]{:S(2)}, u32[]{:S(2)}) collective-permute-start(bf16[2,4,64,128]{3,2,1,0:T(8,128)(2,1)S(1)} %get-tuple-element.44), channel_id=1, source_target_pairs={{0,64},{32,96},{64,128},{96,160},{128,192},{160,224},{192,0},{224,... | collective-permute-start | bytes 393224 | tf_op jit(solution)/shard_map/ppermute | solution.py:30
  91.8 12.3 %all-to-all-start.2 = ((bf16[16,88,128]{2,1,0:T(8,128)(2,1)}), bf16[16,88,128]{2,1,0:T(8,128)(2,1)S(1)}, u32[]{:S(2)}, u32[]{:S(2)}) async-start(bf16[16,88,128]{2,1,0:T(8,128)(2,1)} %total.3), calls=%async_computation.2 | async-start | bytes 720896 | tf_op jit(solution)/shard_map/all_to_all | solution.py:392
  99.5 2.2 %collective-permute-start.9 = (bf16[4,4,64,128]{3,2,1,0:T(8,128)(2,1)S(1)}, bf16[4,4,64,128]{3,2,1,0:T(8,128)(2,1)S(1)}, u32[]{:S(2)}, u32[]{:S(2)}) collective-permute-start(bf16[4,4,64,128]{3,2,1,0:T(8,128)(2,1)S(1)} %other.1), channel_id=1, source_target_pairs={{0,32},{32,0},{64,96},{96,64},{128,160},{160,128},{192,224},{224,1... | collective-permute-start | bytes 786440 | tf_op jit(solution)/shard_map/ppermute | solution.py:30
